TPU v7x, 512 devices: a whole 4x8x8 slice. The times are simulated.
512 devices in a mesh: row: 32 (over y, x), col: 16 (over z, core).
Axes of the slice: x: 4, y: 8, z: 8, core: 2. Of those that a mesh axis runs over, the one named last changes fastest.
Arguments:
- right_side: float32 [64, 16384], P(None, ('row', 'col')), may hold values from -6 to 6
- regular: float32 [16384], P(('row', 'col')), may hold values from 1 to 2
- curvature: bfloat16 [32, 32, 16, 128, 128], P('row', None, 'col'), as said below
- block_rows: int32 [32, 32, 16], P('row', None, 'col'), may hold values from 0 to 3, as said below
- block_cols: int32 [32, 32, 16], P('row', None, 'col'), may hold values from 0 to 3
- block_counts: int32 [32, 32, 16], P('row', None, 'col'), may hold values from 0 to 1, as said below
Outputs:
- solution: float32 [64, 16384], P(None, ('row', 'col'))
- residual: float32 [64, 16384], P(None, ('row', 'col'))
Inputs may be any that keep to these rules, and one draw needn't show every extreme that they name: `block_rows`: the curvature is symmetric: a live term of owner r from source s with block row a and block column b is matched, in the same slot of owner s from source r, by block row b, block column a and the transposed block. `block_counts`: counts for the first index of col are always 1. A with this curvature and regular is symmetric positive definite.
All inputs are finite; a program needn't handle non-finite values.
Results may differ from a plain program's by a relative error of at most 0.0041.
Values may be sent and summed in bfloat16 or wider, within the bound.
No kernel may reach another device: no remote copies, remote signals or barrier semaphores. Data moves between devices by JAX's collectives and lax.ppermute only.
A program may use at most 64 MiB of HBM per device.

v0:
```python
import jax
import jax.numpy as jnp
from jax import lax
from jax.sharding import Mesh
from jax.sharding import PartitionSpec as P

M_DEV = 1
ITERS = 3
COL = ("col_0", "col_1")
ROW_COL = ("row_0", "row_1", "col_0", "col_1")
ROW = ("row_0", "row_1")


def one_axis_at_a_time(shard, axes):
    for axis in axes:
        shard = lax.psum(shard, axis)
    return shard


def gather_axes(shard, axes, dim):
    for axis in reversed(axes):
        shard = lax.all_gather(shard, axis, axis=dim, tiled=True)
    return shard


def in_blocks(shard, dim, peers):
    shape = shard.shape
    blocks = shard.reshape(*shape[:dim], peers, shape[dim] // peers, *shape[dim + 1 :])
    return jnp.moveaxis(blocks, dim, 0)


def sum_at_owner(shard, axis, dim):
    peers = lax.axis_size(axis)
    blocks = lax.all_to_all(in_blocks(shard, dim, peers), axis, 0, 0, tiled=True)
    return jnp.sum(blocks, axis=0)


def chol_solve(matrix, rhs_mat):
    factor = jnp.linalg.cholesky(matrix)
    return jax.scipy.linalg.cho_solve((factor, True), rhs_mat)


def local_gram(left, right):
    return jnp.dot(left, right.T, precision=lax.Precision.HIGHEST)


def live_table(counts_local):
    per_slot = jnp.repeat(counts_local, M_DEV, axis=1)
    slot_rank = jnp.arange(per_slot.shape[1], dtype=jnp.int32) % M_DEV
    return slot_rank[None, :] < per_slot


def apply_terms(dir_piece, curv_local, rows_local, cols_local, live_local, blocks_dev):
    samples = dir_piece.shape[0]
    sources = dir_piece.shape[1]
    block_len = curv_local.shape[-1]
    slot_cap = curv_local.shape[1]
    flat_dirs = dir_piece.reshape(samples, sources * blocks_dev, block_len)
    positions = (jnp.arange(sources, dtype=jnp.int32)[:, None] * blocks_dev + cols_local).reshape(
        -1
    )
    chosen = jnp.take(flat_dirs, positions, axis=1).reshape(samples, sources, slot_cap, block_len)
    products = jnp.einsum("xsmq,smpq->xsmp", chosen, curv_local, preferred_element_type=jnp.float32)
    block_ids = jnp.arange(blocks_dev, dtype=jnp.int32)
    row_table = (
        (rows_local[:, :, None] == block_ids[None, None, :]) & live_local[:, :, None]
    ).astype(jnp.float32)
    return jnp.einsum("xsmp,smb->xbp", products, row_table, precision=lax.Precision.HIGHEST)


def body(right_side, regular, curvature, block_rows, block_cols, block_counts):
    samples = right_side.shape[0]
    pix_here = right_side.shape[1]
    block_len = curvature.shape[-1]
    blocks_dev = pix_here * lax.axis_size(COL) // block_len
    curv_local = curvature[0]
    rows_local = block_rows[0]
    cols_local = block_cols[0]
    live_local = live_table(block_counts[0])
    solution = jnp.zeros_like(right_side)
    residual = right_side
    direction = right_side
    res_gram = one_axis_at_a_time(local_gram(residual, residual), ROW_COL)
    for iteration in range(ITERS):
        dir_bf = direction.astype(jnp.bfloat16)
        own_rows = lax.all_gather(dir_bf, COL, axis=1, tiled=True)
        partials = apply_terms(
            gather_axes(own_rows[:, None, :], ROW, 1),
            curv_local,
            rows_local,
            cols_local,
            live_local,
            blocks_dev,
        )
        coupled = sum_at_owner(partials.reshape(samples, blocks_dev * block_len), COL, 1)
        image = regular[None, :] * direction + coupled
        curv_gram, cross_gram, image_gram = (
            one_axis_at_a_time(local_gram(direction, image), ROW_COL),
            one_axis_at_a_time(local_gram(residual, image), ROW_COL),
            one_axis_at_a_time(local_gram(image, image), ROW_COL),
        )
        curv_gram = 0.5 * (curv_gram + curv_gram.T)
        alpha_mat = chol_solve(curv_gram, res_gram)
        solution = solution + jnp.dot(alpha_mat.T, direction, precision=lax.Precision.HIGHEST)
        residual = residual - jnp.dot(alpha_mat.T, image, precision=lax.Precision.HIGHEST)
        cross_term = jnp.dot(cross_gram, alpha_mat, precision=lax.Precision.HIGHEST)
        quad_term = jnp.dot(
            alpha_mat.T,
            jnp.dot(image_gram, alpha_mat, precision=lax.Precision.HIGHEST),
            precision=lax.Precision.HIGHEST,
        )
        new_gram = res_gram - cross_term - cross_term.T + quad_term
        new_gram = 0.5 * (new_gram + new_gram.T)
        if iteration + 1 < ITERS:
            beta_mat = chol_solve(res_gram, new_gram)
            direction = residual + jnp.dot(beta_mat.T, direction, precision=lax.Precision.HIGHEST)
            res_gram = new_gram
    return (solution, residual)


def solution(mesh):
    finer = Mesh(mesh.devices.reshape(8, 4, 8, 2), ("row_0", "row_1", "col_0", "col_1"))
    placed = (
        P(None, ROW_COL),
        P(ROW_COL),
        P(ROW, None, COL, None, None),
        P(ROW, None, COL),
        P(ROW, None, COL),
        P(ROW, None, COL),
    )
    return jax.shard_map(
        body,
        mesh=finer,
        in_specs=placed,
        out_specs=(P(None, ROW_COL), P(None, ROW_COL)),
        check_vma=False,
    )
```

profile of v0, /device:TPU:1, one launch (start us, length us, event | category | flops | bytes accessed | tf_op | source)
XLA Modules:
  0.0 618.6 jit_solution(11180150527277156011)
XLA Ops:
  8.0 24.8 %all_gather.27 = bf16[64,512]{0,1:T(8,128)(2,1)S(1)} all-gather(bf16[64,32]{0,1:T(8,128)(2,1)S(1)} %convert_element_type.12), channel_id=1, replica_groups=mesh['row_0'=8,'row_1'=4,'col_0'=8,'col_1'=2] {'col_0','col_1'}, dimensions={1}, use_global_device_ids=true | all-gather | bytes 69632 | tf_op jit(solution)/shard_map/all_gather | solution.py:86
  32.8 11.0 %all-gather = bf16[64,2048]{0,1:T(8,128)(2,1)S(1)} all-gather(bf16[64,512]{0,1:T(8,128)(2,1)S(1)} %all_gather.27), channel_id=2, replica_groups=mesh['row_0'=8,'row_1'=4,'col_0'=8,'col_1'=2] {'row_1'}, dimensions={1}, use_global_device_ids=true | all-gather | bytes 327680 | tf_op jit(solution)/shard_map/all_gather | solution.py:22
  46.1 36.7 %all-gather.7.cloned.1.call-done = bf16[64,32,512]{2,0,1:T(8,128)(2,1)} async-done(((bf16[64,4,512]{2,0,1:T(8,128)(2,1)}), bf16[64,32,512]{2,0,1:T(8,128)(2,1)}) %all-gather.7.cloned.1.call-update) | async-done | bytes 2097168 | tf_op jit(solution)/shard_map/all_gather | solution.py:22
  96.5 12.2 %all-to-all-start = ((f32[16,1,2048]{2,1,0:T(1,128)}), f32[16,1,2048]{2,1,0:T(1,128)S(1)}, u32[]{:S(2)}, u32[]{:S(2)}) async-start(f32[16,1,2048]{2,1,0:T(1,128)} %reshape.231), calls=%async_computation | async-start | bytes 262144 | tf_op jit(solution)/shard_map/all_to_all | solution.py:34
  109.0 8.6 %all-to-all-done = f32[16,1,2048]{2,1,0:T(1,128)S(1)} async-done(((f32[16,1,2048]{2,1,0:T(1,128)}), f32[16,1,2048]{2,1,0:T(1,128)S(1)}, u32[]{:S(2)}, u32[]{:S(2)}) %all-to-all-start) | async-done | bytes 131104 | tf_op jit(solution)/shard_map/all_to_all | solution.py:34
  119.8 22.9 %all-reduce.3 = (f32[64,64]{0,1:T(8,128)S(1)}, f32[64,64]{1,0:T(8,128)S(1)}, f32[64,64]{1,0:T(8,128)S(1)}) all-reduce(f32[64,64]{0,1:T(8,128)S(1)} %fusion.74, f32[64,64]{1,0:T(8,128)S(1)} %convolution_bitcast_fusion.6, f32[64,64]{1,0:T(8,128)S(1)} %fusion.54), channel_id=1, replica_groups=mesh['row_0'=8,'row_1'=4,'col_0'=8,'col_1'=2] {'row_0'}, use_global_device_ids=true, to_apply=%region_7.10 | all-reduce | flops 12288 | bytes 98304 | tf_op jit(solution)/shard_map/psum | solution.py:16
  142.7 14.2 %all-reduce.5 = (f32[64,64]{0,1:T(8,128)S(1)}, f32[64,64]{1,0:T(8,128)S(1)}, f32[64,64]{1,0:T(8,128)S(1)}) all-reduce(f32[64,64]{0,1:T(8,128)S(1)} %get-tuple-element.14, f32[64,64]{1,0:T(8,128)S(1)} %get-tuple-element.15, f32[64,64]{1,0:T(8,128)S(1)} %get-tuple-element.16), channel_id=1, replica_groups=mesh['row_0'=8,'row_1'=4,'col_0'=8,'col_1'=2] {'row_1'}, use_global_device_ids=true, to_apply=%region_8.11 | all-reduce | flops 12288 | bytes 98304 | tf_op jit(solution)/shard_map/psum | solution.py:16
  156.9 21.7 %all-reduce.1 = (f32[64,64]{0,1:T(8,128)S(1)}, f32[64,64]{1,0:T(8,128)S(1)}, f32[64,64]{1,0:T(8,128)S(1)}) all-reduce(f32[64,64]{0,1:T(8,128)S(1)} %get-tuple-element.20, f32[64,64]{1,0:T(8,128)S(1)} %get-tuple-element.21, f32[64,64]{1,0:T(8,128)S(1)} %get-tuple-element.22), channel_id=1, replica_groups=mesh['row_0'=8,'row_1'=4,'col_0'=8,'col_1'=2] {'col_0'}, use_global_device_ids=true, to_apply=%region_9.12 | all-reduce | flops 12288 | bytes 98304 | tf_op jit(solution)/shard_map/psum | solution.py:16
  178.6 21.3 %all-reduce.7 = (f32[64,64]{0,1:T(8,128)S(1)}, f32[64,64]{1,0:T(8,128)S(1)}, f32[64,64]{1,0:T(8,128)S(1)}) all-reduce(f32[64,64]{0,1:T(8,128)S(1)} %get-tuple-element.8, f32[64,64]{1,0:T(8,128)S(1)} %get-tuple-element.9, f32[64,64]{1,0:T(8,128)S(1)} %get-tuple-element.10), channel_id=1, replica_groups=mesh['row_0'=8,'row_1'=4,'col_0'=8,'col_1'=2] {'col_1'}, use_global_device_ids=true, to_apply=%region_10.13 | all-reduce | flops 12288 | bytes 98304 | tf_op jit(solution)/shard_map/psum | solution.py:16
  200.1 5.8 cholesky.89
  213.7 5.8 cholesky.100
  226.3 15.8 %all_gather.30 = bf16[64,512]{0,1:T(8,128)(2,1)S(1)} all-gather(bf16[64,32]{0,1:T(8,128)(2,1)S(1)} %get-tuple-element.31), channel_id=1, replica_groups=mesh['row_0'=8,'row_1'=4,'col_0'=8,'col_1'=2] {'col_0','col_1'}, dimensions={1}, use_global_device_ids=true | all-gather | bytes 69632 | tf_op jit(solution)/shard_map/all_gather | solution.py:86
  242.2 10.3 %all-gather.1 = bf16[64,2048]{0,1:T(8,128)(2,1)S(1)} all-gather(bf16[64,512]{0,1:T(8,128)(2,1)S(1)} %all_gather.30), channel_id=3, replica_groups=mesh['row_0'=8,'row_1'=4,'col_0'=8,'col_1'=2] {'row_1'}, dimensions={1}, use_global_device_ids=true | all-gather | bytes 327680 | tf_op jit(solution)/shard_map/all_gather | solution.py:22
  253.6 5.9 cholesky.122
  259.4 30.4 %all-gather.9.cloned.1.call-done = bf16[64,32,512]{2,0,1:T(8,128)(2,1)} async-done(((bf16[64,4,512]{2,0,1:T(8,128)(2,1)}), bf16[64,32,512]{2,0,1:T(8,128)(2,1)}) %all-gather.9.cloned.1.call-update) | async-done | bytes 2097168 | tf_op jit(solution)/shard_map/all_gather | solution.py:22
  303.5 12.2 %all-to-all-start.1 = ((f32[16,1,2048]{2,1,0:T(1,128)}), f32[16,1,2048]{2,1,0:T(1,128)S(1)}, u32[]{:S(2)}, u32[]{:S(2)}) async-start(f32[16,1,2048]{2,1,0:T(1,128)} %reshape.233), calls=%async_computation.1 | async-start | bytes 262144 | tf_op jit(solution)/shard_map/all_to_all | solution.py:34
  326.5 22.9 %all-reduce.2 = (f32[64,64]{1,0:T(8,128)S(1)}, f32[64,64]{1,0:T(8,128)S(1)}, f32[64,64]{1,0:T(8,128)S(1)}) all-reduce(f32[64,64]{1,0:T(8,128)S(1)} %fusion.78, f32[64,64]{1,0:T(8,128)S(1)} %fusion.81, f32[64,64]{1,0:T(8,128)S(1)} %fusion.79), channel_id=1, replica_groups=mesh['row_0'=8,'row_1'=4,'col_0'=8,'col_1'=2] {'row_0'}, use_global_device_ids=true, to_apply=%region_16.20 | all-reduce | flops 12288 | bytes 98304 | tf_op jit(solution)/shard_map/psum | solution.py:16
  349.4 14.2 %all-reduce.4 = (f32[64,64]{1,0:T(8,128)S(1)}, f32[64,64]{1,0:T(8,128)S(1)}, f32[64,64]{1,0:T(8,128)S(1)}) all-reduce(f32[64,64]{1,0:T(8,128)S(1)} %get-tuple-element.11, f32[64,64]{1,0:T(8,128)S(1)} %get-tuple-element.12, f32[64,64]{1,0:T(8,128)S(1)} %get-tuple-element.13), channel_id=1, replica_groups=mesh['row_0'=8,'row_1'=4,'col_0'=8,'col_1'=2] {'row_1'}, use_global_device_ids=true, to_apply=%region_17.21 | all-reduce | flops 12288 | bytes 98304 | tf_op jit(solution)/shard_map/psum | solution.py:16
  363.6 21.6 %all-reduce = (f32[64,64]{1,0:T(8,128)S(1)}, f32[64,64]{1,0:T(8,128)S(1)}, f32[64,64]{1,0:T(8,128)S(1)}) all-reduce(f32[64,64]{1,0:T(8,128)S(1)} %get-tuple-element.17, f32[64,64]{1,0:T(8,128)S(1)} %get-tuple-element.18, f32[64,64]{1,0:T(8,128)S(1)} %get-tuple-element.19), channel_id=1, replica_groups=mesh['row_0'=8,'row_1'=4,'col_0'=8,'col_1'=2] {'col_0'}, use_global_device_ids=true, to_apply=%region_18.22 | all-reduce | flops 12288 | bytes 98304 | tf_op jit(solution)/shard_map/psum | solution.py:16
  385.2 21.5 %all-reduce.6 = (f32[64,64]{1,0:T(8,128)S(1)}, f32[64,64]{1,0:T(8,128)S(1)}, f32[64,64]{1,0:T(8,128)S(1)}) all-reduce(f32[64,64]{1,0:T(8,128)S(1)} %get-tuple-element.4, f32[64,64]{1,0:T(8,128)S(1)} %get-tuple-element.6, f32[64,64]{1,0:T(8,128)S(1)} %get-tuple-element.7), channel_id=1, replica_groups=mesh['row_0'=8,'row_1'=4,'col_0'=8,'col_1'=2] {'col_1'}, use_global_device_ids=true, to_apply=%region_19.23 | all-reduce | flops 12288 | bytes 98304 | tf_op jit(solution)/shard_map/psum | solution.py:16
  406.9 5.8 cholesky.111
  414.1 4.9 custom-call.13
  420.9 15.6 %all_gather.33 = bf16[64,512]{0,1:T(8,128)(2,1)S(1)} all-gather(bf16[64,32]{0,1:T(8,128)(2,1)S(1)} %get-tuple-element.33), channel_id=1, replica_groups=mesh['row_0'=8,'row_1'=4,'col_0'=8,'col_1'=2] {'col_0','col_1'}, dimensions={1}, use_global_device_ids=true | all-gather | bytes 69632 | tf_op jit(solution)/shard_map/all_gather | solution.py:86
  436.4 10.3 %all-gather.2 = bf16[64,2048]{0,1:T(8,128)(2,1)S(1)} all-gather(bf16[64,512]{0,1:T(8,128)(2,1)S(1)} %all_gather.33), channel_id=4, replica_groups=mesh['row_0'=8,'row_1'=4,'col_0'=8,'col_1'=2] {'row_1'}, dimensions={1}, use_global_device_ids=true | all-gather | bytes 327680 | tf_op jit(solution)/shard_map/all_gather | solution.py:22
  447.6 37.4 %all-gather.11.cloned.1.call-done = bf16[64,32,512]{2,0,1:T(8,128)(2,1)} async-done(((bf16[64,4,512]{2,0,1:T(8,128)(2,1)}), bf16[64,32,512]{2,0,1:T(8,128)(2,1)}) %all-gather.11.cloned.1.call-update) | async-done | bytes 2097168 | tf_op jit(solution)/shard_map/all_gather | solution.py:22
  498.7 12.2 %all-to-all-start.2 = ((f32[16,1,2048]{2,1,0:T(1,128)}), f32[16,1,2048]{2,1,0:T(1,128)S(1)}, u32[]{:S(2)}, u32[]{:S(2)}) async-start(f32[16,1,2048]{2,1,0:T(1,128)} %reshape.235), calls=%async_computation.2 | async-start | bytes 262144 | tf_op jit(solution)/shard_map/all_to_all | solution.py:34
  511.2 8.6 %all-to-all-done.2 = f32[16,1,2048]{2,1,0:T(1,128)S(1)} async-done(((f32[16,1,2048]{2,1,0:T(1,128)}), f32[16,1,2048]{2,1,0:T(1,128)S(1)}, u32[]{:S(2)}, u32[]{:S(2)}) %all-to-all-start.2) | async-done | bytes 131104 | tf_op jit(solution)/shard_map/all_to_all | solution.py:34
  521.1 22.1 %psum.232 = f32[64,64]{1,0:T(8,128)S(1)} all-reduce(f32[64,64]{1,0:T(8,128)S(1)} %fusion.53), channel_id=1, replica_groups=mesh['row_0'=8,'row_1'=4,'col_0'=8,'col_1'=2] {'row_0'}, use_global_device_ids=true, to_apply=%region_29.33 | all-reduce | flops 4096 | bytes 32768 | tf_op jit(solution)/shard_map/psum | solution.py:16
  543.2 13.2 %psum.233 = f32[64,64]{1,0:T(8,128)S(1)} all-reduce(f32[64,64]{1,0:T(8,128)S(1)} %psum.232), channel_id=1, replica_groups=mesh['row_0'=8,'row_1'=4,'col_0'=8,'col_1'=2] {'row_1'}, use_global_device_ids=true, to_apply=%region_30.34 | all-reduce | flops 4096 | bytes 32768 | tf_op jit(solution)/shard_map/psum | solution.py:16
  556.4 20.4 %psum.234 = f32[64,64]{1,0:T(8,128)S(1)} all-reduce(f32[64,64]{1,0:T(8,128)S(1)} %psum.233), channel_id=1, replica_groups=mesh['row_0'=8,'row_1'=4,'col_0'=8,'col_1'=2] {'col_0'}, use_global_device_ids=true, to_apply=%region_31.35 | all-reduce | flops 4096 | bytes 32768 | tf_op jit(solution)/shard_map/psum | solution.py:16
  576.8 21.0 %psum.235 = f32[64,64]{1,0:T(8,128)S(1)} all-reduce(f32[64,64]{1,0:T(8,128)S(1)} %psum.234), channel_id=1, replica_groups=mesh['row_0'=8,'row_1'=4,'col_0'=8,'col_1'=2] {'col_1'}, use_global_device_ids=true, to_apply=%region_32.36 | all-reduce | flops 4096 | bytes 32768 | tf_op jit(solution)/shard_map/psum | solution.py:16
  598.0 5.8 cholesky.133
  (129 shorter events, 87.0 us)
Async XLA Ops:
  7.2 85.4 %copy-start = (bf16[1,32,1,128,128]{4,3,2,1,0:T(8,128)(2,1)S(1)}, bf16[1,32,1,128,128]{4,3,2,1,0:T(8,128)(2,1)}, u32[]{:S(2)}) copy-start(bf16[1,32,1,128,128]{4,3,2,1,0:T(8,128)(2,1)} %param.13) | copy-start | bytes 3145732
  7.2 75.7 %all-gather.7.cloned.1.call-start = ((), (), s32[]{:S(2)}) async-start(), calls=%async_computation.3 | async-start | bytes 2359296 | tf_op jit(solution)/shard_map/all_gather | solution.py:22
  91.2 3.3 copy-start.3
  92.6 16.2 %copy-start.1 = (f32[64,32]{0,1:T(8,128)S(1)}, f32[64,32]{0,1:T(8,128)}, u32[]{:S(2)}) copy-start(f32[64,32]{0,1:T(8,128)} %param.11) | copy-start | bytes 24580
  94.5 24.7 %copy-start.2 = (f32[32]{0:T(128)S(1)}, f32[32]{0:T(128)}, u32[]{:S(2)}) copy-start(f32[32]{0:T(128)} %param.12) | copy-start | bytes 388
  96.5 21.1 %all-to-all-start = ((f32[16,1,2048]{2,1,0:T(1,128)}), f32[16,1,2048]{2,1,0:T(1,128)S(1)}, u32[]{:S(2)}, u32[]{:S(2)}) async-start(f32[16,1,2048]{2,1,0:T(1,128)} %reshape.231), calls=%async_computation | async-start | bytes 262144 | tf_op jit(solution)/shard_map/all_to_all | solution.py:34
  108.7 181.2 %all-gather.9.cloned.1.call-start = ((), (), s32[]{:S(2)}) async-start(), calls=%async_computation.4 | async-start | bytes 2359296 | tf_op jit(solution)/shard_map/all_gather | solution.py:22
  303.5 21.1 %all-to-all-start.1 = ((f32[16,1,2048]{2,1,0:T(1,128)}), f32[16,1,2048]{2,1,0:T(1,128)S(1)}, u32[]{:S(2)}, u32[]{:S(2)}) async-start(f32[16,1,2048]{2,1,0:T(1,128)} %reshape.233), calls=%async_computation.1 | async-start | bytes 262144 | tf_op jit(solution)/shard_map/all_to_all | solution.py:34
  315.7 169.4 %all-gather.11.cloned.1.call-start = ((), (), s32[]{:S(2)}) async-start(), calls=%async_computation.5 | async-start | bytes 2359296 | tf_op jit(solution)/shard_map/all_gather | solution.py:22
  498.7 21.1 %all-to-all-start.2 = ((f32[16,1,2048]{2,1,0:T(1,128)}), f32[16,1,2048]{2,1,0:T(1,128)S(1)}, u32[]{:S(2)}, u32[]{:S(2)}) async-start(f32[16,1,2048]{2,1,0:T(1,128)} %reshape.235), calls=%async_computation.2 | async-start | bytes 262144 | tf_op jit(solution)/shard_map/all_to_all | solution.py:34
Sparse Core Ops, SparseCore 0:
  44.9 37.8 all-gather.6
  253.5 36.3 all-gather.8
  447.8 37.2 all-gather.10
where the time goes:
time: 620 us; the launch traced here: 619 us
  blocking collectives  325 us (52%)
  waiting for transfers between devices  124 us (20%)
  other arithmetic  65.6 us (11%)
  starting transfers between devices  37 us (6%)
  local copies, waits for them, and re-layouts  36.5 us (6%)
  matrix products  16.2 us (3%)
  between operations  14.4 us (2%)
    psum x12, blocking collectives, one_axis_at_a_time(): shard = lax.psum(shard, axis)  237 us
    all_gather x3, waiting for transfers between devices, gather_axes(): shard = lax.all_gather(shard, axis, axis=dim, tiled=True)  105 us
    all_gather x3, blocking collectives, body(): own_rows = lax.all_gather(dir_bf, COL, axis=1, tiled=True)  56.2 us
    all_to_all x3, starting transfers between devices, sum_at_owner(): lax.all_to_all(in_blocks(shard, dim, peers), axis, 0, 0, tiled=True)  36.7 us
    another operation x15, other arithmetic, chol_solve(): factor = jnp.linalg.cholesky(matrix)  32.6 us
    all_gather x3, blocking collectives, gather_axes(): shard = lax.all_gather(shard, axis, axis=dim, tiled=True)  31.5 us
    another operation x10, other arithmetic, chol_solve(): return jax.scipy.linalg.cho_solve((factor, True), rhs_mat)  27.7 us
    all_to_all x3, waiting for transfers between devices, sum_at_owner(): lax.all_to_all(in_blocks(shard, dim, peers), axis, 0, 0, tiled=True)  19.6 us
  transfers between devices with their start and end apart: 6, of which 6 were waited for; matrix products, arithmetic and copies ran while one was open for 2% of the time, Pallas kernels for 0%

commit v1 on v0

v1 whole, which is shorter than its diff:
```python
import functools

import jax
import jax.numpy as jnp
from jax import lax
from jax.experimental import pallas as pl
from jax.experimental.pallas import tpu as pltpu
from jax.sharding import Mesh
from jax.sharding import PartitionSpec as P

ITERS = 3
COL = ("col_0", "col_1")
ROW = ("row_0", "row_1")
ROW_COL = ROW + COL
F32 = jnp.float32
BF16 = jnp.bfloat16
SMP = 64
LANE = 128
BLKS = 4
COLS = 16
PIECE = 32
NT = (((1,), (1,)), ((), ()))
NN = (((1,), (0,)), ((), ()))
VMEM = pl.BlockSpec(memory_space=pltpu.VMEM)
SMEM = pl.BlockSpec(memory_space=pltpu.SMEM)


def exact_dot(left, right, dims):
    return lax.dot_general(
        left, right, dims, precision=lax.Precision.HIGHEST, preferred_element_type=F32
    )


def swap(msg, axes):
    return lax.all_to_all(msg, axes, 0, 0, tiled=True)


def call(kernel, in_specs, outs, scratch, name):
    return pl.pallas_call(
        kernel,
        in_specs=in_specs,
        out_specs=[VMEM] * len(outs),
        out_shape=[jax.ShapeDtypeStruct(s, d) for s, d in outs],
        scratch_shapes=scratch,
        name=name,
    )


def pack_kernel(right_ref, reg_ref, out_ref):
    packed = jnp.concatenate([right_ref[16 * j : 16 * j + 16, :] for j in range(4)], axis=1)
    reg_row = jnp.concatenate([reg_ref[...], jnp.zeros((1, LANE - PIECE), F32)], axis=1)
    reg_tile = jnp.broadcast_to(reg_row, (8, LANE))
    for k in range(COLS):
        out_ref[k, 0:16, :] = packed
        out_ref[k, 16:24, :] = reg_tile


def emit_blocks(rows_ref, half_ref, sel_ref):
    for s in range(sel_ref.shape[0]):
        sel_ref[s] = half_ref[rows_ref[s]]


def unpack_kernel(rows_ref, got_ref, res_ref, reg_ref, sel_ref, half_ref):
    group = lax.broadcasted_iota(jnp.int32, (16, LANE), 1) // PIECE
    for b in range(BLKS):
        for j in range(4):
            piece = jnp.zeros((16, LANE), F32)
            for m in range(4):
                shift = (PIECE * (m - j)) % LANE
                part = got_ref[4 * b + m, 0:16, :]
                part = pltpu.roll(part, shift, 1) if shift else part
                piece = jnp.where(group == m, part, piece)
            res_ref[b, 16 * j : 16 * j + 16, :] = piece
            half_ref[b, 16 * j : 16 * j + 16, :] = piece.astype(BF16)
        reg = jnp.zeros((8, LANE), F32)
        for m in range(4):
            part = got_ref[4 * b + m, 16:24, :]
            part = pltpu.roll(part, PIECE * m, 1) if m else part
            reg = jnp.where(group[0:8] == m, part, reg)
        reg_ref[b] = reg
    emit_blocks(rows_ref, half_ref, sel_ref)


def product_kernel(first, *refs):
    rows_ref, counts_ref, chosen_ref, curv_ref, res_ref, reg_ref = refs[:6]
    if first:
        out_ref, acc_ref = refs[6:]
    else:
        img_ref, dir_ref, out_ref, acc_ref = refs[6:]
    acc_ref[...] = jnp.zeros_like(acc_ref)
    for s in range(chosen_ref.shape[0]):
        prod = lax.dot_general(chosen_ref[s], curv_ref[s], NT, preferred_element_type=F32)
        row = rows_ref[s]
        acc_ref[row] = acc_ref[row] + jnp.where(counts_ref[s] > 0, prod, 0.0)
    share = 1.0 / COLS
    pair = jnp.zeros((SMP, LANE), F32)
    mixed = jnp.zeros((SMP, SMP), F32)
    for b in range(BLKS):
        res = res_ref[b]
        part = acc_ref[b] + reg_ref[b, 0:1, :] * res * share
        pair += exact_dot(res, jnp.concatenate([part, res * share], axis=0), NT)
        if not first:
            mixed += exact_dot(res, img_ref[b] * share, NT) + exact_dot(part, dir_ref[b], NT)
    other = jnp.concatenate([mixed, jnp.zeros((SMP, LANE - SMP), F32)], axis=1)
    for k in range(COLS):
        m = k % 4
        out_ref[k, 0:16, :] = acc_ref[k // 4, 16 * m : 16 * m + 16, :]
        source = pair if k < 8 else other
        n = k % 8
        out_ref[k, 16:24, :] = source[8 * n : 8 * n + 8, :]


def col_sum_kernel(got_ref, gram_ref, piece_ref):
    total = got_ref[0]
    for k in range(1, COLS):
        total = total + got_ref[k]
    piece_ref[...] = total[0:16, :]
    gram = total[16:24, :]
    for r in range(gram_ref.shape[0]):
        gram_ref[r] = gram


def row_sum_kernel(got_ref, piece_ref, out_ref):
    total = got_ref[0]
    for r in range(1, got_ref.shape[0]):
        total = total + got_ref[r]
    piece = piece_ref[...]
    for k in range(COLS):
        out_ref[k, 0:16, :] = piece
        out_ref[k, 16:24, :] = total


def factor(matrices):
    row_id = lax.broadcasted_iota(jnp.int32, (8, LANE), 0)
    lane_id = lax.broadcasted_iota(jnp.int32, (SMP, SMP), 1)
    eye = (lax.broadcasted_iota(jnp.int32, (SMP, SMP), 0) == lane_id).astype(F32)
    work = []
    for matrix in matrices:
        wide = jnp.concatenate([matrix, eye], axis=1)
        work.append([wide[8 * t : 8 * t + 8, :] for t in range(8)])
    for j in range(SMP):
        top, low = divmod(j, 8)
        for tiles in work:
            pivot = tiles[top][low : low + 1, :]
            scaled = pivot / pivot[:, j : j + 1]
            for t in range(top, 8):
                column = tiles[t][:, j : j + 1]
                change = column * scaled
                if t == top:
                    if low == 7:
                        continue
                    change = jnp.where(row_id > low, change, 0.0)
                tiles[t] = tiles[t] - change
    done = []
    for tiles in work:
        wide = jnp.concatenate(tiles, axis=0)
        upper = wide[:, 0:SMP]
        inverse = pltpu.roll(wide, SMP, 1)[:, 0:SMP]
        diag = jnp.sum(upper * eye, axis=1, keepdims=True)
        done.append((inverse, inverse / diag))
    return done


def solve_kernel(first, last, *refs):
    refs = list(refs)
    rows_ref = refs.pop(0)
    got_ref, res_ref, reg_ref = refs[:3]
    refs = refs[3:]
    if not first:
        dir_ref, img_ref, sol_ref, inv_ref, scaled_ref, curv_ref = refs[:6]
        refs = refs[6:]
    if last:
        out_sol_ref, out_res_ref, keep_ref = refs
    else:
        new_res_ref, new_dir_ref, new_img_ref, new_sol_ref = refs[:4]
        new_inv_ref, new_scaled_ref, new_curv_ref, sel_ref, half_ref = refs[4:]
    pair = jnp.concatenate([got_ref[k, 16:24, :] for k in range(8)], axis=0)
    gram = pltpu.roll(pair, SMP, 1)[:, 0:SMP]
    curv = pair[:, 0:SMP]
    if not first:
        mixed = jnp.concatenate([got_ref[k, 16:24, :] for k in range(8, 16)], axis=0)[:, 0:SMP]
        beta_t = exact_dot(exact_dot(gram, inv_ref[...], NT), scaled_ref[...], NN)
        curv = curv + exact_dot(mixed + exact_dot(beta_t, curv_ref[...], NN), beta_t, NT)
    curv = 0.5 * (curv + curv.T)
    if last:
        ((inv_c, scaled_c),) = factor([curv])
    else:
        (inv_c, scaled_c), (inv_g, scaled_g) = factor([curv, gram])
        new_inv_ref[...] = inv_g
        new_scaled_ref[...] = scaled_g
        new_curv_ref[...] = curv
    alpha_t = exact_dot(exact_dot(gram, inv_c, NT), scaled_c, NN)
    for b in range(BLKS):
        res = res_ref[b]
        coupled = jnp.concatenate([got_ref[4 * b + m, 0:16, :] for m in range(4)], axis=0)
        image = coupled + reg_ref[b, 0:1, :] * res
        direction = res
        if not first:
            image = image + exact_dot(beta_t, img_ref[b], NN)
            direction = direction + exact_dot(beta_t, dir_ref[b], NN)
        new_res = res - exact_dot(alpha_t, image, NN)
        new_sol = exact_dot(alpha_t, direction, NN)
        if not first:
            new_sol = sol_ref[b] + new_sol
        if last:
            keep_ref[0, b] = new_sol
            keep_ref[1, b] = new_res
        else:
            new_res_ref[b] = new_res
            half_ref[b] = new_res.astype(BF16)
            new_dir_ref[b] = direction
            new_img_ref[b] = image
            new_sol_ref[b] = new_sol
    if last:
        mine = rows_ref[0]
        shift = (LANE - PIECE * (mine % 4)) % LANE
        out_sol_ref[...] = pltpu.roll(keep_ref[0, mine // 4], shift, 1)[:, 0:PIECE]
        out_res_ref[...] = pltpu.roll(keep_ref[1, mine // 4], shift, 1)[:, 0:PIECE]
    else:
        emit_blocks(rows_ref, half_ref, sel_ref)


def body(right_side, regular, curvature, block_rows, block_cols, block_counts):
    sources = block_rows.shape[1]
    curv = curvature.reshape(sources, LANE, LANE)
    rows = block_rows.reshape(sources)
    counts = block_counts.reshape(sources)
    field = ((BLKS, SMP, LANE), F32)
    small = ((SMP, SMP), F32)
    sel = ((sources, SMP, LANE), BF16)
    msg = ((COLS, 24, LANE), F32)
    half = pltpu.VMEM((BLKS, SMP, LANE), BF16)

    (packed,) = call(pack_kernel, [VMEM] * 2, [msg], [], "pack")(
        right_side, regular.reshape(1, PIECE)
    )
    res, reg, out = call(
        unpack_kernel, [SMEM, VMEM], [field, ((BLKS, 8, LANE), F32), sel], [half], "unpack"
    )(rows, swap(packed, COL))
    state = []
    for step in range(ITERS):
        first, last = step == 0, step == ITERS - 1
        chosen = swap(out, ROW)
        before = [] if first else [state[1], state[0]]
        (part,) = call(
            functools.partial(product_kernel, first),
            [SMEM, SMEM] + [VMEM] * (4 + len(before)),
            [msg],
            [pltpu.VMEM((BLKS, SMP, LANE), F32)],
            f"product_{step}",
        )(rows, counts, chosen, curv, res, reg, *before)
        gram, piece = call(
            col_sum_kernel,
            [VMEM],
            [((sources, 8, LANE), F32), ((16, LANE), F32)],
            [],
            f"col_sum_{step}",
        )(swap(part, COL))
        (whole,) = call(row_sum_kernel, [VMEM] * 2, [msg], [], f"row_sum_{step}")(
            swap(gram, ROW), piece
        )
        got = swap(whole, COL)
        specs = [SMEM] + [VMEM] * (3 + len(state))
        solve = functools.partial(solve_kernel, first, last)
        if last:
            mine = lax.axis_index(COL).astype(jnp.int32).reshape(1)
            share = ((SMP, PIECE), F32)
            keep = pltpu.VMEM((2, BLKS, SMP, LANE), F32)
            return tuple(
                call(solve, specs, [share, share], [keep], f"solve_{step}")(
                    mine, got, res, reg, *state
                )
            )
        outs = [field] * 4 + [small] * 3 + [sel]
        res, *state, out = call(solve, specs, outs, [half], f"solve_{step}")(
            rows, got, res, reg, *state
        )


def solution(mesh):
    finer = Mesh(mesh.devices.reshape(8, 4, 8, 2), ROW_COL)
    placed = (
        P(None, ROW_COL),
        P(ROW_COL),
        P(ROW, None, COL, None, None),
        P(ROW, None, COL),
        P(ROW, None, COL),
        P(ROW, None, COL),
    )
    return jax.shard_map(
        body,
        mesh=finer,
        in_specs=placed,
        out_specs=(P(None, ROW_COL), P(None, ROW_COL)),
        check_vma=False,
    )
```

time: 620 us -> 290 us (0.47)
  waiting for transfers between devices: 124 us -> 10.3 us
  blocking collectives: 325 us -> 215 us
  other arithmetic: 65.6 us -> 0 us
  Pallas kernels: 0 us -> 53.7 us
  local copies, waits for them, and re-layouts: 36.5 us -> 4.21 us
  starting transfers between devices: 37 us -> 4.89 us
  matrix products: 16.2 us -> 0 us
  between operations: 14.4 us -> 0.65 us
    psum x12 -> x0, blocking collectives: 237 us -> none  [one_axis_at_a_time(): shard = lax.psum(shard, axis)]
    all_to_all x0 -> x12, blocking collectives: none -> 215 us  [swap(): return lax.all_to_all(msg, axes, 0, 0, tiled=True)]
    all_gather x3 -> x0, waiting for transfers between devices: 105 us -> none  [gather_axes(): shard = lax.all_gather(shard, axis, axis=dim, tiled=True)]
    all_gather x6 -> x0, blocking collectives: 87.8 us -> none  [the longest x3 56.2 us: body(): own_rows = lax.all_gather(dir_bf, COL, axis=1, tiled=True)]
    another operation x25 -> x0, other arithmetic: 60.3 us -> none  [the longest x15 32.6 us: chol_solve(): factor = jnp.linalg.cholesky(matrix)]
    pallas_call x0 -> x14, Pallas kernels: none -> 53.7 us  [the longest x2 19 us: body(): call(solve, specs, outs, [half], f'solve_{step}')]
    all_to_all x3 -> x1, starting transfers between devices: 36.7 us -> 4.89 us  [swap(): return lax.all_to_all(msg, axes, 0, 0, tiled=True)]
    reshape x6 -> x0, local copies, waits for them, and re-layouts: 16.6 us -> none  [apply_terms(): flat_dirs = dir_piece.reshape(samples, sources * blocks_dev, block_len)]
  transfers between devices with their start and end apart: 6 -> 1, of which waited for: 6 -> 1; matrix products, arithmetic and copies ran while one was open for 2% -> 0% of each run, Pallas kernels for 0% -> 0%
where the time goes in v1:
time: 290 us; the launch traced here: 288 us
  blocking collectives  215 us (74%)
  Pallas kernels  53.7 us (19%)
  waiting for transfers between devices  10.3 us (4%)
  starting transfers between devices  4.89 us (2%)
  local copies, waits for them, and re-layouts  4.21 us (1%)
    all_to_all x12, blocking collectives, swap(): return lax.all_to_all(msg, axes, 0, 0, tiled=True)  215 us
    pallas_call x2, Pallas kernels, body(): call(solve, specs, outs, [half], f'solve_{step}')  19 us
    pallas_call x3, Pallas kernels, body(): call(functools.partial(product_kernel, first), [SMEM, SMEM] + [VMEM] * (4...  12.1 us
    all_to_all x1, waiting for transfers between devices, swap(): return lax.all_to_all(msg, axes, 0, 0, tiled=True)  10.3 us
    pallas_call x1, Pallas kernels, body(): call(solve, specs, [share, share], [keep], f'solve_{step}')  9.44 us
  transfers between devices with their start and end apart: 1, of which 1 were waited for; matrix products, arithmetic and copies ran while one was open for 0% of the time, Pallas kernels for 0%

profile of v1, /device:TPU:1, one launch (start us, length us, event | category | flops | bytes accessed | tf_op | source)
XLA Modules:
  0.0 288.5 jit_solution(8751195715016329081)
XLA Ops:
  0.6 1.4 copy.7.right_ref
  2.0 1.5 pack.1
  3.5 22.1 %all_to_all.65.got_ref = f32[16,24,128]{2,1,0:T(8,128)} all-to-all(f32[16,24,128]{2,1,0:T(8,128)} %pack.1), channel_id=1, replica_groups=mesh['row_0'=8,'row_1'=4,'col_0'=8,'col_1'=2] {'col_0','col_1'}, dimensions={0} | all-to-all | bytes 393216 | tf_op jit(solution)/shard_map/all_to_all | solution.py:35
  25.7 2.0 unpack.1
  27.6 26.8 %all_to_all.66.refs_2_ = bf16[32,64,128]{2,1,0:T(8,128)(2,1)} all-to-all(bf16[32,64,128]{2,1,0:T(8,128)(2,1)} %get-tuple-element.27), channel_id=1, replica_groups=mesh['row_0'=8,'row_1'=4,'col_0'=8,'col_1'=2] {'row_0','row_1'}, dimensions={0} | all-to-all | bytes 1048576 | tf_op jit(solution)/shard_map/all_to_all | solution.py:35
  54.4 4.1 %product_0.1 = f32[16,24,128]{2,1,0:T(8,128)} custom-call(s32[32]{0:T(128)} %bitcast.9, s32[32]{0:T(128)} %bitcast.14, bf16[32,64,128]{2,1,0:T(8,128)(2,1)} %all_to_all.66.refs_2_, bf16[32,128,128]{2,1,0:T(8,128)(2,1)} %bitcast.5, f32[4,64,128]{2,1,0:T(8,128)} %get-tuple-element.28.refs_4_.refs_2_, f32[4,8,128]{2,1,0:T(8,128)} %get-tuple-element.29.refs_5_.refs_3_), custom_call_target="tpu_custom_call" | custom-call | tf_op jit(solution)/shard_map/product_0/pallas_call | solution.py:245
  58.6 15.7 %all_to_all.67.got_ref = f32[16,24,128]{2,1,0:T(8,128)} all-to-all(f32[16,24,128]{2,1,0:T(8,128)} %product_0.1), channel_id=1, replica_groups=mesh['row_0'=8,'row_1'=4,'col_0'=8,'col_1'=2] {'col_0','col_1'}, dimensions={0} | all-to-all | bytes 393216 | tf_op jit(solution)/shard_map/all_to_all | solution.py:35
  74.3 1.6 col_sum_0.1
  75.9 14.6 %all_to_all.68.got_ref = f32[32,8,128]{2,1,0:T(8,128)} all-to-all(f32[32,8,128]{2,1,0:T(8,128)} %get-tuple-element.30), channel_id=1, replica_groups=mesh['row_0'=8,'row_1'=4,'col_0'=8,'col_1'=2] {'row_0','row_1'}, dimensions={0} | all-to-all | bytes 262144 | tf_op jit(solution)/shard_map/all_to_all | solution.py:35
  90.5 1.6 row_sum_0.1
  92.1 15.8 %all_to_all.69.refs_1_ = f32[16,24,128]{2,1,0:T(8,128)} all-to-all(f32[16,24,128]{2,1,0:T(8,128)} %row_sum_0.1), channel_id=1, replica_groups=mesh['row_0'=8,'row_1'=4,'col_0'=8,'col_1'=2] {'col_0','col_1'}, dimensions={0} | all-to-all | bytes 393216 | tf_op jit(solution)/shard_map/all_to_all | solution.py:35
  108.0 8.5 %solve_0.1 = (f32[4,64,128]{2,1,0:T(8,128)}, f32[4,64,128]{2,1,0:T(8,128)}, f32[4,64,128]{2,1,0:T(8,128)}, f32[4,64,128]{2,1,0:T(8,128)}, f32[64,64]{1,0:T(8,128...) custom-call(s32[32]{0:T(128)} %bitcast.10, f32[16,24,128]{2,1,0:T(8,128)} %all_to_all.69.refs_1_, ...), custom_call_target="tpu_custom_call" | custom-call | tf_op jit(solution)/shard_map/solve_0/pallas_call | solution.py:275
  116.4 21.9 %all_to_all.70.refs_2_ = bf16[32,64,128]{2,1,0:T(8,128)(2,1)} all-to-all(bf16[32,64,128]{2,1,0:T(8,128)(2,1)} %get-tuple-element.32), channel_id=1, replica_groups=mesh['row_0'=8,'row_1'=4,'col_0'=8,'col_1'=2] {'row_0','row_1'}, dimensions={0} | all-to-all | bytes 1048576 | tf_op jit(solution)/shard_map/all_to_all | solution.py:35
  138.3 4.0 %product_1.1 = f32[16,24,128]{2,1,0:T(8,128)} custom-call(s32[32]{0:T(128)} %bitcast.11, s32[32]{0:T(128)} %bitcast.15, bf16[32,64,128]{2,1,0:T(8,128)(2,1)} %all_to_all.70.refs_2_, bf16[32,128,128]{2,1,0:T(8,128)(2,1)} %bitcast.6, f32[4,64,128]{2,1,0:T(8,128)} %get-tuple-element.33.refs_4_.refs_2_, f32[4,8,128]{2,1,0:T(8,128)} %get-tuple-element.29.refs_5_.refs_3_, ...), custom_call_target="tpu_custom_call" | custom-call | tf_op jit(solution)/shard_map/product_1/pallas_call | solution.py:245
  142.3 15.1 %all_to_all.71.got_ref = f32[16,24,128]{2,1,0:T(8,128)} all-to-all(f32[16,24,128]{2,1,0:T(8,128)} %product_1.1), channel_id=1, replica_groups=mesh['row_0'=8,'row_1'=4,'col_0'=8,'col_1'=2] {'col_0','col_1'}, dimensions={0} | all-to-all | bytes 393216 | tf_op jit(solution)/shard_map/all_to_all | solution.py:35
  157.4 1.6 col_sum_1.1
  159.0 15.0 %all_to_all.72.got_ref = f32[32,8,128]{2,1,0:T(8,128)} all-to-all(f32[32,8,128]{2,1,0:T(8,128)} %get-tuple-element.36), channel_id=1, replica_groups=mesh['row_0'=8,'row_1'=4,'col_0'=8,'col_1'=2] {'row_0','row_1'}, dimensions={0} | all-to-all | bytes 262144 | tf_op jit(solution)/shard_map/all_to_all | solution.py:35
  174.0 1.6 row_sum_1.1
  175.6 15.8 %all_to_all.73.refs_1_ = f32[16,24,128]{2,1,0:T(8,128)} all-to-all(f32[16,24,128]{2,1,0:T(8,128)} %row_sum_1.1), channel_id=1, replica_groups=mesh['row_0'=8,'row_1'=4,'col_0'=8,'col_1'=2] {'col_0','col_1'}, dimensions={0} | all-to-all | bytes 393216 | tf_op jit(solution)/shard_map/all_to_all | solution.py:35
  191.4 10.5 %solve_1.1 = (f32[4,64,128]{2,1,0:T(8,128)}, f32[4,64,128]{2,1,0:T(8,128)}, f32[4,64,128]{2,1,0:T(8,128)}, f32[4,64,128]{2,1,0:T(8,128)}, f32[64,64]{1,0:T(8,128...) custom-call(s32[32]{0:T(128)} %bitcast.12, f32[16,24,128]{2,1,0:T(8,128)} %all_to_all.73.refs_1_, ...), custom_call_target="tpu_custom_call" | custom-call | tf_op jit(solution)/shard_map/solve_1/pallas_call | solution.py:275
  201.9 21.9 %all_to_all.74.refs_2_ = bf16[32,64,128]{2,1,0:T(8,128)(2,1)} all-to-all(bf16[32,64,128]{2,1,0:T(8,128)(2,1)} %get-tuple-element.42), channel_id=1, replica_groups=mesh['row_0'=8,'row_1'=4,'col_0'=8,'col_1'=2] {'row_0','row_1'}, dimensions={0} | all-to-all | bytes 1048576 | tf_op jit(solution)/shard_map/all_to_all | solution.py:35
  223.8 4.0 %product_2.1 = f32[16,24,128]{2,1,0:T(8,128)} custom-call(s32[32]{0:T(128)} %bitcast.13, s32[32]{0:T(128)} %bitcast.16, bf16[32,64,128]{2,1,0:T(8,128)(2,1)} %all_to_all.74.refs_2_, bf16[32,128,128]{2,1,0:T(8,128)(2,1)} %bitcast.7, f32[4,64,128]{2,1,0:T(8,128)} %get-tuple-element.43.refs_4_.refs_2_, f32[4,8,128]{2,1,0:T(8,128)} %get-tuple-element.29.refs_5_.refs_3_, ...), custom_call_target="tpu_custom_call" | custom-call | tf_op jit(solution)/shard_map/product_2/pallas_call | solution.py:245
  227.7 15.1 %all_to_all.75.got_ref = f32[16,24,128]{2,1,0:T(8,128)} all-to-all(f32[16,24,128]{2,1,0:T(8,128)} %product_2.1), channel_id=1, replica_groups=mesh['row_0'=8,'row_1'=4,'col_0'=8,'col_1'=2] {'col_0','col_1'}, dimensions={0} | all-to-all | bytes 393216 | tf_op jit(solution)/shard_map/all_to_all | solution.py:35
  242.9 1.6 col_sum_2.1
  244.5 15.0 %all_to_all.76.got_ref = f32[32,8,128]{2,1,0:T(8,128)} all-to-all(f32[32,8,128]{2,1,0:T(8,128)} %get-tuple-element.46), channel_id=1, replica_groups=mesh['row_0'=8,'row_1'=4,'col_0'=8,'col_1'=2] {'row_0','row_1'}, dimensions={0} | all-to-all | bytes 262144 | tf_op jit(solution)/shard_map/all_to_all | solution.py:35
  259.4 1.6 row_sum_2.1
  261.1 4.9 %all-to-all-start.12 = ((f32[16,24,128]{2,1,0:T(8,128)}), f32[16,24,128]{2,1,0:T(8,128)S(1)}, u32[]{:S(2)}, u32[]{:S(2)}) async-start(f32[16,24,128]{2,1,0:T(8,128)} %row_sum_2.1), calls=%async_computation.12 | async-start | bytes 393216 | tf_op jit(solution)/shard_map/all_to_all | solution.py:35
  265.9 10.3 %all-to-all-done.12.refs_1_ = f32[16,24,128]{2,1,0:T(8,128)S(1)} async-done(((f32[16,24,128]{2,1,0:T(8,128)}), f32[16,24,128]{2,1,0:T(8,128)S(1)}, u32[]{:S(2)}, u32[]{:S(2)}) %all-to-all-start.12) | async-done | bytes 196640 | tf_op jit(solution)/shard_map/all_to_all | solution.py:35
  276.2 0.7 copy-done
  276.9 9.4 %solve_2.1 = (f32[64,32]{1,0:T(8,128)}, f32[64,32]{1,0:T(8,128)}) custom-call(s32[1]{0:T(128)} %bitcast.refs_0_, f32[16,24,128]{2,1,0:T(8,128)} %copy-done, f32[4,64,128]{2,1,0:T(8,128)} %get-tuple-element.43.refs_4_.refs_2_, f32[4,8,128]{2,1,0:T(8,128)} %get-tuple-element.29.refs_5_.refs_3_, f32[4,64,128]{2,1,0:T(8,128)} %get-tuple-element.45.refs_7_.refs_4_, ...), custom_call_target="tpu_custom_call" | custom-call | tf_op jit(solution)/shard_map/solve_2/pallas_call | solution.py:270
  286.3 1.4 copy.8
  287.8 0.7 copy.9
  (3 shorter events, 0.0 us)
Async XLA Ops:
  261.1 15.2 %all-to-all-start.12 = ((f32[16,24,128]{2,1,0:T(8,128)}), f32[16,24,128]{2,1,0:T(8,128)S(1)}, u32[]{:S(2)}, u32[]{:S(2)}) async-start(f32[16,24,128]{2,1,0:T(8,128)} %row_sum_2.1), calls=%async_computation.12 | async-start | bytes 393216 | tf_op jit(solution)/shard_map/all_to_all | solution.py:35
  276.2 0.7 copy-start
  286.3 1.4 copy-start.1

commit v2 on v1

--- a/solution.py
+++ b/solution.py
@@ -35,19 +35,29 @@
     return lax.all_to_all(msg, axes, 0, 0, tiled=True)
 
 
-def call(kernel, in_specs, outs, scratch, name):
-    return pl.pallas_call(
+def call(kernel, in_specs, outs, scratch, name, make=pltpu.VMEM):
+    run = pl.pallas_call(
         kernel,
         in_specs=in_specs,
         out_specs=[VMEM] * len(outs),
-        out_shape=[jax.ShapeDtypeStruct(s, d) for s, d in outs],
+        out_shape=[make(s, d) for s, d in outs],
         scratch_shapes=scratch,
         name=name,
     )
 
+    def placed(*args):
+        near = [
+            pltpu.with_memory_space_constraint(arg, pltpu.VMEM) if spec is VMEM else arg
+            for spec, arg in zip(in_specs, args, strict=True)
+        ]
+        return run(*near)
+
+    return placed
+
 
 def pack_kernel(right_ref, reg_ref, out_ref):
-    packed = jnp.concatenate([right_ref[16 * j : 16 * j + 16, :] for j in range(4)], axis=1)
+    right = right_ref[...].T
+    packed = jnp.concatenate([right[16 * j : 16 * j + 16, :] for j in range(4)], axis=1)
     reg_row = jnp.concatenate([reg_ref[...], jnp.zeros((1, LANE - PIECE), F32)], axis=1)
     reg_tile = jnp.broadcast_to(reg_row, (8, LANE))
     for k in range(COLS):
@@ -214,8 +224,8 @@
     if last:
         mine = rows_ref[0]
         shift = (LANE - PIECE * (mine % 4)) % LANE
-        out_sol_ref[...] = pltpu.roll(keep_ref[0, mine // 4], shift, 1)[:, 0:PIECE]
-        out_res_ref[...] = pltpu.roll(keep_ref[1, mine // 4], shift, 1)[:, 0:PIECE]
+        out_sol_ref[...] = pltpu.roll(keep_ref[0, mine // 4], shift, 1)[:, 0:PIECE].T
+        out_res_ref[...] = pltpu.roll(keep_ref[1, mine // 4], shift, 1)[:, 0:PIECE].T
     else:
         emit_blocks(rows_ref, half_ref, sel_ref)
 
@@ -232,7 +242,7 @@
     half = pltpu.VMEM((BLKS, SMP, LANE), BF16)
 
     (packed,) = call(pack_kernel, [VMEM] * 2, [msg], [], "pack")(
-        right_side, regular.reshape(1, PIECE)
+        right_side.T, regular.reshape(1, PIECE)
     )
     res, reg, out = call(
         unpack_kernel, [SMEM, VMEM], [field, ((BLKS, 8, LANE), F32), sel], [half], "unpack"
@@ -264,13 +274,12 @@
         solve = functools.partial(solve_kernel, first, last)
         if last:
             mine = lax.axis_index(COL).astype(jnp.int32).reshape(1)
-            share = ((SMP, PIECE), F32)
+            share = ((PIECE, SMP), F32)
             keep = pltpu.VMEM((2, BLKS, SMP, LANE), F32)
-            return tuple(
-                call(solve, specs, [share, share], [keep], f"solve_{step}")(
-                    mine, got, res, reg, *state
-                )
-            )
+            shares = call(
+                solve, specs, [share, share], [keep], f"solve_{step}", jax.ShapeDtypeStruct
+            )(mine, got, res, reg, *state)
+            return tuple(part.T for part in shares)
         outs = [field] * 4 + [small] * 3 + [sel]
         res, *state, out = call(solve, specs, outs, [half], f"solve_{step}")(
             rows, got, res, reg, *state

time: 290 us -> 255 us (0.88)
  Pallas kernels: 53.7 us -> 34.4 us
  blocking collectives: 215 us -> 202 us
    pallas_call x14, Pallas kernels: 53.7 us -> 34.4 us  [placed(): return run(*near)]
    all_to_all x12, blocking collectives: 215 us -> 202 us  [swap(): return lax.all_to_all(msg, axes, 0, 0, tiled=True)]
where the time goes in v2:
time: 255 us; the launch traced here: 254 us
  blocking collectives  202 us (79%)
  Pallas kernels  34.4 us (13%)
  waiting for transfers between devices  10.3 us (4%)
  starting transfers between devices  4.89 us (2%)
    all_to_all x12, blocking collectives, swap(): return lax.all_to_all(msg, axes, 0, 0, tiled=True)  202 us
    pallas_call x14, Pallas kernels, placed(): return run(*near)  34.4 us
    all_to_all x1, waiting for transfers between devices, swap(): return lax.all_to_all(msg, axes, 0, 0, tiled=True)  10.3 us
  transfers between devices with their start and end apart: 1, of which 1 were waited for; matrix products, arithmetic and copies ran while one was open for 0% of the time, Pallas kernels for 0%

profile of v2, /device:TPU:1, one launch (start us, length us, event | category | flops | bytes accessed | tf_op | source)
XLA Modules:
  0.0 254.0 jit_solution(7064015634419800718)
XLA Ops:
  0.6 0.0 copy-start
  0.6 0.0 copy-start.7
  0.6 0.8 copy-done.7
  1.4 0.7 copy-done.8
  2.1 0.2 pack.1
  2.3 21.8 %all_to_all.65.got_ref = f32[16,24,128]{2,1,0:T(8,128)S(1)} all-to-all(f32[16,24,128]{2,1,0:T(8,128)S(1)} %pack.1), channel_id=1, replica_groups=mesh['row_0'=8,'row_1'=4,'col_0'=8,'col_1'=2] {'col_0','col_1'}, dimensions={0} | all-to-all | bytes 393216 | tf_op jit(solution)/shard_map/all_to_all | solution.py:35
  24.1 0.9 unpack.1
  25.0 26.5 %all_to_all.66.refs_2_ = bf16[32,64,128]{2,1,0:T(8,128)(2,1)S(1)} all-to-all(bf16[32,64,128]{2,1,0:T(8,128)(2,1)S(1)} %get-tuple-element.29), channel_id=1, replica_groups=mesh['row_0'=8,'row_1'=4,'col_0'=8,'col_1'=2] {'row_0','row_1'}, dimensions={0} | all-to-all | bytes 1048576 | tf_op jit(solution)/shard_map/all_to_all | solution.py:35
  51.5 0.0 copy-done
  51.5 2.7 %product_0.1 = f32[16,24,128]{2,1,0:T(8,128)S(1)} custom-call(s32[32]{0:T(128)} %bitcast.14, s32[32]{0:T(128)} %bitcast.19, bf16[32,64,128]{2,1,0:T(8,128)(2,1)S(1)} %all_to_all.66.refs_2_, bf16[32,128,128]{2,1,0:T(8,128)(2,1)S(1)} %bitcast.8, f32[4,64,128]{2,1,0:T(8,128)S(1)} %get-tuple-element.30.refs_4_.refs_2_, ...), custom_call_target="tpu_custom_call" | custom-call | tf_op jit(solution)/shard_map/product_0/pallas_call | solution.py:53
  54.1 14.3 %all_to_all.67.got_ref = f32[16,24,128]{2,1,0:T(8,128)S(1)} all-to-all(f32[16,24,128]{2,1,0:T(8,128)S(1)} %product_0.1), channel_id=1, replica_groups=mesh['row_0'=8,'row_1'=4,'col_0'=8,'col_1'=2] {'col_0','col_1'}, dimensions={0} | all-to-all | bytes 393216 | tf_op jit(solution)/shard_map/all_to_all | solution.py:35
  68.5 14.1 %all_to_all.68.got_ref = f32[32,8,128]{2,1,0:T(8,128)S(1)} all-to-all(f32[32,8,128]{2,1,0:T(8,128)S(1)} %get-tuple-element.32), channel_id=1, replica_groups=mesh['row_0'=8,'row_1'=4,'col_0'=8,'col_1'=2] {'row_0','row_1'}, dimensions={0} | all-to-all | bytes 262144 | tf_op jit(solution)/shard_map/all_to_all | solution.py:35
  82.7 14.3 %all_to_all.69.refs_1_ = f32[16,24,128]{2,1,0:T(8,128)S(1)} all-to-all(f32[16,24,128]{2,1,0:T(8,128)S(1)} %row_sum_0.1), channel_id=1, replica_groups=mesh['row_0'=8,'row_1'=4,'col_0'=8,'col_1'=2] {'col_0','col_1'}, dimensions={0} | all-to-all | bytes 393216 | tf_op jit(solution)/shard_map/all_to_all | solution.py:35
  96.9 7.4 %solve_0.1 = (f32[4,64,128]{2,1,0:T(8,128)S(1)}, f32[4,64,128]{2,1,0:T(8,128)S(1)}, f32[4,64,128]{2,1,0:T(8,128)S(1)}, f32[4,64,128]{2,1,0:T(8,128)S(1)}, f32[64...) custom-call(s32[32]{0:T(128)} %bitcast.15, ...), custom_call_target="tpu_custom_call" | custom-call | tf_op jit(solution)/shard_map/solve_0/pallas_call | solution.py:53
  104.4 20.3 %all_to_all.70.refs_2_ = bf16[32,64,128]{2,1,0:T(8,128)(2,1)S(1)} all-to-all(bf16[32,64,128]{2,1,0:T(8,128)(2,1)S(1)} %get-tuple-element.34), channel_id=1, replica_groups=mesh['row_0'=8,'row_1'=4,'col_0'=8,'col_1'=2] {'row_0','row_1'}, dimensions={0} | all-to-all | bytes 1048576 | tf_op jit(solution)/shard_map/all_to_all | solution.py:35
  124.6 0.0 copy-done.1
  124.6 0.0 copy-done.3
  124.6 0.0 copy-done.5
  124.7 2.4 product_1.1
  127.1 14.0 %all_to_all.71.got_ref = f32[16,24,128]{2,1,0:T(8,128)S(1)} all-to-all(f32[16,24,128]{2,1,0:T(8,128)S(1)} %product_1.1), channel_id=1, replica_groups=mesh['row_0'=8,'row_1'=4,'col_0'=8,'col_1'=2] {'col_0','col_1'}, dimensions={0} | all-to-all | bytes 393216 | tf_op jit(solution)/shard_map/all_to_all | solution.py:35
  141.1 14.2 %all_to_all.72.got_ref = f32[32,8,128]{2,1,0:T(8,128)S(1)} all-to-all(f32[32,8,128]{2,1,0:T(8,128)S(1)} %get-tuple-element.38), channel_id=1, replica_groups=mesh['row_0'=8,'row_1'=4,'col_0'=8,'col_1'=2] {'row_0','row_1'}, dimensions={0} | all-to-all | bytes 262144 | tf_op jit(solution)/shard_map/all_to_all | solution.py:35
  155.3 0.0 copy-start.4
  155.3 14.4 %all_to_all.73.refs_1_ = f32[16,24,128]{2,1,0:T(8,128)S(1)} all-to-all(f32[16,24,128]{2,1,0:T(8,128)S(1)} %row_sum_1.1), channel_id=1, replica_groups=mesh['row_0'=8,'row_1'=4,'col_0'=8,'col_1'=2] {'col_0','col_1'}, dimensions={0} | all-to-all | bytes 393216 | tf_op jit(solution)/shard_map/all_to_all | solution.py:35
  169.7 9.3 %solve_1.1 = (f32[4,64,128]{2,1,0:T(8,128)S(1)}, f32[4,64,128]{2,1,0:T(8,128)S(1)}, f32[4,64,128]{2,1,0:T(8,128)S(1)}, f32[4,64,128]{2,1,0:T(8,128)S(1)}, f32[64...) custom-call(s32[32]{0:T(128)} %bitcast.17, ...), custom_call_target="tpu_custom_call" | custom-call | tf_op jit(solution)/shard_map/solve_1/pallas_call | solution.py:53
  179.0 20.3 %all_to_all.74.refs_2_ = bf16[32,64,128]{2,1,0:T(8,128)(2,1)S(1)} all-to-all(bf16[32,64,128]{2,1,0:T(8,128)(2,1)S(1)} %get-tuple-element.44), channel_id=1, replica_groups=mesh['row_0'=8,'row_1'=4,'col_0'=8,'col_1'=2] {'row_0','row_1'}, dimensions={0} | all-to-all | bytes 1048576 | tf_op jit(solution)/shard_map/all_to_all | solution.py:35
  199.3 2.4 product_2.1
  201.7 14.0 %all_to_all.75.got_ref = f32[16,24,128]{2,1,0:T(8,128)S(1)} all-to-all(f32[16,24,128]{2,1,0:T(8,128)S(1)} %product_2.1), channel_id=1, replica_groups=mesh['row_0'=8,'row_1'=4,'col_0'=8,'col_1'=2] {'col_0','col_1'}, dimensions={0} | all-to-all | bytes 393216 | tf_op jit(solution)/shard_map/all_to_all | solution.py:35
  215.7 14.2 %all_to_all.76.got_ref = f32[32,8,128]{2,1,0:T(8,128)S(1)} all-to-all(f32[32,8,128]{2,1,0:T(8,128)S(1)} %get-tuple-element.48), channel_id=1, replica_groups=mesh['row_0'=8,'row_1'=4,'col_0'=8,'col_1'=2] {'row_0','row_1'}, dimensions={0} | all-to-all | bytes 262144 | tf_op jit(solution)/shard_map/all_to_all | solution.py:35
  229.9 0.7 row_sum_2.1
  230.6 4.9 %all-to-all-start.12 = ((f32[16,24,128]{2,1,0:T(8,128)}), f32[16,24,128]{2,1,0:T(8,128)S(1)}, u32[]{:S(2)}, u32[]{:S(2)}) async-start(f32[16,24,128]{2,1,0:T(8,128)} %row_sum_2.1), calls=%async_computation.12 | async-start | bytes 393216 | tf_op jit(solution)/shard_map/all_to_all | solution.py:35
  235.5 10.3 %all-to-all-done.12.refs_1_ = f32[16,24,128]{2,1,0:T(8,128)S(1)} async-done(((f32[16,24,128]{2,1,0:T(8,128)}), f32[16,24,128]{2,1,0:T(8,128)S(1)}, u32[]{:S(2)}, u32[]{:S(2)}) %all-to-all-start.12) | async-done | bytes 196640 | tf_op jit(solution)/shard_map/all_to_all | solution.py:35
  245.8 8.2 %solve_2.1 = (f32[32,64]{1,0:T(8,128)}, f32[32,64]{1,0:T(8,128)}) custom-call(s32[1]{0:T(128)} %bitcast.refs_0_, f32[16,24,128]{2,1,0:T(8,128)S(1)} %all-to-all-done.12.refs_1_, f32[4,64,128]{2,1,0:T(8,128)S(1)} %get-tuple-element.45.refs_4_.refs_2_, f32[4,8,128]{2,1,0:T(8,128)S(1)} %get-tuple-element.31.refs_5_.refs_3_, ...), custom_call_target="tpu_custom_call" | custom-call | tf_op jit(solution)/shard_map/solve_2/pallas_call | solution.py:53
  (14 shorter events, 0.2 us)
Async XLA Ops:
  0.6 50.8 %copy-start = (bf16[1,32,1,128,128]{4,3,2,1,0:T(8,128)(2,1)S(1)}, bf16[1,32,1,128,128]{4,3,2,1,0:T(8,128)(2,1)}, u32[]{:S(2)}) copy-start(bf16[1,32,1,128,128]{4,3,2,1,0:T(8,128)(2,1)} %param.8) | copy-start | bytes 3145732
  0.6 0.8 copy-start.7
  1.4 0.7 copy-start.8
  104.4 20.3 %copy-start.1 = (f32[64,64]{1,0:T(8,128)}, f32[64,64]{1,0:T(8,128)S(1)}, u32[]{:S(2)}) copy-start(f32[64,64]{1,0:T(8,128)S(1)} %get-tuple-element.41.refs_7_) | copy-start | bytes 49156
  104.4 20.3 %copy-start.3 = (f32[64,64]{1,0:T(8,128)}, f32[64,64]{1,0:T(8,128)S(1)}, u32[]{:S(2)}) copy-start(f32[64,64]{1,0:T(8,128)S(1)} %get-tuple-element.42.refs_8_) | copy-start | bytes 49156
  104.4 20.3 %copy-start.5 = (f32[64,64]{1,0:T(8,128)}, f32[64,64]{1,0:T(8,128)S(1)}, u32[]{:S(2)}) copy-start(f32[64,64]{1,0:T(8,128)S(1)} %get-tuple-element.43.refs_9_) | copy-start | bytes 49156
  155.3 14.4 %copy-start.2 = (f32[64,64]{1,0:T(8,128)S(1)}, f32[64,64]{1,0:T(8,128)}, u32[]{:S(2)}) copy-start(f32[64,64]{1,0:T(8,128)} %copy-done.1) | copy-start | bytes 49156
  155.3 14.4 %copy-start.4 = (f32[64,64]{1,0:T(8,128)S(1)}, f32[64,64]{1,0:T(8,128)}, u32[]{:S(2)}) copy-start(f32[64,64]{1,0:T(8,128)} %copy-done.3) | copy-start | bytes 49156
  155.3 14.4 %copy-start.6 = (f32[64,64]{1,0:T(8,128)S(1)}, f32[64,64]{1,0:T(8,128)}, u32[]{:S(2)}) copy-start(f32[64,64]{1,0:T(8,128)} %copy-done.5) | copy-start | bytes 49156
  230.6 15.2 %all-to-all-start.12 = ((f32[16,24,128]{2,1,0:T(8,128)}), f32[16,24,128]{2,1,0:T(8,128)S(1)}, u32[]{:S(2)}, u32[]{:S(2)}) async-start(f32[16,24,128]{2,1,0:T(8,128)} %row_sum_2.1), calls=%async_computation.12 | async-start | bytes 393216 | tf_op jit(solution)/shard_map/all_to_all | solution.py:35

commit v3 on v2

--- a/solution.py
+++ b/solution.py
@@ -35,7 +35,7 @@
     return lax.all_to_all(msg, axes, 0, 0, tiled=True)
 
 
-def call(kernel, in_specs, outs, scratch, name, make=pltpu.VMEM):
+def call(kernel, in_specs, outs, scratch, name, make=pltpu.VMEM, near=True):
     run = pl.pallas_call(
         kernel,
         in_specs=in_specs,
@@ -46,11 +46,12 @@
     )
 
     def placed(*args):
-        near = [
-            pltpu.with_memory_space_constraint(arg, pltpu.VMEM) if spec is VMEM else arg
-            for spec, arg in zip(in_specs, args, strict=True)
-        ]
-        return run(*near)
+        if near:
+            args = [
+                pltpu.with_memory_space_constraint(arg, pltpu.VMEM) if spec is VMEM else arg
+                for spec, arg in zip(in_specs, args, strict=True)
+            ]
+        return run(*args)
 
     return placed
 
@@ -140,35 +141,48 @@
         out_ref[k, 16:24, :] = total
 
 
-def factor(matrices):
+def solve_systems(systems, width):
     row_id = lax.broadcasted_iota(jnp.int32, (8, LANE), 0)
-    lane_id = lax.broadcasted_iota(jnp.int32, (SMP, SMP), 1)
-    eye = (lax.broadcasted_iota(jnp.int32, (SMP, SMP), 0) == lane_id).astype(F32)
     work = []
-    for matrix in matrices:
-        wide = jnp.concatenate([matrix, eye], axis=1)
+    for matrix, rhs in systems:
+        wide = jnp.concatenate([matrix, rhs], axis=1)
         work.append([wide[8 * t : 8 * t + 8, :] for t in range(8)])
-    for j in range(SMP):
+    for j in range(0, SMP, width):
         top, low = divmod(j, 8)
         for tiles in work:
-            pivot = tiles[top][low : low + 1, :]
-            scaled = pivot / pivot[:, j : j + 1]
-            for t in range(top, 8):
-                column = tiles[t][:, j : j + 1]
-                change = column * scaled
+            columns = [
+                [
+                    jnp.broadcast_to(tile[:, j + i : j + i + 1], (8, LANE))
+                    for i in range(width)
+                ]
+                for tile in tiles
+            ]
+            rows = [tiles[top][low + i : low + i + 1, :] for i in range(width)]
+            block = [
+                [columns[top][c][low + r : low + r + 1, :] for c in range(width)]
+                for r in range(width)
+            ]
+            recip, lower = [], {}
+            for a in range(width):
+                recip.append(1.0 / block[a][a])
+                for r in range(a + 1, width):
+                    lower[r, a] = block[r][a] * recip[a]
+                    rows[r] = rows[r] - lower[r, a] * rows[a]
+                    for c in range(a + 1, width):
+                        block[r][c] = block[r][c] - lower[r, a] * block[a][c]
+            for a in reversed(range(width)):
+                rows[a] = rows[a] * recip[a]
+                for r in range(a + 1, width):
+                    rows[a] = rows[a] - lower[r, a] * rows[r]
+            for t in range(8):
+                tile = tiles[t]
+                for i in range(width):
+                    tile = tile - columns[t][i] * rows[i]
                 if t == top:
-                    if low == 7:
-                        continue
-                    change = jnp.where(row_id > low, change, 0.0)
-                tiles[t] = tiles[t] - change
-    done = []
-    for tiles in work:
-        wide = jnp.concatenate(tiles, axis=0)
-        upper = wide[:, 0:SMP]
-        inverse = pltpu.roll(wide, SMP, 1)[:, 0:SMP]
-        diag = jnp.sum(upper * eye, axis=1, keepdims=True)
-        done.append((inverse, inverse / diag))
-    return done
+                    for i in range(width):
+                        tile = jnp.where(row_id == low + i, rows[i], tile)
+                tiles[t] = tile
+    return [pltpu.roll(jnp.concatenate(tiles, axis=0), SMP, 1)[:, 0:SMP] for tiles in work]
 
 
 def solve_kernel(first, last, *refs):
@@ -177,29 +191,32 @@
     got_ref, res_ref, reg_ref = refs[:3]
     refs = refs[3:]
     if not first:
-        dir_ref, img_ref, sol_ref, inv_ref, scaled_ref, curv_ref = refs[:6]
-        refs = refs[6:]
+        dir_ref, img_ref, sol_ref, inv_ref, curv_ref = refs[:5]
+        refs = refs[5:]
     if last:
         out_sol_ref, out_res_ref, keep_ref = refs
     else:
         new_res_ref, new_dir_ref, new_img_ref, new_sol_ref = refs[:4]
-        new_inv_ref, new_scaled_ref, new_curv_ref, sel_ref, half_ref = refs[4:]
+        new_inv_ref, new_curv_ref, sel_ref, half_ref = refs[4:]
     pair = jnp.concatenate([got_ref[k, 16:24, :] for k in range(8)], axis=0)
     gram = pltpu.roll(pair, SMP, 1)[:, 0:SMP]
     curv = pair[:, 0:SMP]
     if not first:
         mixed = jnp.concatenate([got_ref[k, 16:24, :] for k in range(8, 16)], axis=0)[:, 0:SMP]
-        beta_t = exact_dot(exact_dot(gram, inv_ref[...], NT), scaled_ref[...], NN)
+        beta_t = exact_dot(gram, inv_ref[...], NN)
         curv = curv + exact_dot(mixed + exact_dot(beta_t, curv_ref[...], NN), beta_t, NT)
     curv = 0.5 * (curv + curv.T)
     if last:
-        ((inv_c, scaled_c),) = factor([curv])
+        (alpha,) = solve_systems([(curv, gram)], 8)
     else:
-        (inv_c, scaled_c), (inv_g, scaled_g) = factor([curv, gram])
-        new_inv_ref[...] = inv_g
-        new_scaled_ref[...] = scaled_g
+        square = (SMP, SMP)
+        same = lax.broadcasted_iota(jnp.int32, square, 0) == lax.broadcasted_iota(
+            jnp.int32, square, 1
+        )
+        alpha, inverse = solve_systems([(curv, gram), (gram, same.astype(F32))], 4)
+        new_inv_ref[...] = inverse
         new_curv_ref[...] = curv
-    alpha_t = exact_dot(exact_dot(gram, inv_c, NT), scaled_c, NN)
+    alpha_t = alpha.T
     for b in range(BLKS):
         res = res_ref[b]
         coupled = jnp.concatenate([got_ref[4 * b + m, 0:16, :] for m in range(4)], axis=0)
@@ -241,9 +258,11 @@
     msg = ((COLS, 24, LANE), F32)
     half = pltpu.VMEM((BLKS, SMP, LANE), BF16)
 
-    (packed,) = call(pack_kernel, [VMEM] * 2, [msg], [], "pack")(
+    (packed,) = call(pack_kernel, [VMEM] * 2, [msg], [], "pack", near=False)(
         right_side.T, regular.reshape(1, PIECE)
     )
+    mine = lax.axis_index(COL).astype(jnp.int32).reshape(1)
+    packed, mine = lax.optimization_barrier((packed, mine))
     res, reg, out = call(
         unpack_kernel, [SMEM, VMEM], [field, ((BLKS, 8, LANE), F32), sel], [half], "unpack"
     )(rows, swap(packed, COL))
@@ -273,14 +292,13 @@
         specs = [SMEM] + [VMEM] * (3 + len(state))
         solve = functools.partial(solve_kernel, first, last)
         if last:
-            mine = lax.axis_index(COL).astype(jnp.int32).reshape(1)
             share = ((PIECE, SMP), F32)
             keep = pltpu.VMEM((2, BLKS, SMP, LANE), F32)
             shares = call(
                 solve, specs, [share, share], [keep], f"solve_{step}", jax.ShapeDtypeStruct
             )(mine, got, res, reg, *state)
             return tuple(part.T for part in shares)
-        outs = [field] * 4 + [small] * 3 + [sel]
+        outs = [field] * 4 + [small] * 2 + [sel]
         res, *state, out = call(solve, specs, outs, [half], f"solve_{step}")(
             rows, got, res, reg, *state
         )

time: 255 us -> 242 us (0.949)
  blocking collectives: 202 us -> 216 us
  waiting for transfers between devices: 10.3 us -> 0 us
  Pallas kernels: 34.4 us -> 24.5 us
  starting transfers between devices: 4.89 us -> 0 us
    all_to_all x12 -> x13, blocking collectives: 202 us -> 216 us  [swap(): return lax.all_to_all(msg, axes, 0, 0, tiled=True)]
    all_to_all x1 -> x0, waiting for transfers between devices: 10.3 us -> none  [swap(): return lax.all_to_all(msg, axes, 0, 0, tiled=True)]
    pallas_call x14, Pallas kernels: 34.4 us -> 24.5 us  [placed(): return run(*args)]
    all_to_all x1 -> x0, starting transfers between devices: 4.89 us -> none  [swap(): return lax.all_to_all(msg, axes, 0, 0, tiled=True)]
  transfers between devices with their start and end apart: 1 -> 0, of which waited for: 1 -> 0; matrix products, arithmetic and copies ran while one was open for 0% -> 0% of each run, Pallas kernels for 0% -> 0%
where the time goes in v3:
time: 242 us
  blocking collectives  216 us (89%)
  Pallas kernels  24.5 us (10%)
    all_to_all x13, blocking collectives, swap(): return lax.all_to_all(msg, axes, 0, 0, tiled=True)  216 us
    pallas_call x14, Pallas kernels, placed(): return run(*args)  24.5 us

profile of v3, /device:TPU:1, one launch (start us, length us, event | category | flops | bytes accessed | tf_op | source)
XLA Modules:
  0.0 241.5 jit_solution(16721065144844829526)
XLA Ops:
  0.6 0.0 copy-start
  0.6 1.0 pack.1
  1.6 21.8 %all_to_all.65.got_ref = f32[16,24,128]{2,1,0:T(8,128)S(1)} all-to-all(f32[16,24,128]{2,1,0:T(8,128)S(1)} %pack.1), channel_id=1, replica_groups=mesh['row_0'=8,'row_1'=4,'col_0'=8,'col_1'=2] {'col_0','col_1'}, dimensions={0} | all-to-all | bytes 393216 | tf_op jit(solution)/shard_map/all_to_all | solution.py:35
  23.4 0.9 unpack.1
  24.3 26.5 %all_to_all.66.refs_2_ = bf16[32,64,128]{2,1,0:T(8,128)(2,1)S(1)} all-to-all(bf16[32,64,128]{2,1,0:T(8,128)(2,1)S(1)} %get-tuple-element.31), channel_id=1, replica_groups=mesh['row_0'=8,'row_1'=4,'col_0'=8,'col_1'=2] {'row_0','row_1'}, dimensions={0} | all-to-all | bytes 1048576 | tf_op jit(solution)/shard_map/all_to_all | solution.py:35
  50.8 0.0 copy-done
  50.8 2.7 %product_0.1 = f32[16,24,128]{2,1,0:T(8,128)S(1)} custom-call(s32[32]{0:T(128)} %bitcast.12, s32[32]{0:T(128)} %bitcast.18, bf16[32,64,128]{2,1,0:T(8,128)(2,1)S(1)} %all_to_all.66.refs_2_, bf16[32,128,128]{2,1,0:T(8,128)(2,1)S(1)} %bitcast.8, f32[4,64,128]{2,1,0:T(8,128)S(1)} %get-tuple-element.32.refs_4_.refs_2_, ...), custom_call_target="tpu_custom_call" | custom-call | tf_op jit(solution)/shard_map/product_0/pallas_call | solution.py:54
  53.5 14.3 %all_to_all.67.got_ref = f32[16,24,128]{2,1,0:T(8,128)S(1)} all-to-all(f32[16,24,128]{2,1,0:T(8,128)S(1)} %product_0.1), channel_id=1, replica_groups=mesh['row_0'=8,'row_1'=4,'col_0'=8,'col_1'=2] {'col_0','col_1'}, dimensions={0} | all-to-all | bytes 393216 | tf_op jit(solution)/shard_map/all_to_all | solution.py:35
  67.8 14.1 %all_to_all.68.got_ref = f32[32,8,128]{2,1,0:T(8,128)S(1)} all-to-all(f32[32,8,128]{2,1,0:T(8,128)S(1)} %get-tuple-element.34), channel_id=1, replica_groups=mesh['row_0'=8,'row_1'=4,'col_0'=8,'col_1'=2] {'row_0','row_1'}, dimensions={0} | all-to-all | bytes 262144 | tf_op jit(solution)/shard_map/all_to_all | solution.py:35
  82.0 14.3 %all_to_all.69.refs_1_ = f32[16,24,128]{2,1,0:T(8,128)S(1)} all-to-all(f32[16,24,128]{2,1,0:T(8,128)S(1)} %row_sum_0.1), channel_id=1, replica_groups=mesh['row_0'=8,'row_1'=4,'col_0'=8,'col_1'=2] {'col_0','col_1'}, dimensions={0} | all-to-all | bytes 393216 | tf_op jit(solution)/shard_map/all_to_all | solution.py:35
  96.3 4.0 %solve_0.1 = (f32[4,64,128]{2,1,0:T(8,128)S(1)}, f32[4,64,128]{2,1,0:T(8,128)S(1)}, f32[4,64,128]{2,1,0:T(8,128)S(1)}, f32[4,64,128]{2,1,0:T(8,128)S(1)}, f32[64...) custom-call(s32[32]{0:T(128)} %bitcast.13, f32[16,24,128]{2,1,0:T(8,128)S(1)} %all_to_all.69.refs_1_, ...), custom_call_target="tpu_custom_call" | custom-call | tf_op jit(solution)/shard_map/solve_0/pallas_call | solution.py:54
  100.3 20.3 %all_to_all.70.refs_2_ = bf16[32,64,128]{2,1,0:T(8,128)(2,1)S(1)} all-to-all(bf16[32,64,128]{2,1,0:T(8,128)(2,1)S(1)} %get-tuple-element.36), channel_id=1, replica_groups=mesh['row_0'=8,'row_1'=4,'col_0'=8,'col_1'=2] {'row_0','row_1'}, dimensions={0} | all-to-all | bytes 1048576 | tf_op jit(solution)/shard_map/all_to_all | solution.py:35
  120.6 2.4 %product_1.1 = f32[16,24,128]{2,1,0:T(8,128)S(1)} custom-call(s32[32]{0:T(128)} %bitcast.14, s32[32]{0:T(128)} %bitcast.19, bf16[32,64,128]{2,1,0:T(8,128)(2,1)S(1)} %all_to_all.70.refs_2_, bf16[32,128,128]{2,1,0:T(8,128)(2,1)S(1)} %bitcast.9, f32[4,64,128]{2,1,0:T(8,128)S(1)} %get-tuple-element.37.refs_4_.refs_2_, ...), custom_call_target="tpu_custom_call" | custom-call | tf_op jit(solution)/shard_map/product_1/pallas_call | solution.py:54
  123.0 14.0 %all_to_all.71.got_ref = f32[16,24,128]{2,1,0:T(8,128)S(1)} all-to-all(f32[16,24,128]{2,1,0:T(8,128)S(1)} %product_1.1), channel_id=1, replica_groups=mesh['row_0'=8,'row_1'=4,'col_0'=8,'col_1'=2] {'col_0','col_1'}, dimensions={0} | all-to-all | bytes 393216 | tf_op jit(solution)/shard_map/all_to_all | solution.py:35
  137.0 14.2 %all_to_all.72.got_ref = f32[32,8,128]{2,1,0:T(8,128)S(1)} all-to-all(f32[32,8,128]{2,1,0:T(8,128)S(1)} %get-tuple-element.40), channel_id=1, replica_groups=mesh['row_0'=8,'row_1'=4,'col_0'=8,'col_1'=2] {'row_0','row_1'}, dimensions={0} | all-to-all | bytes 262144 | tf_op jit(solution)/shard_map/all_to_all | solution.py:35
  151.2 14.3 %all_to_all.73.refs_1_ = f32[16,24,128]{2,1,0:T(8,128)S(1)} all-to-all(f32[16,24,128]{2,1,0:T(8,128)S(1)} %row_sum_1.1), channel_id=1, replica_groups=mesh['row_0'=8,'row_1'=4,'col_0'=8,'col_1'=2] {'col_0','col_1'}, dimensions={0} | all-to-all | bytes 393216 | tf_op jit(solution)/shard_map/all_to_all | solution.py:35
  165.5 5.9 %solve_1.1 = (f32[4,64,128]{2,1,0:T(8,128)S(1)}, f32[4,64,128]{2,1,0:T(8,128)S(1)}, f32[4,64,128]{2,1,0:T(8,128)S(1)}, f32[4,64,128]{2,1,0:T(8,128)S(1)}, f32[64...) custom-call(s32[32]{0:T(128)} %bitcast.15, f32[16,24,128]{2,1,0:T(8,128)S(1)} %all_to_all.73.refs_1_, ...), custom_call_target="tpu_custom_call" | custom-call | tf_op jit(solution)/shard_map/solve_1/pallas_call | solution.py:54
  171.4 20.3 %all_to_all.74.refs_2_ = bf16[32,64,128]{2,1,0:T(8,128)(2,1)S(1)} all-to-all(bf16[32,64,128]{2,1,0:T(8,128)(2,1)S(1)} %get-tuple-element.45), channel_id=1, replica_groups=mesh['row_0'=8,'row_1'=4,'col_0'=8,'col_1'=2] {'row_0','row_1'}, dimensions={0} | all-to-all | bytes 1048576 | tf_op jit(solution)/shard_map/all_to_all | solution.py:35
  191.6 2.4 %product_2.1 = f32[16,24,128]{2,1,0:T(8,128)S(1)} custom-call(s32[32]{0:T(128)} %bitcast.16, s32[32]{0:T(128)} %bitcast.20, bf16[32,64,128]{2,1,0:T(8,128)(2,1)S(1)} %all_to_all.74.refs_2_, bf16[32,128,128]{2,1,0:T(8,128)(2,1)S(1)} %bitcast.10, f32[4,64,128]{2,1,0:T(8,128)S(1)} %get-tuple-element.46.refs_4_.refs_2_, ...), custom_call_target="tpu_custom_call" | custom-call | tf_op jit(solution)/shard_map/product_2/pallas_call | solution.py:54
  194.0 14.0 %all_to_all.75.got_ref = f32[16,24,128]{2,1,0:T(8,128)S(1)} all-to-all(f32[16,24,128]{2,1,0:T(8,128)S(1)} %product_2.1), channel_id=1, replica_groups=mesh['row_0'=8,'row_1'=4,'col_0'=8,'col_1'=2] {'col_0','col_1'}, dimensions={0} | all-to-all | bytes 393216 | tf_op jit(solution)/shard_map/all_to_all | solution.py:35
  208.1 14.2 %all_to_all.76.got_ref = f32[32,8,128]{2,1,0:T(8,128)S(1)} all-to-all(f32[32,8,128]{2,1,0:T(8,128)S(1)} %get-tuple-element.49), channel_id=1, replica_groups=mesh['row_0'=8,'row_1'=4,'col_0'=8,'col_1'=2] {'row_0','row_1'}, dimensions={0} | all-to-all | bytes 262144 | tf_op jit(solution)/shard_map/all_to_all | solution.py:35
  222.3 14.3 %all_to_all.77.refs_1_ = f32[16,24,128]{2,1,0:T(8,128)S(1)} all-to-all(f32[16,24,128]{2,1,0:T(8,128)S(1)} %row_sum_2.1), channel_id=1, replica_groups=mesh['row_0'=8,'row_1'=4,'col_0'=8,'col_1'=2] {'col_0','col_1'}, dimensions={0} | all-to-all | bytes 393216 | tf_op jit(solution)/shard_map/all_to_all | solution.py:35
  236.5 5.0 %solve_2.1 = (f32[32,64]{1,0:T(8,128)}, f32[32,64]{1,0:T(8,128)}) custom-call(s32[1]{0:T(128)} %bitcast.2.refs_0_, f32[16,24,128]{2,1,0:T(8,128)S(1)} %all_to_all.77.refs_1_, f32[4,64,128]{2,1,0:T(8,128)S(1)} %get-tuple-element.46.refs_4_.refs_2_, f32[4,8,128]{2,1,0:T(8,128)S(1)} %get-tuple-element.33.refs_5_.refs_3_, ...), custom_call_target="tpu_custom_call" | custom-call | tf_op jit(solution)/shard_map/solve_2/pallas_call | solution.py:54
  (6 shorter events, 0.2 us)
Async XLA Ops:
  0.6 50.2 %copy-start = (bf16[1,32,1,128,128]{4,3,2,1,0:T(8,128)(2,1)S(1)}, bf16[1,32,1,128,128]{4,3,2,1,0:T(8,128)(2,1)}, u32[]{:S(2)}) copy-start(bf16[1,32,1,128,128]{4,3,2,1,0:T(8,128)(2,1)} %param.8) | copy-start | bytes 3145732

commit v4 on v3

v4 whole, which is shorter than its diff:
```python
import functools

import jax
import jax.numpy as jnp
from jax import lax
from jax.experimental import pallas as pl
from jax.experimental.pallas import tpu as pltpu
from jax.sharding import Mesh
from jax.sharding import PartitionSpec as P

ITERS = 3
COL = ("col_0", "col_1")
ROW = ("row_0", "row_1")
ROW_COL = ROW + COL
F32 = jnp.float32
BF16 = jnp.bfloat16
SMP = 64
LANE = 128
BLKS = 4
COLS = 16
PIECE = 32
STRIP = 8
OWN = 2 * STRIP
NT = (((1,), (1,)), ((), ()))
NN = (((1,), (0,)), ((), ()))
VMEM = pl.BlockSpec(memory_space=pltpu.VMEM)
SMEM = pl.BlockSpec(memory_space=pltpu.SMEM)


def exact_dot(left, right, dims):
    return lax.dot_general(
        left, right, dims, precision=lax.Precision.HIGHEST, preferred_element_type=F32
    )


def swap(msg, axes):
    return lax.all_to_all(msg, axes, 0, 0, tiled=True)


def call(kernel, in_specs, outs, scratch, name, make=pltpu.VMEM, near=True):
    run = pl.pallas_call(
        kernel,
        in_specs=in_specs,
        out_specs=[VMEM] * len(outs),
        out_shape=[make(s, d) for s, d in outs],
        scratch_shapes=scratch,
        name=name,
    )

    def placed(*args):
        if near:
            args = [
                pltpu.with_memory_space_constraint(arg, pltpu.VMEM) if spec is VMEM else arg
                for spec, arg in zip(in_specs, args, strict=True)
            ]
        return run(*args)

    return placed


def thirds(value):
    high = value.astype(BF16).astype(F32)
    middle = (value - high).astype(BF16).astype(F32)
    return high, middle, value - high - middle


def pack_kernel(right_ref, reg_ref, rows_ref, cols_ref, counts_ref, curv_ref, out_ref):
    sources = curv_ref.shape[0]
    base = STRIP * sources
    for s in range(sources):
        flipped = curv_ref[s].astype(F32).T
        for k in range(COLS):
            strip = flipped[STRIP * k : STRIP * k + STRIP, :].astype(BF16)
            out_ref[k, STRIP * s : STRIP * s + STRIP, :] = strip
    right = right_ref[...].T
    packed = jnp.concatenate([right[16 * j : 16 * j + 16, :] for j in range(4)], axis=1)
    cols = cols_ref[...]
    place = ((cols // 2) * BLKS + rows_ref[...]) * 2 + cols % 2
    place = jnp.where(counts_ref[...] > 0, place, -1).astype(F32)
    lines = [*thirds(reg_ref[...]), place]
    lines.append(jnp.zeros((16 - len(lines), PIECE), F32))
    notes = jnp.concatenate(lines, axis=0)
    notes = jnp.concatenate([notes, jnp.zeros((16, LANE - PIECE), F32)], axis=1)
    tiles = [tile.astype(BF16) for tile in (*thirds(packed), notes)]
    for k in range(COLS):
        for i, tile in enumerate(tiles):
            out_ref[k, base + 16 * i : base + 16 * i + 16, :] = tile


def pixel_rows(fields):
    return [jnp.concatenate([fields[b].T, fields[2 + b].T], axis=1) for b in range(2)]


def unpack_kernel(place_ref, got_ref, res_ref, reg_ref, own_ref, own_reg_ref, out_ref, tall_ref):
    base = got_ref.shape[1] - 4 * 16
    packed, notes = [], []
    for k in range(COLS):
        parts = [got_ref[k, base + 16 * i : base + 16 * i + 16, :].astype(F32) for i in range(4)]
        packed.append(parts[0] + parts[1] + parts[2])
        note = parts[3]
        notes.append(note[0:1] + note[1:2] + note[2:3])
    group = lax.broadcasted_iota(jnp.int32, (16, LANE), 1) // PIECE
    fields, regs = [], []
    for b in range(BLKS):
        pieces = []
        for j in range(4):
            piece = jnp.zeros((16, LANE), F32)
            for m in range(4):
                shift = (PIECE * (m - j)) % LANE
                part = packed[4 * b + m]
                part = pltpu.roll(part, shift, 1) if shift else part
                piece = jnp.where(group == m, part, piece)
            pieces.append(piece)
        fields.append(jnp.concatenate(pieces, axis=0))
        reg = jnp.zeros((8, LANE), F32)
        for m in range(4):
            part = jnp.broadcast_to(notes[4 * b + m], (8, LANE))
            part = pltpu.roll(part, PIECE * m, 1) if m else part
            reg = jnp.where(group[0:8] == m, part, reg)
        regs.append(jnp.broadcast_to(reg[0:1], (SMP, LANE)))
        res_ref[b] = fields[b]
        reg_ref[b] = reg
    start = pl.multiple_of(place_ref[0] * STRIP, STRIP)
    for target, values in ((own_ref, fields), (own_reg_ref, regs)):
        for b, tall in enumerate(pixel_rows(values)):
            tall_ref[b] = tall
            target[STRIP * b : STRIP * b + STRIP, :] = tall_ref[b, pl.ds(start, STRIP), :]
    own = own_ref[...]
    for r in range(out_ref.shape[0]):
        out_ref[r] = own


def dense_kernel(place_ref, got_ref, high_ref, low_ref, sum_ref):
    sources = place_ref.shape[1]
    sum_ref[...] = jnp.zeros_like(sum_ref)
    for s in range(sources):
        for k in range(COLS):
            place = place_ref[k, s]
            strip = got_ref[k, STRIP * s : STRIP * s + STRIP, :].astype(F32)
            strip = jnp.where(place >= 0, strip, 0.0)
            spot = jnp.maximum(place, 0)
            plane = spot // 2
            rows = pl.ds(pl.multiple_of(OWN * s + STRIP * (spot % 2), STRIP), STRIP)
            sum_ref[plane, rows, :] = sum_ref[plane, rows, :] + strip
    for plane in range(2 * BLKS):
        total = sum_ref[plane]
        high = total.astype(BF16)
        high_ref[plane] = high
        low_ref[plane] = (total - high.astype(F32)).astype(BF16)


def product_kernel(first, *refs):
    spread_ref, high_ref, low_ref, res_ref, reg_ref = refs[:5]
    if first:
        (out_ref,) = refs[5:]
    else:
        img_ref, dir_ref, out_ref = refs[5:]
    pixels = OWN * spread_ref.shape[0]
    spread = spread_ref[...].reshape(pixels, LANE)
    inputs = jnp.concatenate(
        [spread[LANE * i : LANE * i + LANE, :].T for i in range(pixels // LANE)], axis=1
    ).astype(BF16)
    share = 1.0 / COLS
    pair = jnp.zeros((SMP, LANE), F32)
    mixed = jnp.zeros((SMP, SMP), F32)
    coupled = []
    for b in range(BLKS):
        acc = jnp.zeros((SMP, LANE), F32)
        for half in range(2):
            left = inputs[SMP * half : SMP * half + SMP, :]
            for weights in (high_ref, low_ref):
                acc += lax.dot_general(
                    left, weights[BLKS * half + b], NN, preferred_element_type=F32
                )
        coupled.append(acc)
        res = res_ref[b]
        part = acc + reg_ref[b, 0:1, :] * res * share
        pair += exact_dot(res, jnp.concatenate([part, res * share], axis=0), NT)
        if not first:
            mixed += exact_dot(res, img_ref[b] * share, NT) + exact_dot(part, dir_ref[b], NT)
    other = jnp.concatenate([mixed, jnp.zeros((SMP, LANE - SMP), F32)], axis=1)
    tall = pixel_rows(coupled)
    for k in range(COLS):
        for b in range(2):
            out_ref[k, STRIP * b : STRIP * b + STRIP, :] = tall[b][STRIP * k : STRIP * k + STRIP]
        source = pair if k < 8 else other
        n = k % 8
        out_ref[k, OWN : OWN + 8, :] = source[8 * n : 8 * n + 8, :]


def col_sum_kernel(last, got_ref, own_ref, own_reg_ref, out_ref, piece_ref):
    total = got_ref[0]
    for k in range(1, COLS):
        total = total + got_ref[k]
    coupled = total[0:OWN, :]
    piece_ref[...] = coupled
    gram = total[OWN : OWN + 8, :]
    full = coupled + own_reg_ref[...] * own_ref[...]
    for r in range(out_ref.shape[0]):
        if last:
            out_ref[r] = gram
        else:
            out_ref[r, 0:OWN, :] = full
            out_ref[r, OWN : OWN + 8, :] = gram


def row_sum_kernel(got_ref, piece_ref, out_ref):
    top = got_ref.shape[1] - 8
    total = got_ref[0, top:, :]
    for r in range(1, got_ref.shape[0]):
        total = total + got_ref[r, top:, :]
    piece = piece_ref[...]
    for k in range(COLS):
        out_ref[k, 0:OWN, :] = piece
        out_ref[k, OWN : OWN + 8, :] = total


def solve_systems(systems, width):
    row_id = lax.broadcasted_iota(jnp.int32, (8, LANE), 0)
    work = []
    for matrix, rhs in systems:
        wide = jnp.concatenate([matrix, rhs], axis=1)
        work.append([wide[8 * t : 8 * t + 8, :] for t in range(8)])
    for j in range(0, SMP, width):
        top, low = divmod(j, 8)
        for tiles in work:
            columns = [
                [
                    jnp.broadcast_to(tile[:, j + i : j + i + 1], (8, LANE))
                    for i in range(width)
                ]
                for tile in tiles
            ]
            rows = [tiles[top][low + i : low + i + 1, :] for i in range(width)]
            block = [
                [columns[top][c][low + r : low + r + 1, :] for c in range(width)]
                for r in range(width)
            ]
            recip, lower = [], {}
            for a in range(width):
                recip.append(1.0 / block[a][a])
                for r in range(a + 1, width):
                    lower[r, a] = block[r][a] * recip[a]
                    rows[r] = rows[r] - lower[r, a] * rows[a]
                    for c in range(a + 1, width):
                        block[r][c] = block[r][c] - lower[r, a] * block[a][c]
            for a in reversed(range(width)):
                rows[a] = rows[a] * recip[a]
                for r in range(a + 1, width):
                    rows[a] = rows[a] - lower[r, a] * rows[r]
            for t in range(8):
                tile = tiles[t]
                for i in range(width):
                    tile = tile - columns[t][i] * rows[i]
                if t == top:
                    for i in range(width):
                        tile = jnp.where(row_id == low + i, rows[i], tile)
                tiles[t] = tile
    return [pltpu.roll(jnp.concatenate(tiles, axis=0), SMP, 1)[:, 0:SMP] for tiles in work]


def both_halves(matrix):
    zero = jnp.zeros((SMP, SMP), F32)
    upper = jnp.concatenate([matrix, zero], axis=1)
    lower = jnp.concatenate([zero, matrix], axis=1)
    return jnp.concatenate([upper, lower], axis=0)


def solve_kernel(first, last, *refs):
    refs = list(refs)
    place_ref, got_ref, res_ref, reg_ref = refs[:4]
    refs = refs[4:]
    if not first:
        dir_ref, img_ref, sol_ref, inv_ref, curv_ref = refs[:5]
        refs = refs[5:]
    if last:
        out_sol_ref, out_res_ref, keep_ref = refs
    else:
        spread_ref, fresh_ref = refs[:2]
        refs = refs[2:]
        if not first:
            spread_img_ref = refs.pop(0)
        new_res_ref, new_dir_ref, new_img_ref, new_sol_ref = refs[:4]
        new_inv_ref, new_curv_ref, new_spread_ref, new_spread_img_ref, own_ref = refs[4:]
    pair = jnp.concatenate([got_ref[k, OWN : OWN + 8, :] for k in range(8)], axis=0)
    gram = pltpu.roll(pair, SMP, 1)[:, 0:SMP]
    curv = pair[:, 0:SMP]
    if not first:
        mixed = jnp.concatenate([got_ref[k, OWN : OWN + 8, :] for k in range(8, 16)], axis=0)
        mixed = mixed[:, 0:SMP]
        beta_t = exact_dot(gram, inv_ref[...], NN)
        curv = curv + exact_dot(mixed + exact_dot(beta_t, curv_ref[...], NN), beta_t, NT)
    curv = 0.5 * (curv + curv.T)
    if last:
        (alpha,) = solve_systems([(curv, gram)], 8)
    else:
        square = (SMP, SMP)
        same = lax.broadcasted_iota(jnp.int32, square, 0) == lax.broadcasted_iota(
            jnp.int32, square, 1
        )
        alpha, inverse = solve_systems([(curv, gram), (gram, same.astype(F32))], 4)
        new_inv_ref[...] = inverse
        new_curv_ref[...] = curv
        sources = spread_ref.shape[0]
        pixels = OWN * sources
        spread_img = fresh_ref[:, 0:OWN, :].reshape(pixels, LANE)
        if not first:
            old = spread_img_ref[...].reshape(pixels, LANE)
            spread_img = spread_img + exact_dot(old, both_halves(beta_t.T), NN)
        spread = spread_ref[...].reshape(pixels, LANE)
        spread = spread - exact_dot(spread_img, both_halves(alpha), NN)
        new_spread_ref[...] = spread.reshape(sources, OWN, LANE)
        new_spread_img_ref[...] = spread_img.reshape(sources, OWN, LANE)
        own_ref[...] = new_spread_ref[place_ref[1]]
    alpha_t = alpha.T
    wide = [
        jnp.concatenate(
            [got_ref[k, STRIP * b : STRIP * b + STRIP, :] for k in range(COLS)], axis=0
        ).T
        for b in range(2)
    ]
    for b in range(BLKS):
        res = res_ref[b]
        half = SMP * (b // 2)
        image = wide[b % 2][half : half + SMP, :] + reg_ref[b, 0:1, :] * res
        direction = res
        if not first:
            image = image + exact_dot(beta_t, img_ref[b], NN)
            direction = direction + exact_dot(beta_t, dir_ref[b], NN)
        new_res = res - exact_dot(alpha_t, image, NN)
        new_sol = exact_dot(alpha_t, direction, NN)
        if not first:
            new_sol = sol_ref[b] + new_sol
        if last:
            keep_ref[0, b] = new_sol
            keep_ref[1, b] = new_res
        else:
            new_res_ref[b] = new_res
            new_dir_ref[b] = direction
            new_img_ref[b] = image
            new_sol_ref[b] = new_sol
    if last:
        mine = place_ref[0]
        shift = (LANE - PIECE * (mine % 4)) % LANE
        out_sol_ref[...] = pltpu.roll(keep_ref[0, mine // 4], shift, 1)[:, 0:PIECE].T
        out_res_ref[...] = pltpu.roll(keep_ref[1, mine // 4], shift, 1)[:, 0:PIECE].T


def body(right_side, regular, curvature, block_rows, block_cols, block_counts):
    sources = block_rows.shape[1]
    pixels = OWN * sources
    curv = curvature.reshape(sources, LANE, LANE)
    tables = [table.reshape(1, sources) for table in (block_rows, block_cols, block_counts)]
    field = ((BLKS, SMP, LANE), F32)
    small = ((SMP, SMP), F32)
    own_share = ((OWN, LANE), F32)
    spread_share = ((sources, OWN, LANE), F32)
    msg = ((COLS, OWN + 8, LANE), F32)
    start = ((COLS, STRIP * sources + 64, LANE), BF16)
    dense = ((2 * BLKS, pixels, LANE), BF16)

    (packed,) = call(pack_kernel, [VMEM] * 6, [start], [], "pack", near=False)(
        right_side.T, regular.reshape(1, PIECE), *tables, curv
    )
    here = jnp.stack([lax.axis_index(COL), lax.axis_index(ROW)]).astype(jnp.int32)
    packed, here = lax.optimization_barrier((packed, here))
    packed = swap(packed, COL)
    res, reg, own, own_reg, out = call(
        unpack_kernel,
        [SMEM, VMEM],
        [field, ((BLKS, 8, LANE), F32), own_share, own_share, spread_share],
        [pltpu.VMEM((2, LANE, LANE), F32)],
        "unpack",
    )(here, packed)
    spread = swap(out, ROW)
    places = packed[:, STRIP * sources + 51, 0:sources].astype(jnp.int32)
    high, low = call(
        dense_kernel,
        [SMEM, VMEM],
        [dense, dense],
        [pltpu.VMEM(dense[0], F32)],
        "dense",
    )(places, packed)
    state, spread_img = [], []
    for step in range(ITERS):
        first, last = step == 0, step == ITERS - 1
        before = [] if first else [state[1], state[0]]
        (part,) = call(
            functools.partial(product_kernel, first),
            [VMEM] * (5 + len(before)),
            [msg],
            [],
            f"product_{step}",
        )(spread, high, low, res, reg, *before)
        out, piece = call(
            functools.partial(col_sum_kernel, last),
            [VMEM] * 3,
            [((sources, 8 if last else OWN + 8, LANE), F32), own_share],
            [],
            f"col_sum_{step}",
        )(swap(part, COL), own, own_reg)
        fresh = swap(out, ROW)
        (whole,) = call(row_sum_kernel, [VMEM] * 2, [msg], [], f"row_sum_{step}")(fresh, piece)
        got = swap(whole, COL)
        solve = functools.partial(solve_kernel, first, last)
        if last:
            share = ((PIECE, SMP), F32)
            keep = pltpu.VMEM((2, BLKS, SMP, LANE), F32)
            shares = call(
                solve,
                [SMEM] + [VMEM] * (3 + len(state)),
                [share, share],
                [keep],
                f"solve_{step}",
                jax.ShapeDtypeStruct,
            )(here, got, res, reg, *state)
            return tuple(part.T for part in shares)
        inputs = [got, res, reg, *state, spread, fresh, *spread_img]
        outs = [field] * 4 + [small] * 2 + [spread_share] * 2 + [own_share]
        res, *state, spread, img, own = call(
            solve, [SMEM] + [VMEM] * len(inputs), outs, [], f"solve_{step}"
        )(here, *inputs)
        spread_img = [img]


def solution(mesh):
    finer = Mesh(mesh.devices.reshape(8, 4, 8, 2), ROW_COL)
    placed = (
        P(None, ROW_COL),
        P(ROW_COL),
        P(ROW, None, COL, None, None),
        P(ROW, None, COL),
        P(ROW, None, COL),
        P(ROW, None, COL),
    )
    return jax.shard_map(
        body,
        mesh=finer,
        in_specs=placed,
        out_specs=(P(None, ROW_COL), P(None, ROW_COL)),
        check_vma=False,
    )
```

time: 242 us -> 249 us (1.029)
  blocking collectives: 216 us -> 179 us
  local copies, waits for them, and re-layouts: 0.01 us -> 20.6 us
  starting transfers between devices: 0 us -> 9.8 us
  Pallas kernels: 24.5 us -> 30.4 us
  waiting for transfers between devices: 0 us -> 5.89 us
    all_to_all x13 -> x10, blocking collectives: 216 us -> 179 us  [swap(): return lax.all_to_all(msg, axes, 0, 0, tiled=True)]
    unnamed x2 -> x74, local copies, waits for them, and re-layouts: 0.01 us -> 20.6 us
    all_to_all x0 -> x1, starting transfers between devices: none -> 9.8 us  [swap(): return lax.all_to_all(msg, axes, 0, 0, tiled=True)]
    pallas_call x14 -> x15, Pallas kernels: 24.5 us -> 30.4 us  [placed(): return run(*args)]
    all_to_all x0 -> x1, waiting for transfers between devices: none -> 5.89 us  [swap(): return lax.all_to_all(msg, axes, 0, 0, tiled=True)]
  transfers between devices with their start and end apart: 0 -> 1, of which waited for: 0 -> 1; matrix products, arithmetic and copies ran while one was open for 0% -> 0% of each run, Pallas kernels for 0% -> 2%
where the time goes in v4:
time: 249 us; the launch traced here: 248 us
  blocking collectives  179 us (72%)
  Pallas kernels  30.4 us (12%)
  local copies, waits for them, and re-layouts  20.6 us (8%)
  starting transfers between devices  9.8 us (4%)
  waiting for transfers between devices  5.89 us (2%)
    all_to_all x10, blocking collectives, swap(): return lax.all_to_all(msg, axes, 0, 0, tiled=True)  179 us
    pallas_call x15, Pallas kernels, placed(): return run(*args)  30.4 us
    unnamed x74, local copies, waits for them, and re-layouts  20.6 us
    all_to_all x1, starting transfers between devices, swap(): return lax.all_to_all(msg, axes, 0, 0, tiled=True)  9.8 us
    all_to_all x1, waiting for transfers between devices, swap(): return lax.all_to_all(msg, axes, 0, 0, tiled=True)  5.89 us
  transfers between devices with their start and end apart: 1, of which 1 were waited for; matrix products, arithmetic and copies ran while one was open for 0% of the time, Pallas kernels for 2%

profile of v4, /device:TPU:1, one launch (start us, length us, event | category | flops | bytes accessed | tf_op | source)
XLA Modules:
  0.0 248.0 jit_solution(10174294632038069297)
XLA Ops:
  1.2 1.7 pack.1
  2.9 45.7 %all_to_all.55.got_ref = bf16[16,320,128]{2,1,0:T(8,128)(2,1)S(1)} all-to-all(bf16[16,320,128]{2,1,0:T(8,128)(2,1)S(1)} %pack.1), channel_id=1, replica_groups=mesh['row_0'=8,'row_1'=4,'col_0'=8,'col_1'=2] {'col_0','col_1'}, dimensions={0} | all-to-all | bytes 2621440 | tf_op jit(solution)/shard_map/all_to_all | solution.py:37
  48.6 1.8 unpack.1
  50.4 9.8 %all-to-all-start.1 = ((f32[32,16,128]{2,1,0:T(8,128)}), f32[32,16,128]{2,1,0:T(8,128)}, u32[]{:S(2)}, u32[]{:S(2)}) async-start(f32[32,16,128]{2,1,0:T(8,128)} %get-tuple-element.38), calls=%async_computation.1 | async-start | bytes 524288 | tf_op jit(solution)/shard_map/all_to_all | solution.py:37
  60.8 3.9 %dense.1 = (bf16[8,512,128]{2,1,0:T(8,128)(2,1)S(1)}, bf16[8,512,128]{2,1,0:T(8,128)(2,1)S(1)}) custom-call(s32[16,32]{1,0:T(8,128)} %bitcast.12, bf16[16,320,128]{2,1,0:T(8,128)(2,1)S(1)} %all_to_all.55.got_ref), custom_call_target="tpu_custom_call" | custom-call | tf_op jit(solution)/shard_map/dense/pallas_call | solution.py:56
  64.7 1.0 copy-done
  65.7 1.0 copy-done.4
  66.7 5.9 %all-to-all-done.1.refs_0_.refs_4_ = f32[32,16,128]{2,1,0:T(8,128)} async-done(((f32[32,16,128]{2,1,0:T(8,128)}), f32[32,16,128]{2,1,0:T(8,128)}, u32[]{:S(2)}, u32[]{:S(2)}) %all-to-all-start.1) | async-done | bytes 262176 | tf_op jit(solution)/shard_map/all_to_all | solution.py:37
  72.6 1.2 copy-done.1
  73.8 1.2 copy-done.5
  75.1 0.9 copy-done.21
  76.0 2.3 product_0.1
  78.3 14.2 %all_to_all.56.got_ref = f32[16,24,128]{2,1,0:T(8,128)S(1)} all-to-all(f32[16,24,128]{2,1,0:T(8,128)S(1)} %product_0.1), channel_id=1, replica_groups=mesh['row_0'=8,'row_1'=4,'col_0'=8,'col_1'=2] {'col_0','col_1'}, dimensions={0} | all-to-all | bytes 393216 | tf_op jit(solution)/shard_map/all_to_all | solution.py:37
  92.5 18.1 %all_to_all.57.got_ref.refs_5_ = f32[32,24,128]{2,1,0:T(8,128)S(1)} all-to-all(f32[32,24,128]{2,1,0:T(8,128)S(1)} %get-tuple-element.45), channel_id=1, replica_groups=mesh['row_0'=8,'row_1'=4,'col_0'=8,'col_1'=2] {'row_0','row_1'}, dimensions={0} | all-to-all | bytes 786432 | tf_op jit(solution)/shard_map/all_to_all | solution.py:37
  110.7 14.1 %all_to_all.58.refs_1_ = f32[16,24,128]{2,1,0:T(8,128)S(1)} all-to-all(f32[16,24,128]{2,1,0:T(8,128)S(1)} %row_sum_0.1), channel_id=1, replica_groups=mesh['row_0'=8,'row_1'=4,'col_0'=8,'col_1'=2] {'col_0','col_1'}, dimensions={0} | all-to-all | bytes 393216 | tf_op jit(solution)/shard_map/all_to_all | solution.py:37
  124.8 4.8 %solve_0.1 = (f32[4,64,128]{2,1,0:T(8,128)S(1)}, f32[4,64,128]{2,1,0:T(8,128)S(1)}, f32[4,64,128]{2,1,0:T(8,128)S(1)}, f32[4,64,128]{2,1,0:T(8,128)S(1)}, f32[64...) custom-call(s32[2]{0:T(128)} %pad_add_fusion.place_ref.refs_0_, ...), custom_call_target="tpu_custom_call" | custom-call | tf_op jit(solution)/shard_map/solve_0/pallas_call | solution.py:56
  132.2 1.4 copy-done.2
  133.5 1.2 copy-done.6
  134.7 1.7 product_1.1
  136.5 13.1 %all_to_all.59.got_ref = f32[16,24,128]{2,1,0:T(8,128)S(1)} all-to-all(f32[16,24,128]{2,1,0:T(8,128)S(1)} %product_1.1), channel_id=1, replica_groups=mesh['row_0'=8,'row_1'=4,'col_0'=8,'col_1'=2] {'col_0','col_1'}, dimensions={0} | all-to-all | bytes 393216 | tf_op jit(solution)/shard_map/all_to_all | solution.py:37
  149.6 18.7 %all_to_all.60.got_ref.refs_10_ = f32[32,24,128]{2,1,0:T(8,128)S(1)} all-to-all(f32[32,24,128]{2,1,0:T(8,128)S(1)} %get-tuple-element.52), channel_id=1, replica_groups=mesh['row_0'=8,'row_1'=4,'col_0'=8,'col_1'=2] {'row_0','row_1'}, dimensions={0} | all-to-all | bytes 786432 | tf_op jit(solution)/shard_map/all_to_all | solution.py:37
  168.3 14.5 %all_to_all.61.refs_1_ = f32[16,24,128]{2,1,0:T(8,128)S(1)} all-to-all(f32[16,24,128]{2,1,0:T(8,128)S(1)} %row_sum_1.1), channel_id=1, replica_groups=mesh['row_0'=8,'row_1'=4,'col_0'=8,'col_1'=2] {'col_0','col_1'}, dimensions={0} | all-to-all | bytes 393216 | tf_op jit(solution)/shard_map/all_to_all | solution.py:37
  182.8 6.8 %solve_1.1 = (f32[4,64,128]{2,1,0:T(8,128)S(1)}, f32[4,64,128]{2,1,0:T(8,128)S(1)}, f32[4,64,128]{2,1,0:T(8,128)S(1)}, f32[4,64,128]{2,1,0:T(8,128)S(1)}, f32[64...) custom-call(s32[2]{0:T(128)} %pad_add_fusion.place_ref.refs_0_, ...), custom_call_target="tpu_custom_call" | custom-call | tf_op jit(solution)/shard_map/solve_1/pallas_call | solution.py:56
  193.6 1.2 copy-done.3
  194.8 1.2 copy-done.7
  196.0 0.9 copy-done.15
  198.7 0.9 copy-done.26
  199.7 1.6 product_2.1
  201.3 13.0 %all_to_all.62.got_ref = f32[16,24,128]{2,1,0:T(8,128)S(1)} all-to-all(f32[16,24,128]{2,1,0:T(8,128)S(1)} %product_2.1), channel_id=1, replica_groups=mesh['row_0'=8,'row_1'=4,'col_0'=8,'col_1'=2] {'col_0','col_1'}, dimensions={0} | all-to-all | bytes 393216 | tf_op jit(solution)/shard_map/all_to_all | solution.py:37
  214.4 13.7 %all_to_all.63.got_ref = f32[32,8,128]{2,1,0:T(8,128)S(1)} all-to-all(f32[32,8,128]{2,1,0:T(8,128)S(1)} %get-tuple-element.63), channel_id=1, replica_groups=mesh['row_0'=8,'row_1'=4,'col_0'=8,'col_1'=2] {'row_0','row_1'}, dimensions={0} | all-to-all | bytes 262144 | tf_op jit(solution)/shard_map/all_to_all | solution.py:37
  228.1 14.2 %all_to_all.64.refs_1_ = f32[16,24,128]{2,1,0:T(8,128)S(1)} all-to-all(f32[16,24,128]{2,1,0:T(8,128)S(1)} %row_sum_2.1), channel_id=1, replica_groups=mesh['row_0'=8,'row_1'=4,'col_0'=8,'col_1'=2] {'col_0','col_1'}, dimensions={0} | all-to-all | bytes 393216 | tf_op jit(solution)/shard_map/all_to_all | solution.py:37
  242.3 5.7 %solve_2.1 = (f32[32,64]{1,0:T(8,128)}, f32[32,64]{1,0:T(8,128)}) custom-call(s32[2]{0:T(128)} %pad_add_fusion.place_ref.refs_0_, f32[16,24,128]{2,1,0:T(8,128)S(1)} %all_to_all.64.refs_1_, f32[4,64,128]{2,1,0:T(8,128)S(1)} %copy-done.15, f32[4,8,128]{2,1,0:T(8,128)S(1)} %get-tuple-element.42.refs_4_.refs_3_, f32[4,64,128]{2,1,0:T(8,128)S(1)} %copy-done.17, ...), custom_call_target="tpu_custom_call" | custom-call | tf_op jit(solution)/shard_map/solve_2/pallas_call | solution.py:56
  (71 shorter events, 9.8 us)
Async XLA Ops:
  50.4 10.4 %copy-start.20 = (f32[4,64,128]{2,1,0:T(8,128)}, f32[4,64,128]{2,1,0:T(8,128)S(1)}, u32[]{:S(2)}) copy-start(f32[4,64,128]{2,1,0:T(8,128)S(1)} %get-tuple-element.41.refs_3_.refs_2_) | copy-start | bytes 393220
  50.4 22.2 %all-to-all-start.1 = ((f32[32,16,128]{2,1,0:T(8,128)}), f32[32,16,128]{2,1,0:T(8,128)}, u32[]{:S(2)}, u32[]{:S(2)}) async-start(f32[32,16,128]{2,1,0:T(8,128)} %get-tuple-element.38), calls=%async_computation.1 | async-start | bytes 524288 | tf_op jit(solution)/shard_map/all_to_all | solution.py:37
  64.7 1.0 copy-start
  65.7 1.0 copy-start.4
  72.6 1.2 copy-start.1
  73.8 1.2 copy-start.5
  75.1 0.9 copy-start.21
  78.3 46.5 %copy-start.22 = (f32[4,64,128]{2,1,0:T(8,128)S(1)}, f32[4,64,128]{2,1,0:T(8,128)}, u32[]{:S(2)}) copy-start(f32[4,64,128]{2,1,0:T(8,128)} %copy-done.20) | copy-start | bytes 393220
  129.6 0.7 copy-start.23
  132.1 4.3 %copy-start.8 = (f32[4,64,128]{2,1,0:T(8,128)}, f32[4,64,128]{2,1,0:T(8,128)S(1)}, u32[]{:S(2)}) copy-start(f32[4,64,128]{2,1,0:T(8,128)S(1)} %get-tuple-element.48.refs_3_.refs_2_) | copy-start | bytes 393220
  132.1 4.3 %copy-start.10 = (f32[4,64,128]{2,1,0:T(8,128)}, f32[4,64,128]{2,1,0:T(8,128)S(1)}, u32[]{:S(2)}) copy-start(f32[4,64,128]{2,1,0:T(8,128)S(1)} %get-tuple-element.50.refs_6_.refs_4_) | copy-start | bytes 393220
  132.1 4.3 %copy-start.12 = (f32[4,64,128]{2,1,0:T(8,128)}, f32[4,64,128]{2,1,0:T(8,128)S(1)}, u32[]{:S(2)}) copy-start(f32[4,64,128]{2,1,0:T(8,128)S(1)} %get-tuple-element.49.refs_5_) | copy-start | bytes 393220
  132.1 1.4 copy-start.2
  133.5 1.2 copy-start.6
  136.4 46.4 %copy-start.24 = (f32[32,16,128]{2,1,0:T(8,128)S(1)}, f32[32,16,128]{2,1,0:T(8,128)}, u32[]{:S(2)}) copy-start(f32[32,16,128]{2,1,0:T(8,128)} %copy-done.23) | copy-start | bytes 786436
  136.4 46.3 %copy-start.28 = (f32[4,64,128]{2,1,0:T(8,128)S(1)}, f32[4,64,128]{2,1,0:T(8,128)}, u32[]{:S(2)}) copy-start(f32[4,64,128]{2,1,0:T(8,128)} %copy-done.27) | copy-start | bytes 393220
  136.4 46.3 %copy-start.34 = (f32[64,64]{1,0:T(8,128)S(1)}, f32[64,64]{1,0:T(8,128)}, u32[]{:S(2)}) copy-start(f32[64,64]{1,0:T(8,128)} %copy-done.33) | copy-start | bytes 49156
  136.4 46.3 %copy-start.36 = (f32[64,64]{1,0:T(8,128)S(1)}, f32[64,64]{1,0:T(8,128)}, u32[]{:S(2)}) copy-start(f32[64,64]{1,0:T(8,128)} %copy-done.35) | copy-start | bytes 49156
  149.6 33.2 %copy-start.9 = (f32[4,64,128]{2,1,0:T(8,128)S(1)}, f32[4,64,128]{2,1,0:T(8,128)}, u32[]{:S(2)}) copy-start(f32[4,64,128]{2,1,0:T(8,128)} %copy-done.8) | copy-start | bytes 393220
  149.6 33.3 %copy-start.11 = (f32[4,64,128]{2,1,0:T(8,128)S(1)}, f32[4,64,128]{2,1,0:T(8,128)}, u32[]{:S(2)}) copy-start(f32[4,64,128]{2,1,0:T(8,128)} %copy-done.10) | copy-start | bytes 393220
  149.6 33.3 %copy-start.13 = (f32[4,64,128]{2,1,0:T(8,128)S(1)}, f32[4,64,128]{2,1,0:T(8,128)}, u32[]{:S(2)}) copy-start(f32[4,64,128]{2,1,0:T(8,128)} %copy-done.12) | copy-start | bytes 393220
  189.6 0.7 copy-start.14
  190.3 0.7 copy-start.16
  191.6 0.7 copy-start.25
  193.6 1.2 copy-start.3
  194.8 1.2 copy-start.7
  196.0 0.9 copy-start.15
  196.9 0.9 copy-start.17
  197.8 0.9 copy-start.19
  198.7 0.9 copy-start.26
  201.3 41.0 %copy-start.30 = (f32[4,64,128]{2,1,0:T(8,128)S(1)}, f32[4,64,128]{2,1,0:T(8,128)}, u32[]{:S(2)}) copy-start(f32[4,64,128]{2,1,0:T(8,128)} %copy-done.29) | copy-start | bytes 393220
  201.3 41.0 %copy-start.32 = (f32[64,64]{1,0:T(8,128)S(1)}, f32[64,64]{1,0:T(8,128)}, u32[]{:S(2)}) copy-start(f32[64,64]{1,0:T(8,128)} %copy-done.31) | copy-start | bytes 49156
  (6 other events, 3.8 us)

commit v5 on v4

--- a/solution.py
+++ b/solution.py
@@ -21,6 +21,8 @@
 PIECE = 32
 STRIP = 8
 OWN = 2 * STRIP
+GRANT = 16 * 2**20
+NOTES = 56
 NT = (((1,), (1,)), ((), ()))
 NN = (((1,), (0,)), ((), ()))
 VMEM = pl.BlockSpec(memory_space=pltpu.VMEM)
@@ -44,6 +46,7 @@
         out_specs=[VMEM] * len(outs),
         out_shape=[make(s, d) for s, d in outs],
         scratch_shapes=scratch,
+        compiler_params=pltpu.CompilerParams(vmem_limit_bytes=GRANT if near else None),
         name=name,
     )
 
@@ -78,13 +81,13 @@
     place = ((cols // 2) * BLKS + rows_ref[...]) * 2 + cols % 2
     place = jnp.where(counts_ref[...] > 0, place, -1).astype(F32)
     lines = [*thirds(reg_ref[...]), place]
-    lines.append(jnp.zeros((16 - len(lines), PIECE), F32))
+    lines.append(jnp.zeros((8 - len(lines), PIECE), F32))
     notes = jnp.concatenate(lines, axis=0)
-    notes = jnp.concatenate([notes, jnp.zeros((16, LANE - PIECE), F32)], axis=1)
+    notes = jnp.concatenate([notes, jnp.zeros((8, LANE - PIECE), F32)], axis=1)
     tiles = [tile.astype(BF16) for tile in (*thirds(packed), notes)]
     for k in range(COLS):
         for i, tile in enumerate(tiles):
-            out_ref[k, base + 16 * i : base + 16 * i + 16, :] = tile
+            out_ref[k, base + 16 * i : base + 16 * i + tile.shape[0], :] = tile
 
 
 def pixel_rows(fields):
@@ -92,12 +95,12 @@
 
 
 def unpack_kernel(place_ref, got_ref, res_ref, reg_ref, own_ref, own_reg_ref, out_ref, tall_ref):
-    base = got_ref.shape[1] - 4 * 16
+    base = got_ref.shape[1] - NOTES
     packed, notes = [], []
     for k in range(COLS):
-        parts = [got_ref[k, base + 16 * i : base + 16 * i + 16, :].astype(F32) for i in range(4)]
+        parts = [got_ref[k, base + 16 * i : base + 16 * i + 16, :].astype(F32) for i in range(3)]
         packed.append(parts[0] + parts[1] + parts[2])
-        note = parts[3]
+        note = got_ref[k, base + 48 : base + NOTES, :].astype(F32)
         notes.append(note[0:1] + note[1:2] + note[2:3])
     group = lax.broadcasted_iota(jnp.int32, (16, LANE), 1) // PIECE
     fields, regs = [], []
@@ -311,7 +314,7 @@
         spread = spread - exact_dot(spread_img, both_halves(alpha), NN)
         new_spread_ref[...] = spread.reshape(sources, OWN, LANE)
         new_spread_img_ref[...] = spread_img.reshape(sources, OWN, LANE)
-        own_ref[...] = new_spread_ref[place_ref[1]]
+        own_ref[...] = new_spread_ref[place_ref[0]]
     alpha_t = alpha.T
     wide = [
         jnp.concatenate(
@@ -356,14 +359,15 @@
     own_share = ((OWN, LANE), F32)
     spread_share = ((sources, OWN, LANE), F32)
     msg = ((COLS, OWN + 8, LANE), F32)
-    start = ((COLS, STRIP * sources + 64, LANE), BF16)
+    start = ((COLS, STRIP * sources + NOTES, LANE), BF16)
     dense = ((2 * BLKS, pixels, LANE), BF16)
 
     (packed,) = call(pack_kernel, [VMEM] * 6, [start], [], "pack", near=False)(
         right_side.T, regular.reshape(1, PIECE), *tables, curv
     )
-    here = jnp.stack([lax.axis_index(COL), lax.axis_index(ROW)]).astype(jnp.int32)
-    packed, here = lax.optimization_barrier((packed, here))
+    col_here = lax.axis_index(COL).astype(jnp.int32).reshape(1)
+    row_here = lax.axis_index(ROW).astype(jnp.int32).reshape(1)
+    packed, col_here, row_here = lax.optimization_barrier((packed, col_here, row_here))
     packed = swap(packed, COL)
     res, reg, own, own_reg, out = call(
         unpack_kernel,
@@ -371,7 +375,7 @@
         [field, ((BLKS, 8, LANE), F32), own_share, own_share, spread_share],
         [pltpu.VMEM((2, LANE, LANE), F32)],
         "unpack",
-    )(here, packed)
+    )(col_here, packed)
     spread = swap(out, ROW)
     places = packed[:, STRIP * sources + 51, 0:sources].astype(jnp.int32)
     high, low = call(
@@ -413,13 +417,13 @@
                 [keep],
                 f"solve_{step}",
                 jax.ShapeDtypeStruct,
-            )(here, got, res, reg, *state)
+            )(col_here, got, res, reg, *state)
             return tuple(part.T for part in shares)
         inputs = [got, res, reg, *state, spread, fresh, *spread_img]
         outs = [field] * 4 + [small] * 2 + [spread_share] * 2 + [own_share]
         res, *state, spread, img, own = call(
             solve, [SMEM] + [VMEM] * len(inputs), outs, [], f"solve_{step}"
-        )(here, *inputs)
+        )(row_here, *inputs)
         spread_img = [img]
 
 

time: 249 us -> 226 us (0.908)
  local copies, waits for them, and re-layouts: 20.6 us -> 0 us
  waiting for transfers between devices: 5.89 us -> 9.08 us
    unnamed x74 -> x0, local copies, waits for them, and re-layouts: 20.6 us -> none
    all_to_all x1, waiting for transfers between devices: 5.89 us -> 9.08 us  [swap(): return lax.all_to_all(msg, axes, 0, 0, tiled=True)]
where the time goes in v5:
time: 226 us; the launch traced here: 225 us
  blocking collectives  177 us (78%)
  Pallas kernels  28.3 us (13%)
  starting transfers between devices  9.8 us (4%)
  waiting for transfers between devices  9.08 us (4%)
    all_to_all x10, blocking collectives, swap(): return lax.all_to_all(msg, axes, 0, 0, tiled=True)  177 us
    pallas_call x15, Pallas kernels, placed(): return run(*args)  28.3 us
    all_to_all x1, starting transfers between devices, swap(): return lax.all_to_all(msg, axes, 0, 0, tiled=True)  9.8 us
    all_to_all x1, waiting for transfers between devices, swap(): return lax.all_to_all(msg, axes, 0, 0, tiled=True)  9.08 us
  transfers between devices with their start and end apart: 1, of which 1 were waited for; matrix products, arithmetic and copies ran while one was open for 0% of the time, Pallas kernels for 2%

profile of v5, /device:TPU:1, one launch (start us, length us, event | category | flops | bytes accessed | tf_op | source)
XLA Modules:
  0.0 225.4 jit_solution(10215502937922187258)
XLA Ops:
  0.6 1.7 pack.1
  2.4 45.0 %all_to_all.55.got_ref = bf16[16,312,128]{2,1,0:T(8,128)(2,1)S(1)} all-to-all(bf16[16,312,128]{2,1,0:T(8,128)(2,1)S(1)} %pack.1), channel_id=1, replica_groups=mesh['row_0'=8,'row_1'=4,'col_0'=8,'col_1'=2] {'col_0','col_1'}, dimensions={0} | all-to-all | bytes 2555904 | tf_op jit(solution)/shard_map/all_to_all | solution.py:39
  47.3 1.1 unpack.1
  48.4 9.8 %all-to-all-start.1 = ((f32[32,16,128]{2,1,0:T(8,128)}), f32[32,16,128]{2,1,0:T(8,128)}, u32[]{:S(2)}, u32[]{:S(2)}) async-start(f32[32,16,128]{2,1,0:T(8,128)} %get-tuple-element.40), calls=%async_computation.1 | async-start | bytes 524288 | tf_op jit(solution)/shard_map/all_to_all | solution.py:39
  58.3 3.8 %dense.1 = (bf16[8,512,128]{2,1,0:T(8,128)(2,1)S(1)}, bf16[8,512,128]{2,1,0:T(8,128)(2,1)S(1)}) custom-call(s32[16,32]{1,0:T(8,128)S(1)} %bitcast.11, bf16[16,312,128]{2,1,0:T(8,128)(2,1)S(1)} %all_to_all.55.got_ref), custom_call_target="tpu_custom_call" | custom-call | tf_op jit(solution)/shard_map/dense/pallas_call | solution.py:59
  62.1 9.1 %all-to-all-done.1.refs_0_.refs_4_ = f32[32,16,128]{2,1,0:T(8,128)} async-done(((f32[32,16,128]{2,1,0:T(8,128)}), f32[32,16,128]{2,1,0:T(8,128)}, u32[]{:S(2)}, u32[]{:S(2)}) %all-to-all-start.1) | async-done | bytes 262176 | tf_op jit(solution)/shard_map/all_to_all | solution.py:39
  71.1 2.3 %product_0.1 = f32[16,24,128]{2,1,0:T(8,128)S(1)} custom-call(f32[32,16,128]{2,1,0:T(8,128)} %all-to-all-done.1.refs_0_.refs_4_, bf16[8,512,128]{2,1,0:T(8,128)(2,1)S(1)} %get-tuple-element.41.refs_1_, bf16[8,512,128]{2,1,0:T(8,128)(2,1)S(1)} %get-tuple-element.42.refs_2_, f32[4,64,128]{2,1,0:T(8,128)S(1)} %get-tuple-element.43.refs_3_.refs_2_, ...), custom_call_target="tpu_custom_call" | custom-call | tf_op jit(solution)/shard_map/product_0/pallas_call | solution.py:59
  73.4 13.6 %all_to_all.56.got_ref = f32[16,24,128]{2,1,0:T(8,128)S(1)} all-to-all(f32[16,24,128]{2,1,0:T(8,128)S(1)} %product_0.1), channel_id=1, replica_groups=mesh['row_0'=8,'row_1'=4,'col_0'=8,'col_1'=2] {'col_0','col_1'}, dimensions={0} | all-to-all | bytes 393216 | tf_op jit(solution)/shard_map/all_to_all | solution.py:39
  87.0 18.1 %all_to_all.57.got_ref.refs_5_ = f32[32,24,128]{2,1,0:T(8,128)S(1)} all-to-all(f32[32,24,128]{2,1,0:T(8,128)S(1)} %get-tuple-element.47), channel_id=1, replica_groups=mesh['row_0'=8,'row_1'=4,'col_0'=8,'col_1'=2] {'row_0','row_1'}, dimensions={0} | all-to-all | bytes 786432 | tf_op jit(solution)/shard_map/all_to_all | solution.py:39
  105.2 14.1 %all_to_all.58.refs_1_ = f32[16,24,128]{2,1,0:T(8,128)S(1)} all-to-all(f32[16,24,128]{2,1,0:T(8,128)S(1)} %row_sum_0.1), channel_id=1, replica_groups=mesh['row_0'=8,'row_1'=4,'col_0'=8,'col_1'=2] {'col_0','col_1'}, dimensions={0} | all-to-all | bytes 393216 | tf_op jit(solution)/shard_map/all_to_all | solution.py:39
  119.3 4.8 %solve_0.1 = (f32[4,64,128]{2,1,0:T(8,128)S(1)}, f32[4,64,128]{2,1,0:T(8,128)S(1)}, f32[4,64,128]{2,1,0:T(8,128)S(1)}, f32[4,64,128]{2,1,0:T(8,128)S(1)}, f32[64...) custom-call(s32[1]{0:T(128)} %bitcast.7.refs_0_, ...), custom_call_target="tpu_custom_call" | custom-call | tf_op jit(solution)/shard_map/solve_0/pallas_call | solution.py:59
  124.1 1.6 product_1.1
  125.7 13.0 %all_to_all.59.got_ref = f32[16,24,128]{2,1,0:T(8,128)S(1)} all-to-all(f32[16,24,128]{2,1,0:T(8,128)S(1)} %product_1.1), channel_id=1, replica_groups=mesh['row_0'=8,'row_1'=4,'col_0'=8,'col_1'=2] {'col_0','col_1'}, dimensions={0} | all-to-all | bytes 393216 | tf_op jit(solution)/shard_map/all_to_all | solution.py:39
  138.7 18.5 %all_to_all.60.got_ref.refs_10_ = f32[32,24,128]{2,1,0:T(8,128)S(1)} all-to-all(f32[32,24,128]{2,1,0:T(8,128)S(1)} %get-tuple-element.54), channel_id=1, replica_groups=mesh['row_0'=8,'row_1'=4,'col_0'=8,'col_1'=2] {'row_0','row_1'}, dimensions={0} | all-to-all | bytes 786432 | tf_op jit(solution)/shard_map/all_to_all | solution.py:39
  157.3 14.5 %all_to_all.61.refs_1_ = f32[16,24,128]{2,1,0:T(8,128)S(1)} all-to-all(f32[16,24,128]{2,1,0:T(8,128)S(1)} %row_sum_1.1), channel_id=1, replica_groups=mesh['row_0'=8,'row_1'=4,'col_0'=8,'col_1'=2] {'col_0','col_1'}, dimensions={0} | all-to-all | bytes 393216 | tf_op jit(solution)/shard_map/all_to_all | solution.py:39
  171.8 6.1 %solve_1.1 = (f32[4,64,128]{2,1,0:T(8,128)S(1)}, f32[4,64,128]{2,1,0:T(8,128)S(1)}, f32[4,64,128]{2,1,0:T(8,128)S(1)}, f32[4,64,128]{2,1,0:T(8,128)S(1)}, f32[64...) custom-call(s32[1]{0:T(128)} %bitcast.7.refs_0_, ...), custom_call_target="tpu_custom_call" | custom-call | tf_op jit(solution)/shard_map/solve_1/pallas_call | solution.py:59
  177.9 1.6 product_2.1
  179.6 12.8 %all_to_all.62.got_ref = f32[16,24,128]{2,1,0:T(8,128)S(1)} all-to-all(f32[16,24,128]{2,1,0:T(8,128)S(1)} %product_2.1), channel_id=1, replica_groups=mesh['row_0'=8,'row_1'=4,'col_0'=8,'col_1'=2] {'col_0','col_1'}, dimensions={0} | all-to-all | bytes 393216 | tf_op jit(solution)/shard_map/all_to_all | solution.py:39
  192.4 13.7 %all_to_all.63.got_ref = f32[32,8,128]{2,1,0:T(8,128)S(1)} all-to-all(f32[32,8,128]{2,1,0:T(8,128)S(1)} %get-tuple-element.65), channel_id=1, replica_groups=mesh['row_0'=8,'row_1'=4,'col_0'=8,'col_1'=2] {'row_0','row_1'}, dimensions={0} | all-to-all | bytes 262144 | tf_op jit(solution)/shard_map/all_to_all | solution.py:39
  206.1 14.2 %all_to_all.64.refs_1_ = f32[16,24,128]{2,1,0:T(8,128)S(1)} all-to-all(f32[16,24,128]{2,1,0:T(8,128)S(1)} %row_sum_2.1), channel_id=1, replica_groups=mesh['row_0'=8,'row_1'=4,'col_0'=8,'col_1'=2] {'col_0','col_1'}, dimensions={0} | all-to-all | bytes 393216 | tf_op jit(solution)/shard_map/all_to_all | solution.py:39
  220.4 5.0 %solve_2.1 = (f32[32,64]{1,0:T(8,128)}, f32[32,64]{1,0:T(8,128)}) custom-call(s32[1]{0:T(128)} %bitcast.6.place_ref.refs_0_, f32[16,24,128]{2,1,0:T(8,128)S(1)} %all_to_all.64.refs_1_, f32[4,64,128]{2,1,0:T(8,128)S(1)} %get-tuple-element.61.refs_3_.refs_2_, f32[4,8,128]{2,1,0:T(8,128)S(1)} %get-tuple-element.44.refs_4_.refs_3_, ...), custom_call_target="tpu_custom_call" | custom-call | tf_op jit(solution)/shard_map/solve_2/pallas_call | solution.py:59
  (7 shorter events, 0.3 us)
Async XLA Ops:
  48.4 22.7 %all-to-all-start.1 = ((f32[32,16,128]{2,1,0:T(8,128)}), f32[32,16,128]{2,1,0:T(8,128)}, u32[]{:S(2)}, u32[]{:S(2)}) async-start(f32[32,16,128]{2,1,0:T(8,128)} %get-tuple-element.40), calls=%async_computation.1 | async-start | bytes 524288 | tf_op jit(solution)/shard_map/all_to_all | solution.py:39

commit v6 on v5

--- a/solution.py
+++ b/solution.py
@@ -162,7 +162,10 @@
     spread = spread_ref[...].reshape(pixels, LANE)
     inputs = jnp.concatenate(
         [spread[LANE * i : LANE * i + LANE, :].T for i in range(pixels // LANE)], axis=1
-    ).astype(BF16)
+    )
+    parts = [inputs.astype(BF16)]
+    if not first:
+        parts.append((inputs - parts[0].astype(F32)).astype(BF16))
     share = 1.0 / COLS
     pair = jnp.zeros((SMP, LANE), F32)
     mixed = jnp.zeros((SMP, SMP), F32)
@@ -170,11 +173,14 @@
     for b in range(BLKS):
         acc = jnp.zeros((SMP, LANE), F32)
         for half in range(2):
-            left = inputs[SMP * half : SMP * half + SMP, :]
-            for weights in (high_ref, low_ref):
-                acc += lax.dot_general(
-                    left, weights[BLKS * half + b], NN, preferred_element_type=F32
-                )
+            for i, weights in enumerate((high_ref, low_ref)):
+                for part in parts[: 2 - i]:
+                    acc += lax.dot_general(
+                        part[SMP * half : SMP * half + SMP, :],
+                        weights[BLKS * half + b],
+                        NN,
+                        preferred_element_type=F32,
+                    )
         coupled.append(acc)
         res = res_ref[b]
         part = acc + reg_ref[b, 0:1, :] * res * share
@@ -271,8 +277,9 @@
 
 def solve_kernel(first, last, *refs):
     refs = list(refs)
-    place_ref, got_ref, res_ref, reg_ref = refs[:4]
-    refs = refs[4:]
+    col_ref, row_ref, got_ref, res_ref, reg_ref = refs[:5]
+    refs = refs[5:]
+    mine = col_ref[0] // 4
     if not first:
         dir_ref, img_ref, sol_ref, inv_ref, curv_ref = refs[:5]
         refs = refs[5:]
@@ -314,7 +321,7 @@
         spread = spread - exact_dot(spread_img, both_halves(alpha), NN)
         new_spread_ref[...] = spread.reshape(sources, OWN, LANE)
         new_spread_img_ref[...] = spread_img.reshape(sources, OWN, LANE)
-        own_ref[...] = new_spread_ref[place_ref[0]]
+        own_ref[...] = new_spread_ref[row_ref[0]]
     alpha_t = alpha.T
     wide = [
         jnp.concatenate(
@@ -322,31 +329,36 @@
         ).T
         for b in range(2)
     ]
-    for b in range(BLKS):
+
+    def advance(coupled, b):
         res = res_ref[b]
-        half = SMP * (b // 2)
-        image = wide[b % 2][half : half + SMP, :] + reg_ref[b, 0:1, :] * res
+        image = coupled + reg_ref[b][0:1, :] * res
         direction = res
         if not first:
             image = image + exact_dot(beta_t, img_ref[b], NN)
             direction = direction + exact_dot(beta_t, dir_ref[b], NN)
-        new_res = res - exact_dot(alpha_t, image, NN)
-        new_sol = exact_dot(alpha_t, direction, NN)
-        if not first:
-            new_sol = sol_ref[b] + new_sol
-        if last:
-            keep_ref[0, b] = new_sol
-            keep_ref[1, b] = new_res
-        else:
-            new_res_ref[b] = new_res
-            new_dir_ref[b] = direction
-            new_img_ref[b] = image
-            new_sol_ref[b] = new_sol
+        return res - exact_dot(alpha_t, image, NN), image, direction
+
     if last:
-        mine = place_ref[0]
-        shift = (LANE - PIECE * (mine % 4)) % LANE
-        out_sol_ref[...] = pltpu.roll(keep_ref[0, mine // 4], shift, 1)[:, 0:PIECE].T
-        out_res_ref[...] = pltpu.roll(keep_ref[1, mine // 4], shift, 1)[:, 0:PIECE].T
+        for b in range(2):
+            keep_ref[b] = wide[b]
+        start = pl.multiple_of(SMP * (mine // 2), SMP)
+        new_res, _, direction = advance(keep_ref[mine % 2, pl.ds(start, SMP), :], mine)
+    else:
+        for b in range(BLKS):
+            half = SMP * (b // 2)
+            coupled = wide[b % 2][half : half + SMP, :]
+            new_res_ref[b], new_img_ref[b], new_dir_ref[b] = advance(coupled, b)
+        direction = new_dir_ref[mine]
+    new_sol = exact_dot(alpha_t, direction, NN)
+    if not first:
+        new_sol = sol_ref[...] + new_sol
+    if last:
+        shift = (LANE - PIECE * (col_ref[0] % 4)) % LANE
+        out_sol_ref[...] = pltpu.roll(new_sol, shift, 1)[:, 0:PIECE].T
+        out_res_ref[...] = pltpu.roll(new_res, shift, 1)[:, 0:PIECE].T
+    else:
+        new_sol_ref[...] = new_sol
 
 
 def body(right_side, regular, curvature, block_rows, block_cols, block_counts):
@@ -409,21 +421,21 @@
         solve = functools.partial(solve_kernel, first, last)
         if last:
             share = ((PIECE, SMP), F32)
-            keep = pltpu.VMEM((2, BLKS, SMP, LANE), F32)
+            keep = pltpu.VMEM((2, LANE, LANE), F32)
             shares = call(
                 solve,
-                [SMEM] + [VMEM] * (3 + len(state)),
+                [SMEM] * 2 + [VMEM] * (3 + len(state)),
                 [share, share],
                 [keep],
                 f"solve_{step}",
                 jax.ShapeDtypeStruct,
-            )(col_here, got, res, reg, *state)
+            )(col_here, row_here, got, res, reg, *state)
             return tuple(part.T for part in shares)
         inputs = [got, res, reg, *state, spread, fresh, *spread_img]
-        outs = [field] * 4 + [small] * 2 + [spread_share] * 2 + [own_share]
+        outs = [field] * 3 + [((SMP, LANE), F32)] + [small] * 2 + [spread_share] * 2 + [own_share]
         res, *state, spread, img, own = call(
-            solve, [SMEM] + [VMEM] * len(inputs), outs, [], f"solve_{step}"
-        )(row_here, *inputs)
+            solve, [SMEM] * 2 + [VMEM] * len(inputs), outs, [], f"solve_{step}"
+        )(col_here, row_here, *inputs)
         spread_img = [img]
 
 

time: 226 us -> 226 us (level)
  no operation moved by 1% of the time
where the time goes in v6:
time: 226 us; the launch traced here: 225 us
  blocking collectives  178 us (79%)
  Pallas kernels  28.2 us (12%)
  starting transfers between devices  9.8 us (4%)
  waiting for transfers between devices  9.08 us (4%)
    all_to_all x10, blocking collectives, swap(): return lax.all_to_all(msg, axes, 0, 0, tiled=True)  178 us
    pallas_call x15, Pallas kernels, placed(): return run(*args)  28.2 us
    all_to_all x1, starting transfers between devices, swap(): return lax.all_to_all(msg, axes, 0, 0, tiled=True)  9.8 us
    all_to_all x1, waiting for transfers between devices, swap(): return lax.all_to_all(msg, axes, 0, 0, tiled=True)  9.08 us
  transfers between devices with their start and end apart: 1, of which 1 were waited for; matrix products, arithmetic and copies ran while one was open for 0% of the time, Pallas kernels for 2%

profile of v6, /device:TPU:1, one launch (start us, length us, event | category | flops | bytes accessed | tf_op | source)
XLA Modules:
  0.0 225.4 jit_solution(6427466213458029094)
XLA Ops:
  0.6 1.7 pack.1
  2.4 45.0 %all_to_all.55.got_ref = bf16[16,312,128]{2,1,0:T(8,128)(2,1)S(1)} all-to-all(bf16[16,312,128]{2,1,0:T(8,128)(2,1)S(1)} %pack.1), channel_id=1, replica_groups=mesh['row_0'=8,'row_1'=4,'col_0'=8,'col_1'=2] {'col_0','col_1'}, dimensions={0} | all-to-all | bytes 2555904 | tf_op jit(solution)/shard_map/all_to_all | solution.py:39
  47.3 1.1 unpack.1
  48.4 9.8 %all-to-all-start.1 = ((f32[32,16,128]{2,1,0:T(8,128)}), f32[32,16,128]{2,1,0:T(8,128)}, u32[]{:S(2)}, u32[]{:S(2)}) async-start(f32[32,16,128]{2,1,0:T(8,128)} %get-tuple-element.40), calls=%async_computation.1 | async-start | bytes 524288 | tf_op jit(solution)/shard_map/all_to_all | solution.py:39
  58.3 3.8 %dense.1 = (bf16[8,512,128]{2,1,0:T(8,128)(2,1)S(1)}, bf16[8,512,128]{2,1,0:T(8,128)(2,1)S(1)}) custom-call(s32[16,32]{1,0:T(8,128)S(1)} %bitcast.11, bf16[16,312,128]{2,1,0:T(8,128)(2,1)S(1)} %all_to_all.55.got_ref), custom_call_target="tpu_custom_call" | custom-call | tf_op jit(solution)/shard_map/dense/pallas_call | solution.py:59
  62.1 9.1 %all-to-all-done.1.refs_0_.refs_5_ = f32[32,16,128]{2,1,0:T(8,128)} async-done(((f32[32,16,128]{2,1,0:T(8,128)}), f32[32,16,128]{2,1,0:T(8,128)}, u32[]{:S(2)}, u32[]{:S(2)}) %all-to-all-start.1) | async-done | bytes 262176 | tf_op jit(solution)/shard_map/all_to_all | solution.py:39
  71.1 2.3 %product_0.1 = f32[16,24,128]{2,1,0:T(8,128)S(1)} custom-call(f32[32,16,128]{2,1,0:T(8,128)} %all-to-all-done.1.refs_0_.refs_5_, bf16[8,512,128]{2,1,0:T(8,128)(2,1)S(1)} %get-tuple-element.41.refs_1_, bf16[8,512,128]{2,1,0:T(8,128)(2,1)S(1)} %get-tuple-element.42.refs_2_, f32[4,64,128]{2,1,0:T(8,128)S(1)} %get-tuple-element.43.refs_3_, ...), custom_call_target="tpu_custom_call" | custom-call | tf_op jit(solution)/shard_map/product_0/pallas_call | solution.py:59
  73.4 13.6 %all_to_all.56.got_ref = f32[16,24,128]{2,1,0:T(8,128)S(1)} all-to-all(f32[16,24,128]{2,1,0:T(8,128)S(1)} %product_0.1), channel_id=1, replica_groups=mesh['row_0'=8,'row_1'=4,'col_0'=8,'col_1'=2] {'col_0','col_1'}, dimensions={0} | all-to-all | bytes 393216 | tf_op jit(solution)/shard_map/all_to_all | solution.py:39
  87.0 18.1 %all_to_all.57.got_ref.refs_6_ = f32[32,24,128]{2,1,0:T(8,128)S(1)} all-to-all(f32[32,24,128]{2,1,0:T(8,128)S(1)} %get-tuple-element.47), channel_id=1, replica_groups=mesh['row_0'=8,'row_1'=4,'col_0'=8,'col_1'=2] {'row_0','row_1'}, dimensions={0} | all-to-all | bytes 786432 | tf_op jit(solution)/shard_map/all_to_all | solution.py:39
  105.2 14.1 %all_to_all.58.refs_2_ = f32[16,24,128]{2,1,0:T(8,128)S(1)} all-to-all(f32[16,24,128]{2,1,0:T(8,128)S(1)} %row_sum_0.1), channel_id=1, replica_groups=mesh['row_0'=8,'row_1'=4,'col_0'=8,'col_1'=2] {'col_0','col_1'}, dimensions={0} | all-to-all | bytes 393216 | tf_op jit(solution)/shard_map/all_to_all | solution.py:39
  119.3 4.7 %solve_0.1 = (f32[4,64,128]{2,1,0:T(8,128)S(1)}, f32[4,64,128]{2,1,0:T(8,128)S(1)}, f32[4,64,128]{2,1,0:T(8,128)S(1)}, f32[64,128]{1,0:T(8,128)S(1)}, f32[64,64]...) custom-call(s32[1]{0:T(128)} %bitcast.6.place_ref.refs_0_, ...), custom_call_target="tpu_custom_call" | custom-call | tf_op jit(solution)/shard_map/solve_0/pallas_call | solution.py:59
  124.0 2.2 product_1.1
  126.1 13.0 %all_to_all.59.got_ref = f32[16,24,128]{2,1,0:T(8,128)S(1)} all-to-all(f32[16,24,128]{2,1,0:T(8,128)S(1)} %product_1.1), channel_id=1, replica_groups=mesh['row_0'=8,'row_1'=4,'col_0'=8,'col_1'=2] {'col_0','col_1'}, dimensions={0} | all-to-all | bytes 393216 | tf_op jit(solution)/shard_map/all_to_all | solution.py:39
  139.1 18.5 %all_to_all.60.got_ref.refs_11_ = f32[32,24,128]{2,1,0:T(8,128)S(1)} all-to-all(f32[32,24,128]{2,1,0:T(8,128)S(1)} %get-tuple-element.54), channel_id=1, replica_groups=mesh['row_0'=8,'row_1'=4,'col_0'=8,'col_1'=2] {'row_0','row_1'}, dimensions={0} | all-to-all | bytes 786432 | tf_op jit(solution)/shard_map/all_to_all | solution.py:39
  157.7 14.5 %all_to_all.61.refs_2_ = f32[16,24,128]{2,1,0:T(8,128)S(1)} all-to-all(f32[16,24,128]{2,1,0:T(8,128)S(1)} %row_sum_1.1), channel_id=1, replica_groups=mesh['row_0'=8,'row_1'=4,'col_0'=8,'col_1'=2] {'col_0','col_1'}, dimensions={0} | all-to-all | bytes 393216 | tf_op jit(solution)/shard_map/all_to_all | solution.py:39
  172.3 5.9 %solve_1.1 = (f32[4,64,128]{2,1,0:T(8,128)S(1)}, f32[4,64,128]{2,1,0:T(8,128)S(1)}, f32[4,64,128]{2,1,0:T(8,128)S(1)}, f32[64,128]{1,0:T(8,128)S(1)}, f32[64,64]...) custom-call(s32[1]{0:T(128)} %bitcast.6.place_ref.refs_0_, ...), custom_call_target="tpu_custom_call" | custom-call | tf_op jit(solution)/shard_map/solve_1/pallas_call | solution.py:59
  178.2 2.2 product_2.1
  180.4 12.9 %all_to_all.62.got_ref = f32[16,24,128]{2,1,0:T(8,128)S(1)} all-to-all(f32[16,24,128]{2,1,0:T(8,128)S(1)} %product_2.1), channel_id=1, replica_groups=mesh['row_0'=8,'row_1'=4,'col_0'=8,'col_1'=2] {'col_0','col_1'}, dimensions={0} | all-to-all | bytes 393216 | tf_op jit(solution)/shard_map/all_to_all | solution.py:39
  193.3 13.7 %all_to_all.63.got_ref = f32[32,8,128]{2,1,0:T(8,128)S(1)} all-to-all(f32[32,8,128]{2,1,0:T(8,128)S(1)} %get-tuple-element.65), channel_id=1, replica_groups=mesh['row_0'=8,'row_1'=4,'col_0'=8,'col_1'=2] {'row_0','row_1'}, dimensions={0} | all-to-all | bytes 262144 | tf_op jit(solution)/shard_map/all_to_all | solution.py:39
  207.0 14.2 %all_to_all.64.refs_2_ = f32[16,24,128]{2,1,0:T(8,128)S(1)} all-to-all(f32[16,24,128]{2,1,0:T(8,128)S(1)} %row_sum_2.1), channel_id=1, replica_groups=mesh['row_0'=8,'row_1'=4,'col_0'=8,'col_1'=2] {'col_0','col_1'}, dimensions={0} | all-to-all | bytes 393216 | tf_op jit(solution)/shard_map/all_to_all | solution.py:39
  221.3 4.1 %solve_2.1 = (f32[32,64]{1,0:T(8,128)}, f32[32,64]{1,0:T(8,128)}) custom-call(s32[1]{0:T(128)} %bitcast.6.place_ref.refs_0_, s32[1]{0:T(128)} %bitcast.7.refs_1_, f32[16,24,128]{2,1,0:T(8,128)S(1)} %all_to_all.64.refs_2_, f32[4,64,128]{2,1,0:T(8,128)S(1)} %get-tuple-element.61.refs_3_, f32[4,8,128]{2,1,0:T(8,128)S(1)} %get-tuple-element.44.refs_4_, ...), custom_call_target="tpu_custom_call" | custom-call | tf_op jit(solution)/shard_map/solve_2/pallas_call | solution.py:59
  (7 shorter events, 0.3 us)
Async XLA Ops:
  48.4 22.7 %all-to-all-start.1 = ((f32[32,16,128]{2,1,0:T(8,128)}), f32[32,16,128]{2,1,0:T(8,128)}, u32[]{:S(2)}, u32[]{:S(2)}) async-start(f32[32,16,128]{2,1,0:T(8,128)} %get-tuple-element.40), calls=%async_computation.1 | async-start | bytes 524288 | tf_op jit(solution)/shard_map/all_to_all | solution.py:39

commit v7 on v6

--- a/solution.py
+++ b/solution.py
@@ -152,6 +152,10 @@
         low_ref[plane] = (total - high.astype(F32)).astype(BF16)
 
 
+def flat(field_ref):
+    return jnp.concatenate([field_ref[b] for b in range(BLKS)], axis=1)
+
+
 def product_kernel(first, *refs):
     spread_ref, high_ref, low_ref, res_ref, reg_ref = refs[:5]
     if first:
@@ -163,30 +167,31 @@
     inputs = jnp.concatenate(
         [spread[LANE * i : LANE * i + LANE, :].T for i in range(pixels // LANE)], axis=1
     )
-    parts = [inputs.astype(BF16)]
-    if not first:
-        parts.append((inputs - parts[0].astype(F32)).astype(BF16))
-    share = 1.0 / COLS
-    pair = jnp.zeros((SMP, LANE), F32)
-    mixed = jnp.zeros((SMP, SMP), F32)
+    top = inputs.astype(BF16)
+    low = (inputs - top.astype(F32)).astype(BF16)
     coupled = []
     for b in range(BLKS):
         acc = jnp.zeros((SMP, LANE), F32)
         for half in range(2):
-            for i, weights in enumerate((high_ref, low_ref)):
-                for part in parts[: 2 - i]:
-                    acc += lax.dot_general(
-                        part[SMP * half : SMP * half + SMP, :],
-                        weights[BLKS * half + b],
-                        NN,
-                        preferred_element_type=F32,
-                    )
+            cut = slice(SMP * half, SMP * half + SMP)
+            plane = BLKS * half + b
+            left = top[cut] if first else jnp.concatenate([top[cut], low[cut]], axis=0)
+            main = lax.dot_general(left, high_ref[plane], NN, preferred_element_type=F32)
+            acc += main if first else main[0:SMP] + main[SMP:]
+            acc += lax.dot_general(top[cut], low_ref[plane], NN, preferred_element_type=F32)
         coupled.append(acc)
-        res = res_ref[b]
-        part = acc + reg_ref[b, 0:1, :] * res * share
-        pair += exact_dot(res, jnp.concatenate([part, res * share], axis=0), NT)
-        if not first:
-            mixed += exact_dot(res, img_ref[b] * share, NT) + exact_dot(part, dir_ref[b], NT)
+    share = 1.0 / COLS
+    res = flat(res_ref)
+    part = jnp.concatenate(
+        [coupled[b] + reg_ref[b, 0:1, :] * res_ref[b] * share for b in range(BLKS)], axis=1
+    )
+    pair = exact_dot(res, jnp.concatenate([part, res * share], axis=0), NT)
+    if first:
+        mixed = jnp.zeros((SMP, SMP), F32)
+    else:
+        left = jnp.concatenate([res, part], axis=1)
+        right = jnp.concatenate([flat(img_ref) * share, flat(dir_ref)], axis=1)
+        mixed = exact_dot(left, right, NT)
     other = jnp.concatenate([mixed, jnp.zeros((SMP, LANE - SMP), F32)], axis=1)
     tall = pixel_rows(coupled)
     for k in range(COLS):
@@ -308,7 +313,7 @@
         same = lax.broadcasted_iota(jnp.int32, square, 0) == lax.broadcasted_iota(
             jnp.int32, square, 1
         )
-        alpha, inverse = solve_systems([(curv, gram), (gram, same.astype(F32))], 4)
+        alpha, inverse = solve_systems([(curv, gram), (gram, same.astype(F32))], 8)
         new_inv_ref[...] = inverse
         new_curv_ref[...] = curv
         sources = spread_ref.shape[0]
@@ -330,25 +335,35 @@
         for b in range(2)
     ]
 
-    def advance(coupled, b):
-        res = res_ref[b]
-        image = coupled + reg_ref[b][0:1, :] * res
+    def advance(image, res, pick):
         direction = res
         if not first:
-            image = image + exact_dot(beta_t, img_ref[b], NN)
-            direction = direction + exact_dot(beta_t, dir_ref[b], NN)
+            image = image + exact_dot(beta_t, pick(img_ref), NN)
+            direction = direction + exact_dot(beta_t, pick(dir_ref), NN)
         return res - exact_dot(alpha_t, image, NN), image, direction
 
     if last:
         for b in range(2):
             keep_ref[b] = wide[b]
         start = pl.multiple_of(SMP * (mine // 2), SMP)
-        new_res, _, direction = advance(keep_ref[mine % 2, pl.ds(start, SMP), :], mine)
-    else:
+        res = res_ref[mine]
+        image = keep_ref[mine % 2, pl.ds(start, SMP), :] + reg_ref[mine][0:1, :] * res
+        new_res, _, direction = advance(image, res, lambda ref: ref[mine])
+    else:
+        image = jnp.concatenate(
+            [
+                wide[b % 2][SMP * (b // 2) : SMP * (b // 2) + SMP, :]
+                + reg_ref[b, 0:1, :] * res_ref[b]
+                for b in range(BLKS)
+            ],
+            axis=1,
+        )
+        new_res, image, direction = advance(image, flat(res_ref), flat)
         for b in range(BLKS):
-            half = SMP * (b // 2)
-            coupled = wide[b % 2][half : half + SMP, :]
-            new_res_ref[b], new_img_ref[b], new_dir_ref[b] = advance(coupled, b)
+            cut = slice(LANE * b, LANE * b + LANE)
+            new_res_ref[b] = new_res[:, cut]
+            new_img_ref[b] = image[:, cut]
+            new_dir_ref[b] = direction[:, cut]
         direction = new_dir_ref[mine]
     new_sol = exact_dot(alpha_t, direction, NN)
     if not first:

time: 226 us -> 222 us (0.982)
  Pallas kernels: 28.2 us -> 24.1 us
    pallas_call x15, Pallas kernels: 28.2 us -> 24.1 us  [placed(): return run(*args)]
where the time goes in v7:
time: 222 us; the launch traced here: 221 us
  blocking collectives  177 us (80%)
  Pallas kernels  24.1 us (11%)
  starting transfers between devices  9.8 us (4%)
  waiting for transfers between devices  9.06 us (4%)
    all_to_all x10, blocking collectives, swap(): return lax.all_to_all(msg, axes, 0, 0, tiled=True)  177 us
    pallas_call x15, Pallas kernels, placed(): return run(*args)  24.1 us
    all_to_all x1, starting transfers between devices, swap(): return lax.all_to_all(msg, axes, 0, 0, tiled=True)  9.8 us
    all_to_all x1, waiting for transfers between devices, swap(): return lax.all_to_all(msg, axes, 0, 0, tiled=True)  9.06 us
  transfers between devices with their start and end apart: 1, of which 1 were waited for; matrix products, arithmetic and copies ran while one was open for 0% of the time, Pallas kernels for 2%

profile of v7, /device:TPU:1, one launch (start us, length us, event | category | flops | bytes accessed | tf_op | source)
XLA Modules:
  0.0 221.1 jit_solution(14128413180378059718)
XLA Ops:
  0.6 1.7 pack.1
  2.4 45.0 %all_to_all.55.got_ref = bf16[16,312,128]{2,1,0:T(8,128)(2,1)S(1)} all-to-all(bf16[16,312,128]{2,1,0:T(8,128)(2,1)S(1)} %pack.1), channel_id=1, replica_groups=mesh['row_0'=8,'row_1'=4,'col_0'=8,'col_1'=2] {'col_0','col_1'}, dimensions={0} | all-to-all | bytes 2555904 | tf_op jit(solution)/shard_map/all_to_all | solution.py:39
  47.3 1.1 unpack.1
  48.4 9.8 %all-to-all-start.1 = ((f32[32,16,128]{2,1,0:T(8,128)}), f32[32,16,128]{2,1,0:T(8,128)}, u32[]{:S(2)}, u32[]{:S(2)}) async-start(f32[32,16,128]{2,1,0:T(8,128)} %get-tuple-element.40), calls=%async_computation.1 | async-start | bytes 524288 | tf_op jit(solution)/shard_map/all_to_all | solution.py:39
  58.3 3.8 %dense.1 = (bf16[8,512,128]{2,1,0:T(8,128)(2,1)S(1)}, bf16[8,512,128]{2,1,0:T(8,128)(2,1)S(1)}) custom-call(s32[16,32]{1,0:T(8,128)S(1)} %bitcast.11, bf16[16,312,128]{2,1,0:T(8,128)(2,1)S(1)} %all_to_all.55.got_ref), custom_call_target="tpu_custom_call" | custom-call | tf_op jit(solution)/shard_map/dense/pallas_call | solution.py:59
  62.1 9.1 %all-to-all-done.1.refs_0_.refs_5_ = f32[32,16,128]{2,1,0:T(8,128)} async-done(((f32[32,16,128]{2,1,0:T(8,128)}), f32[32,16,128]{2,1,0:T(8,128)}, u32[]{:S(2)}, u32[]{:S(2)}) %all-to-all-start.1) | async-done | bytes 262176 | tf_op jit(solution)/shard_map/all_to_all | solution.py:39
  71.1 1.8 product_0.1
  72.9 13.6 %all_to_all.56.got_ref = f32[16,24,128]{2,1,0:T(8,128)S(1)} all-to-all(f32[16,24,128]{2,1,0:T(8,128)S(1)} %product_0.1), channel_id=1, replica_groups=mesh['row_0'=8,'row_1'=4,'col_0'=8,'col_1'=2] {'col_0','col_1'}, dimensions={0} | all-to-all | bytes 393216 | tf_op jit(solution)/shard_map/all_to_all | solution.py:39
  86.5 18.1 %all_to_all.57.got_ref.refs_6_ = f32[32,24,128]{2,1,0:T(8,128)S(1)} all-to-all(f32[32,24,128]{2,1,0:T(8,128)S(1)} %get-tuple-element.47), channel_id=1, replica_groups=mesh['row_0'=8,'row_1'=4,'col_0'=8,'col_1'=2] {'row_0','row_1'}, dimensions={0} | all-to-all | bytes 786432 | tf_op jit(solution)/shard_map/all_to_all | solution.py:39
  104.7 14.1 %all_to_all.58.refs_2_ = f32[16,24,128]{2,1,0:T(8,128)S(1)} all-to-all(f32[16,24,128]{2,1,0:T(8,128)S(1)} %row_sum_0.1), channel_id=1, replica_groups=mesh['row_0'=8,'row_1'=4,'col_0'=8,'col_1'=2] {'col_0','col_1'}, dimensions={0} | all-to-all | bytes 393216 | tf_op jit(solution)/shard_map/all_to_all | solution.py:39
  118.8 4.1 %solve_0.1 = (f32[4,64,128]{2,1,0:T(8,128)S(1)}, f32[4,64,128]{2,1,0:T(8,128)S(1)}, f32[4,64,128]{2,1,0:T(8,128)S(1)}, f32[64,128]{1,0:T(8,128)S(1)}, f32[64,64]...) custom-call(s32[1]{0:T(128)} %bitcast.6.place_ref.refs_0_, ...), custom_call_target="tpu_custom_call" | custom-call | tf_op jit(solution)/shard_map/solve_0/pallas_call | solution.py:59
  122.9 1.1 product_1.1
  124.0 13.0 %all_to_all.59.got_ref = f32[16,24,128]{2,1,0:T(8,128)S(1)} all-to-all(f32[16,24,128]{2,1,0:T(8,128)S(1)} %product_1.1), channel_id=1, replica_groups=mesh['row_0'=8,'row_1'=4,'col_0'=8,'col_1'=2] {'col_0','col_1'}, dimensions={0} | all-to-all | bytes 393216 | tf_op jit(solution)/shard_map/all_to_all | solution.py:39
  137.0 18.5 %all_to_all.60.got_ref.refs_11_ = f32[32,24,128]{2,1,0:T(8,128)S(1)} all-to-all(f32[32,24,128]{2,1,0:T(8,128)S(1)} %get-tuple-element.54), channel_id=1, replica_groups=mesh['row_0'=8,'row_1'=4,'col_0'=8,'col_1'=2] {'row_0','row_1'}, dimensions={0} | all-to-all | bytes 786432 | tf_op jit(solution)/shard_map/all_to_all | solution.py:39
  155.6 14.5 %all_to_all.61.refs_2_ = f32[16,24,128]{2,1,0:T(8,128)S(1)} all-to-all(f32[16,24,128]{2,1,0:T(8,128)S(1)} %row_sum_1.1), channel_id=1, replica_groups=mesh['row_0'=8,'row_1'=4,'col_0'=8,'col_1'=2] {'col_0','col_1'}, dimensions={0} | all-to-all | bytes 393216 | tf_op jit(solution)/shard_map/all_to_all | solution.py:39
  170.0 5.1 %solve_1.1 = (f32[4,64,128]{2,1,0:T(8,128)S(1)}, f32[4,64,128]{2,1,0:T(8,128)S(1)}, f32[4,64,128]{2,1,0:T(8,128)S(1)}, f32[64,128]{1,0:T(8,128)S(1)}, f32[64,64]...) custom-call(s32[1]{0:T(128)} %bitcast.6.place_ref.refs_0_, ...), custom_call_target="tpu_custom_call" | custom-call | tf_op jit(solution)/shard_map/solve_1/pallas_call | solution.py:59
  175.1 1.1 product_2.1
  176.2 12.8 %all_to_all.62.got_ref = f32[16,24,128]{2,1,0:T(8,128)S(1)} all-to-all(f32[16,24,128]{2,1,0:T(8,128)S(1)} %product_2.1), channel_id=1, replica_groups=mesh['row_0'=8,'row_1'=4,'col_0'=8,'col_1'=2] {'col_0','col_1'}, dimensions={0} | all-to-all | bytes 393216 | tf_op jit(solution)/shard_map/all_to_all | solution.py:39
  189.1 13.7 %all_to_all.63.got_ref = f32[32,8,128]{2,1,0:T(8,128)S(1)} all-to-all(f32[32,8,128]{2,1,0:T(8,128)S(1)} %get-tuple-element.65), channel_id=1, replica_groups=mesh['row_0'=8,'row_1'=4,'col_0'=8,'col_1'=2] {'row_0','row_1'}, dimensions={0} | all-to-all | bytes 262144 | tf_op jit(solution)/shard_map/all_to_all | solution.py:39
  202.8 14.2 %all_to_all.64.refs_2_ = f32[16,24,128]{2,1,0:T(8,128)S(1)} all-to-all(f32[16,24,128]{2,1,0:T(8,128)S(1)} %row_sum_2.1), channel_id=1, replica_groups=mesh['row_0'=8,'row_1'=4,'col_0'=8,'col_1'=2] {'col_0','col_1'}, dimensions={0} | all-to-all | bytes 393216 | tf_op jit(solution)/shard_map/all_to_all | solution.py:39
  217.0 4.1 %solve_2.1 = (f32[32,64]{1,0:T(8,128)}, f32[32,64]{1,0:T(8,128)}) custom-call(s32[1]{0:T(128)} %bitcast.6.place_ref.refs_0_, s32[1]{0:T(128)} %bitcast.7.refs_1_, f32[16,24,128]{2,1,0:T(8,128)S(1)} %all_to_all.64.refs_2_, f32[4,64,128]{2,1,0:T(8,128)S(1)} %get-tuple-element.61.refs_3_, f32[4,8,128]{2,1,0:T(8,128)S(1)} %get-tuple-element.44.refs_4_, ...), custom_call_target="tpu_custom_call" | custom-call | tf_op jit(solution)/shard_map/solve_2/pallas_call | solution.py:59
  (7 shorter events, 0.3 us)
Async XLA Ops:
  48.4 22.7 %all-to-all-start.1 = ((f32[32,16,128]{2,1,0:T(8,128)}), f32[32,16,128]{2,1,0:T(8,128)}, u32[]{:S(2)}, u32[]{:S(2)}) async-start(f32[32,16,128]{2,1,0:T(8,128)} %get-tuple-element.40), calls=%async_computation.1 | async-start | bytes 524288 | tf_op jit(solution)/shard_map/all_to_all | solution.py:39

commit v8 on v7

--- a/solution.py
+++ b/solution.py
@@ -156,7 +156,7 @@
     return jnp.concatenate([field_ref[b] for b in range(BLKS)], axis=1)
 
 
-def product_kernel(first, *refs):
+def product_kernel(first, last, *refs):
     spread_ref, high_ref, low_ref, res_ref, reg_ref = refs[:5]
     if first:
         (out_ref,) = refs[5:]
@@ -193,10 +193,16 @@
         right = jnp.concatenate([flat(img_ref) * share, flat(dir_ref)], axis=1)
         mixed = exact_dot(left, right, NT)
     other = jnp.concatenate([mixed, jnp.zeros((SMP, LANE - SMP), F32)], axis=1)
-    tall = pixel_rows(coupled)
+    tall = [field.T for field in coupled] if last else pixel_rows(coupled)
     for k in range(COLS):
-        for b in range(2):
-            out_ref[k, STRIP * b : STRIP * b + STRIP, :] = tall[b][STRIP * k : STRIP * k + STRIP]
+        if last:
+            m = PIECE * (k % 4)
+            near, far = tall[k // 4][m : m + 16], tall[k // 4][m + 16 : m + 32]
+            out_ref[k, 0:OWN, :] = jnp.concatenate([near, far], axis=1)
+        else:
+            for b in range(2):
+                strip = tall[b][STRIP * k : STRIP * k + STRIP]
+                out_ref[k, STRIP * b : STRIP * b + STRIP, :] = strip
         source = pair if k < 8 else other
         n = k % 8
         out_ref[k, OWN : OWN + 8, :] = source[8 * n : 8 * n + 8, :]
@@ -218,15 +224,22 @@
             out_ref[r, OWN : OWN + 8, :] = gram
 
 
-def row_sum_kernel(got_ref, piece_ref, out_ref):
+def row_sum_kernel(last, got_ref, *refs):
     top = got_ref.shape[1] - 8
     total = got_ref[0, top:, :]
     for r in range(1, got_ref.shape[0]):
         total = total + got_ref[r, top:, :]
-    piece = piece_ref[...]
+    if last:
+        (out_ref,) = refs
+    else:
+        piece_ref, out_ref = refs
+        piece = piece_ref[...]
     for k in range(COLS):
-        out_ref[k, 0:OWN, :] = piece
-        out_ref[k, OWN : OWN + 8, :] = total
+        if last:
+            out_ref[k] = total
+        else:
+            out_ref[k, 0:OWN, :] = piece
+            out_ref[k, OWN : OWN + 8, :] = total
 
 
 def solve_systems(systems, width):
@@ -289,7 +302,7 @@
         dir_ref, img_ref, sol_ref, inv_ref, curv_ref = refs[:5]
         refs = refs[5:]
     if last:
-        out_sol_ref, out_res_ref, keep_ref = refs
+        piece_ref, out_sol_ref, out_res_ref = refs
     else:
         spread_ref, fresh_ref = refs[:2]
         refs = refs[2:]
@@ -297,11 +310,12 @@
             spread_img_ref = refs.pop(0)
         new_res_ref, new_dir_ref, new_img_ref, new_sol_ref = refs[:4]
         new_inv_ref, new_curv_ref, new_spread_ref, new_spread_img_ref, own_ref = refs[4:]
-    pair = jnp.concatenate([got_ref[k, OWN : OWN + 8, :] for k in range(8)], axis=0)
+    base = got_ref.shape[1] - 8
+    pair = jnp.concatenate([got_ref[k, base:, :] for k in range(8)], axis=0)
     gram = pltpu.roll(pair, SMP, 1)[:, 0:SMP]
     curv = pair[:, 0:SMP]
     if not first:
-        mixed = jnp.concatenate([got_ref[k, OWN : OWN + 8, :] for k in range(8, 16)], axis=0)
+        mixed = jnp.concatenate([got_ref[k, base:, :] for k in range(8, 16)], axis=0)
         mixed = mixed[:, 0:SMP]
         beta_t = exact_dot(gram, inv_ref[...], NN)
         curv = curv + exact_dot(mixed + exact_dot(beta_t, curv_ref[...], NN), beta_t, NT)
@@ -327,6 +341,22 @@
         new_spread_ref[...] = spread.reshape(sources, OWN, LANE)
         new_spread_img_ref[...] = spread_img.reshape(sources, OWN, LANE)
         own_ref[...] = new_spread_ref[row_ref[0]]
+    if last:
+        shift = (LANE - PIECE * (col_ref[0] % 4)) % LANE
+
+        def cut(rows):
+            return pltpu.roll(rows, shift, 1)[:, 0:PIECE].T
+
+        res = cut(res_ref[mine])
+        reg = cut(jnp.broadcast_to(reg_ref[mine][0:1, :], (SMP, LANE)))
+        piece = piece_ref[...]
+        halves = [piece[:, 0:SMP], pltpu.roll(piece, SMP, 1)[:, 0:SMP]]
+        image = jnp.concatenate(halves, axis=0) + reg * res
+        image = image + exact_dot(cut(img_ref[mine]), beta_t, NT)
+        direction = res + exact_dot(cut(dir_ref[mine]), beta_t, NT)
+        out_sol_ref[...] = cut(sol_ref[...]) + exact_dot(direction, alpha, NN)
+        out_res_ref[...] = res - exact_dot(image, alpha, NN)
+        return
     alpha_t = alpha.T
     wide = [
         jnp.concatenate(
@@ -334,46 +364,26 @@
         ).T
         for b in range(2)
     ]
-
-    def advance(image, res, pick):
-        direction = res
-        if not first:
-            image = image + exact_dot(beta_t, pick(img_ref), NN)
-            direction = direction + exact_dot(beta_t, pick(dir_ref), NN)
-        return res - exact_dot(alpha_t, image, NN), image, direction
-
-    if last:
-        for b in range(2):
-            keep_ref[b] = wide[b]
-        start = pl.multiple_of(SMP * (mine // 2), SMP)
-        res = res_ref[mine]
-        image = keep_ref[mine % 2, pl.ds(start, SMP), :] + reg_ref[mine][0:1, :] * res
-        new_res, _, direction = advance(image, res, lambda ref: ref[mine])
-    else:
-        image = jnp.concatenate(
-            [
-                wide[b % 2][SMP * (b // 2) : SMP * (b // 2) + SMP, :]
-                + reg_ref[b, 0:1, :] * res_ref[b]
-                for b in range(BLKS)
-            ],
-            axis=1,
-        )
-        new_res, image, direction = advance(image, flat(res_ref), flat)
-        for b in range(BLKS):
-            cut = slice(LANE * b, LANE * b + LANE)
-            new_res_ref[b] = new_res[:, cut]
-            new_img_ref[b] = image[:, cut]
-            new_dir_ref[b] = direction[:, cut]
-        direction = new_dir_ref[mine]
-    new_sol = exact_dot(alpha_t, direction, NN)
+    res = flat(res_ref)
+    direction = res
+    image = jnp.concatenate(
+        [
+            wide[b % 2][SMP * (b // 2) : SMP * (b // 2) + SMP, :] + reg_ref[b, 0:1, :] * res_ref[b]
+            for b in range(BLKS)
+        ],
+        axis=1,
+    )
     if not first:
-        new_sol = sol_ref[...] + new_sol
-    if last:
-        shift = (LANE - PIECE * (col_ref[0] % 4)) % LANE
-        out_sol_ref[...] = pltpu.roll(new_sol, shift, 1)[:, 0:PIECE].T
-        out_res_ref[...] = pltpu.roll(new_res, shift, 1)[:, 0:PIECE].T
-    else:
-        new_sol_ref[...] = new_sol
+        image = image + exact_dot(beta_t, flat(img_ref), NN)
+        direction = direction + exact_dot(beta_t, flat(dir_ref), NN)
+    new_res = res - exact_dot(alpha_t, image, NN)
+    for b in range(BLKS):
+        part = slice(LANE * b, LANE * b + LANE)
+        new_res_ref[b] = new_res[:, part]
+        new_img_ref[b] = image[:, part]
+        new_dir_ref[b] = direction[:, part]
+    new_sol = exact_dot(alpha_t, new_dir_ref[mine], NN)
+    new_sol_ref[...] = new_sol if first else sol_ref[...] + new_sol
 
 
 def body(right_side, regular, curvature, block_rows, block_cols, block_counts):
@@ -417,7 +427,7 @@
         first, last = step == 0, step == ITERS - 1
         before = [] if first else [state[1], state[0]]
         (part,) = call(
-            functools.partial(product_kernel, first),
+            functools.partial(product_kernel, first, last),
             [VMEM] * (5 + len(before)),
             [msg],
             [],
@@ -431,20 +441,26 @@
             f"col_sum_{step}",
         )(swap(part, COL), own, own_reg)
         fresh = swap(out, ROW)
-        (whole,) = call(row_sum_kernel, [VMEM] * 2, [msg], [], f"row_sum_{step}")(fresh, piece)
+        pieces = [] if last else [piece]
+        (whole,) = call(
+            functools.partial(row_sum_kernel, last),
+            [VMEM] * (1 + len(pieces)),
+            [((COLS, 8, LANE), F32) if last else msg],
+            [],
+            f"row_sum_{step}",
+        )(fresh, *pieces)
         got = swap(whole, COL)
         solve = functools.partial(solve_kernel, first, last)
         if last:
             share = ((PIECE, SMP), F32)
-            keep = pltpu.VMEM((2, LANE, LANE), F32)
             shares = call(
                 solve,
-                [SMEM] * 2 + [VMEM] * (3 + len(state)),
+                [SMEM] * 2 + [VMEM] * (4 + len(state)),
                 [share, share],
-                [keep],
+                [],
                 f"solve_{step}",
                 jax.ShapeDtypeStruct,
-            )(col_here, row_here, got, res, reg, *state)
+            )(col_here, row_here, got, res, reg, *state, piece)
             return tuple(part.T for part in shares)
         inputs = [got, res, reg, *state, spread, fresh, *spread_img]
         outs = [field] * 3 + [((SMP, LANE), F32)] + [small] * 2 + [spread_share] * 2 + [own_share]

time: 222 us -> 219 us (0.986)
    all_to_all x10, blocking collectives: 177 us -> 175 us  [swap(): return lax.all_to_all(msg, axes, 0, 0, tiled=True)]
where the time goes in v8:
time: 219 us; the launch traced here: 218 us
  blocking collectives  175 us (80%)
  Pallas kernels  23.9 us (11%)
  starting transfers between devices  9.8 us (4%)
  waiting for transfers between devices  9.08 us (4%)
    all_to_all x10, blocking collectives, swap(): return lax.all_to_all(msg, axes, 0, 0, tiled=True)  175 us
    pallas_call x15, Pallas kernels, placed(): return run(*args)  23.9 us
    all_to_all x1, starting transfers between devices, swap(): return lax.all_to_all(msg, axes, 0, 0, tiled=True)  9.8 us
    all_to_all x1, waiting for transfers between devices, swap(): return lax.all_to_all(msg, axes, 0, 0, tiled=True)  9.08 us
  transfers between devices with their start and end apart: 1, of which 1 were waited for; matrix products, arithmetic and copies ran while one was open for 0% of the time, Pallas kernels for 2%

profile of v8, /device:TPU:1, one launch (start us, length us, event | category | flops | bytes accessed | tf_op | source)
XLA Modules:
  0.0 218.5 jit_solution(3715610187462821080)
XLA Ops:
  0.6 1.7 pack.1
  2.4 45.0 %all_to_all.55.got_ref = bf16[16,312,128]{2,1,0:T(8,128)(2,1)S(1)} all-to-all(bf16[16,312,128]{2,1,0:T(8,128)(2,1)S(1)} %pack.1), channel_id=1, replica_groups=mesh['row_0'=8,'row_1'=4,'col_0'=8,'col_1'=2] {'col_0','col_1'}, dimensions={0} | all-to-all | bytes 2555904 | tf_op jit(solution)/shard_map/all_to_all | solution.py:39
  47.3 1.1 unpack.1
  48.4 9.8 %all-to-all-start.1 = ((f32[32,16,128]{2,1,0:T(8,128)}), f32[32,16,128]{2,1,0:T(8,128)}, u32[]{:S(2)}, u32[]{:S(2)}) async-start(f32[32,16,128]{2,1,0:T(8,128)} %get-tuple-element.40), calls=%async_computation.1 | async-start | bytes 524288 | tf_op jit(solution)/shard_map/all_to_all | solution.py:39
  58.3 3.8 %dense.1 = (bf16[8,512,128]{2,1,0:T(8,128)(2,1)S(1)}, bf16[8,512,128]{2,1,0:T(8,128)(2,1)S(1)}) custom-call(s32[16,32]{1,0:T(8,128)S(1)} %bitcast.11, bf16[16,312,128]{2,1,0:T(8,128)(2,1)S(1)} %all_to_all.55.got_ref), custom_call_target="tpu_custom_call" | custom-call | tf_op jit(solution)/shard_map/dense/pallas_call | solution.py:59
  62.1 9.1 %all-to-all-done.1.refs_0_.refs_5_ = f32[32,16,128]{2,1,0:T(8,128)} async-done(((f32[32,16,128]{2,1,0:T(8,128)}), f32[32,16,128]{2,1,0:T(8,128)}, u32[]{:S(2)}, u32[]{:S(2)}) %all-to-all-start.1) | async-done | bytes 262176 | tf_op jit(solution)/shard_map/all_to_all | solution.py:39
  71.1 1.8 product_0.1
  72.9 13.6 %all_to_all.56.got_ref = f32[16,24,128]{2,1,0:T(8,128)S(1)} all-to-all(f32[16,24,128]{2,1,0:T(8,128)S(1)} %product_0.1), channel_id=1, replica_groups=mesh['row_0'=8,'row_1'=4,'col_0'=8,'col_1'=2] {'col_0','col_1'}, dimensions={0} | all-to-all | bytes 393216 | tf_op jit(solution)/shard_map/all_to_all | solution.py:39
  86.5 18.1 %all_to_all.57.got_ref.refs_6_ = f32[32,24,128]{2,1,0:T(8,128)S(1)} all-to-all(f32[32,24,128]{2,1,0:T(8,128)S(1)} %get-tuple-element.47), channel_id=1, replica_groups=mesh['row_0'=8,'row_1'=4,'col_0'=8,'col_1'=2] {'row_0','row_1'}, dimensions={0} | all-to-all | bytes 786432 | tf_op jit(solution)/shard_map/all_to_all | solution.py:39
  104.7 14.1 %all_to_all.58.refs_2_ = f32[16,24,128]{2,1,0:T(8,128)S(1)} all-to-all(f32[16,24,128]{2,1,0:T(8,128)S(1)} %row_sum_0.1), channel_id=1, replica_groups=mesh['row_0'=8,'row_1'=4,'col_0'=8,'col_1'=2] {'col_0','col_1'}, dimensions={0} | all-to-all | bytes 393216 | tf_op jit(solution)/shard_map/all_to_all | solution.py:39
  118.8 4.1 %solve_0.1 = (f32[4,64,128]{2,1,0:T(8,128)S(1)}, f32[4,64,128]{2,1,0:T(8,128)S(1)}, f32[4,64,128]{2,1,0:T(8,128)S(1)}, f32[64,128]{1,0:T(8,128)S(1)}, f32[64,64]...) custom-call(s32[1]{0:T(128)} %bitcast.6.place_ref.refs_0_, ...), custom_call_target="tpu_custom_call" | custom-call | tf_op jit(solution)/shard_map/solve_0/pallas_call | solution.py:59
  122.9 1.1 product_1.1
  124.0 13.0 %all_to_all.59.got_ref = f32[16,24,128]{2,1,0:T(8,128)S(1)} all-to-all(f32[16,24,128]{2,1,0:T(8,128)S(1)} %product_1.1), channel_id=1, replica_groups=mesh['row_0'=8,'row_1'=4,'col_0'=8,'col_1'=2] {'col_0','col_1'}, dimensions={0} | all-to-all | bytes 393216 | tf_op jit(solution)/shard_map/all_to_all | solution.py:39
  137.0 18.5 %all_to_all.60.got_ref.refs_11_ = f32[32,24,128]{2,1,0:T(8,128)S(1)} all-to-all(f32[32,24,128]{2,1,0:T(8,128)S(1)} %get-tuple-element.54), channel_id=1, replica_groups=mesh['row_0'=8,'row_1'=4,'col_0'=8,'col_1'=2] {'row_0','row_1'}, dimensions={0} | all-to-all | bytes 786432 | tf_op jit(solution)/shard_map/all_to_all | solution.py:39
  155.6 14.5 %all_to_all.61.refs_2_ = f32[16,24,128]{2,1,0:T(8,128)S(1)} all-to-all(f32[16,24,128]{2,1,0:T(8,128)S(1)} %row_sum_1.1), channel_id=1, replica_groups=mesh['row_0'=8,'row_1'=4,'col_0'=8,'col_1'=2] {'col_0','col_1'}, dimensions={0} | all-to-all | bytes 393216 | tf_op jit(solution)/shard_map/all_to_all | solution.py:39
  170.0 5.1 %solve_1.1 = (f32[4,64,128]{2,1,0:T(8,128)S(1)}, f32[4,64,128]{2,1,0:T(8,128)S(1)}, f32[4,64,128]{2,1,0:T(8,128)S(1)}, f32[64,128]{1,0:T(8,128)S(1)}, f32[64,64]...) custom-call(s32[1]{0:T(128)} %bitcast.6.place_ref.refs_0_, ...), custom_call_target="tpu_custom_call" | custom-call | tf_op jit(solution)/shard_map/solve_1/pallas_call | solution.py:59
  175.1 1.1 product_2.1
  176.2 12.8 %all_to_all.62.got_ref = f32[16,24,128]{2,1,0:T(8,128)S(1)} all-to-all(f32[16,24,128]{2,1,0:T(8,128)S(1)} %product_2.1), channel_id=1, replica_groups=mesh['row_0'=8,'row_1'=4,'col_0'=8,'col_1'=2] {'col_0','col_1'}, dimensions={0} | all-to-all | bytes 393216 | tf_op jit(solution)/shard_map/all_to_all | solution.py:39
  189.1 13.7 %all_to_all.63.got_ref = f32[32,8,128]{2,1,0:T(8,128)S(1)} all-to-all(f32[32,8,128]{2,1,0:T(8,128)S(1)} %get-tuple-element.65), channel_id=1, replica_groups=mesh['row_0'=8,'row_1'=4,'col_0'=8,'col_1'=2] {'row_0','row_1'}, dimensions={0} | all-to-all | bytes 262144 | tf_op jit(solution)/shard_map/all_to_all | solution.py:39
  202.8 11.8 %all_to_all.64.refs_2_ = f32[16,8,128]{2,1,0:T(8,128)S(1)} all-to-all(f32[16,8,128]{2,1,0:T(8,128)S(1)} %row_sum_2.1), channel_id=1, replica_groups=mesh['row_0'=8,'row_1'=4,'col_0'=8,'col_1'=2] {'col_0','col_1'}, dimensions={0} | all-to-all | bytes 131072 | tf_op jit(solution)/shard_map/all_to_all | solution.py:39
  214.6 3.9 %solve_2.1 = (f32[32,64]{1,0:T(8,128)}, f32[32,64]{1,0:T(8,128)}) custom-call(s32[1]{0:T(128)} %bitcast.6.place_ref.refs_0_, s32[1]{0:T(128)} %bitcast.7.refs_1_, f32[16,8,128]{2,1,0:T(8,128)S(1)} %all_to_all.64.refs_2_, f32[4,64,128]{2,1,0:T(8,128)S(1)} %get-tuple-element.61.refs_3_, f32[4,8,128]{2,1,0:T(8,128)S(1)} %get-tuple-element.44.refs_4_, ...), custom_call_target="tpu_custom_call" | custom-call | tf_op jit(solution)/shard_map/solve_2/pallas_call | solution.py:59
  (7 shorter events, 0.2 us)
Async XLA Ops:
  48.4 22.7 %all-to-all-start.1 = ((f32[32,16,128]{2,1,0:T(8,128)}), f32[32,16,128]{2,1,0:T(8,128)}, u32[]{:S(2)}, u32[]{:S(2)}) async-start(f32[32,16,128]{2,1,0:T(8,128)} %get-tuple-element.40), calls=%async_computation.1 | async-start | bytes 524288 | tf_op jit(solution)/shard_map/all_to_all | solution.py:39

commit v9 on v8

--- a/solution.py
+++ b/solution.py
@@ -33,6 +33,19 @@
     return lax.dot_general(
         left, right, dims, precision=lax.Precision.HIGHEST, preferred_element_type=F32
     )
+
+
+def close_dot(left, right):
+    heads = [side.astype(BF16) for side in (left, right)]
+    tails = [
+        (side - head.astype(F32)).astype(BF16)
+        for side, head in zip((left, right), heads, strict=True)
+    ]
+
+    def dot(a, b):
+        return lax.dot_general(a, b, NN, preferred_element_type=F32)
+
+    return dot(heads[0], heads[1]) + (dot(tails[0], heads[1]) + dot(heads[0], tails[1]))
 
 
 def swap(msg, axes):
@@ -94,7 +107,29 @@
     return [jnp.concatenate([fields[b].T, fields[2 + b].T], axis=1) for b in range(2)]
 
 
-def unpack_kernel(place_ref, got_ref, res_ref, reg_ref, own_ref, own_reg_ref, out_ref, tall_ref):
+def own_kernel(place_ref, got_ref, own_ref, out_ref, tall_ref):
+    base = got_ref.shape[1] - NOTES
+    place = place_ref[0]
+    strips = []
+    for b in range(BLKS):
+        parts = [
+            got_ref[BLKS * b + place // 4, base + 16 * i : base + 16 * i + 16, :].astype(F32)
+            for i in range(3)
+        ]
+        tall_ref[b] = (parts[0] + parts[1] + parts[2]).T
+        start = STRIP * (place % 4)
+        pieces = [
+            tall_ref[b, pl.ds(pl.multiple_of(PIECE * j + start, STRIP), STRIP), :] for j in range(4)
+        ]
+        strips.append(jnp.concatenate(pieces, axis=1))
+    for b in range(2):
+        tile = jnp.concatenate([strips[b], strips[2 + b]], axis=1)
+        own_ref[STRIP * b : STRIP * b + STRIP, :] = tile
+        for r in range(out_ref.shape[0]):
+            out_ref[r, STRIP * b : STRIP * b + STRIP, :] = tile
+
+
+def unpack_kernel(place_ref, got_ref, res_ref, reg_ref, own_reg_ref, tall_ref):
     base = got_ref.shape[1] - NOTES
     packed, notes = [], []
     for k in range(COLS):
@@ -124,13 +159,9 @@
         res_ref[b] = fields[b]
         reg_ref[b] = reg
     start = pl.multiple_of(place_ref[0] * STRIP, STRIP)
-    for target, values in ((own_ref, fields), (own_reg_ref, regs)):
-        for b, tall in enumerate(pixel_rows(values)):
-            tall_ref[b] = tall
-            target[STRIP * b : STRIP * b + STRIP, :] = tall_ref[b, pl.ds(start, STRIP), :]
-    own = own_ref[...]
-    for r in range(out_ref.shape[0]):
-        out_ref[r] = own
+    for b, tall in enumerate(pixel_rows(regs)):
+        tall_ref[b] = tall
+        own_reg_ref[STRIP * b : STRIP * b + STRIP, :] = tall_ref[b, pl.ds(start, STRIP), :]
 
 
 def dense_kernel(place_ref, got_ref, high_ref, low_ref, sum_ref):
@@ -299,8 +330,8 @@
     refs = refs[5:]
     mine = col_ref[0] // 4
     if not first:
-        dir_ref, img_ref, sol_ref, inv_ref, curv_ref = refs[:5]
-        refs = refs[5:]
+        dir_ref, img_ref, sol_ref, lead_ref = refs[:4]
+        refs = refs[4:]
     if last:
         piece_ref, out_sol_ref, out_res_ref = refs
     else:
@@ -309,7 +340,7 @@
         if not first:
             spread_img_ref = refs.pop(0)
         new_res_ref, new_dir_ref, new_img_ref, new_sol_ref = refs[:4]
-        new_inv_ref, new_curv_ref, new_spread_ref, new_spread_img_ref, own_ref = refs[4:]
+        new_lead_ref, new_spread_ref, new_spread_img_ref, own_ref = refs[4:]
     base = got_ref.shape[1] - 8
     pair = jnp.concatenate([got_ref[k, base:, :] for k in range(8)], axis=0)
     gram = pltpu.roll(pair, SMP, 1)[:, 0:SMP]
@@ -317,8 +348,9 @@
     if not first:
         mixed = jnp.concatenate([got_ref[k, base:, :] for k in range(8, 16)], axis=0)
         mixed = mixed[:, 0:SMP]
-        beta_t = exact_dot(gram, inv_ref[...], NN)
-        curv = curv + exact_dot(mixed + exact_dot(beta_t, curv_ref[...], NN), beta_t, NT)
+        both = exact_dot(gram, lead_ref[...], NN)
+        beta_t = both[:, 0:SMP]
+        curv = curv + exact_dot(mixed + pltpu.roll(both, SMP, 1)[:, 0:SMP], beta_t, NT)
     curv = 0.5 * (curv + curv.T)
     if last:
         (alpha,) = solve_systems([(curv, gram)], 8)
@@ -328,16 +360,15 @@
             jnp.int32, square, 1
         )
         alpha, inverse = solve_systems([(curv, gram), (gram, same.astype(F32))], 8)
-        new_inv_ref[...] = inverse
-        new_curv_ref[...] = curv
+        new_lead_ref[...] = jnp.concatenate([inverse, exact_dot(inverse, curv, NN)], axis=1)
         sources = spread_ref.shape[0]
         pixels = OWN * sources
         spread_img = fresh_ref[:, 0:OWN, :].reshape(pixels, LANE)
         if not first:
             old = spread_img_ref[...].reshape(pixels, LANE)
-            spread_img = spread_img + exact_dot(old, both_halves(beta_t.T), NN)
+            spread_img = spread_img + close_dot(old, both_halves(beta_t.T))
         spread = spread_ref[...].reshape(pixels, LANE)
-        spread = spread - exact_dot(spread_img, both_halves(alpha), NN)
+        spread = spread - close_dot(spread_img, both_halves(alpha))
         new_spread_ref[...] = spread.reshape(sources, OWN, LANE)
         new_spread_img_ref[...] = spread_img.reshape(sources, OWN, LANE)
         own_ref[...] = new_spread_ref[row_ref[0]]
@@ -392,7 +423,6 @@
     curv = curvature.reshape(sources, LANE, LANE)
     tables = [table.reshape(1, sources) for table in (block_rows, block_cols, block_counts)]
     field = ((BLKS, SMP, LANE), F32)
-    small = ((SMP, SMP), F32)
     own_share = ((OWN, LANE), F32)
     spread_share = ((sources, OWN, LANE), F32)
     msg = ((COLS, OWN + 8, LANE), F32)
@@ -406,10 +436,17 @@
     row_here = lax.axis_index(ROW).astype(jnp.int32).reshape(1)
     packed, col_here, row_here = lax.optimization_barrier((packed, col_here, row_here))
     packed = swap(packed, COL)
-    res, reg, own, own_reg, out = call(
+    own, out = call(
+        own_kernel,
+        [SMEM, VMEM],
+        [own_share, spread_share],
+        [pltpu.VMEM((BLKS, LANE, 16), F32)],
+        "own",
+    )(col_here, packed)
+    res, reg, own_reg = call(
         unpack_kernel,
         [SMEM, VMEM],
-        [field, ((BLKS, 8, LANE), F32), own_share, own_share, spread_share],
+        [field, ((BLKS, 8, LANE), F32), own_share],
         [pltpu.VMEM((2, LANE, LANE), F32)],
         "unpack",
     )(col_here, packed)
@@ -463,7 +500,7 @@
             )(col_here, row_here, got, res, reg, *state, piece)
             return tuple(part.T for part in shares)
         inputs = [got, res, reg, *state, spread, fresh, *spread_img]
-        outs = [field] * 3 + [((SMP, LANE), F32)] + [small] * 2 + [spread_share] * 2 + [own_share]
+        outs = [field] * 3 + [((SMP, LANE), F32)] * 2 + [spread_share] * 2 + [own_share]
         res, *state, spread, img, own = call(
             solve, [SMEM] * 2 + [VMEM] * len(inputs), outs, [], f"solve_{step}"
         )(col_here, row_here, *inputs)

time: 219 us -> 219 us (level)
    pallas_call x15 -> x16, Pallas kernels: 23.9 us -> 24.5 us  [placed(): return run(*args)]
where the time goes in v9:
time: 219 us
  blocking collectives  175 us (80%)
  Pallas kernels  24.5 us (11%)
  starting transfers between devices  9.8 us (4%)
  waiting for transfers between devices  8.72 us (4%)
    all_to_all x10, blocking collectives, swap(): return lax.all_to_all(msg, axes, 0, 0, tiled=True)  175 us
    pallas_call x16, Pallas kernels, placed(): return run(*args)  24.5 us
    all_to_all x1, starting transfers between devices, swap(): return lax.all_to_all(msg, axes, 0, 0, tiled=True)  9.8 us
    all_to_all x1, waiting for transfers between devices, swap(): return lax.all_to_all(msg, axes, 0, 0, tiled=True)  8.72 us
  transfers between devices with their start and end apart: 1, of which 1 were waited for; matrix products, arithmetic and copies ran while one was open for 0% of the time, Pallas kernels for 2%

profile of v9, /device:TPU:1, one launch (start us, length us, event | category | flops | bytes accessed | tf_op | source)
XLA Modules:
  0.0 218.7 jit_solution(6940824284722547963)
XLA Ops:
  0.6 1.7 pack.1
  2.4 45.0 %all_to_all.55.got_ref = bf16[16,312,128]{2,1,0:T(8,128)(2,1)S(1)} all-to-all(bf16[16,312,128]{2,1,0:T(8,128)(2,1)S(1)} %pack.1), channel_id=1, replica_groups=mesh['row_0'=8,'row_1'=4,'col_0'=8,'col_1'=2] {'col_0','col_1'}, dimensions={0} | all-to-all | bytes 2555904 | tf_op jit(solution)/shard_map/all_to_all | solution.py:52
  47.3 1.0 own.1
  48.3 9.8 %all-to-all-start.1 = ((f32[32,16,128]{2,1,0:T(8,128)}), f32[32,16,128]{2,1,0:T(8,128)}, u32[]{:S(2)}, u32[]{:S(2)}) async-start(f32[32,16,128]{2,1,0:T(8,128)} %get-tuple-element.38), calls=%async_computation.1 | async-start | bytes 524288 | tf_op jit(solution)/shard_map/all_to_all | solution.py:52
  58.1 0.4 unpack.1
  58.5 3.8 %dense.1 = (bf16[8,512,128]{2,1,0:T(8,128)(2,1)S(1)}, bf16[8,512,128]{2,1,0:T(8,128)(2,1)S(1)}) custom-call(s32[16,32]{1,0:T(8,128)S(1)} %bitcast.11, bf16[16,312,128]{2,1,0:T(8,128)(2,1)S(1)} %all_to_all.55.got_ref), custom_call_target="tpu_custom_call" | custom-call | tf_op jit(solution)/shard_map/dense/pallas_call | solution.py:72
  62.3 8.7 %all-to-all-done.1.refs_0_.refs_5_ = f32[32,16,128]{2,1,0:T(8,128)} async-done(((f32[32,16,128]{2,1,0:T(8,128)}), f32[32,16,128]{2,1,0:T(8,128)}, u32[]{:S(2)}, u32[]{:S(2)}) %all-to-all-start.1) | async-done | bytes 262176 | tf_op jit(solution)/shard_map/all_to_all | solution.py:52
  71.0 1.8 product_0.1
  72.8 13.6 %all_to_all.56.got_ref = f32[16,24,128]{2,1,0:T(8,128)S(1)} all-to-all(f32[16,24,128]{2,1,0:T(8,128)S(1)} %product_0.1), channel_id=1, replica_groups=mesh['row_0'=8,'row_1'=4,'col_0'=8,'col_1'=2] {'col_0','col_1'}, dimensions={0} | all-to-all | bytes 393216 | tf_op jit(solution)/shard_map/all_to_all | solution.py:52
  86.4 18.1 %all_to_all.57.got_ref.refs_6_ = f32[32,24,128]{2,1,0:T(8,128)S(1)} all-to-all(f32[32,24,128]{2,1,0:T(8,128)S(1)} %get-tuple-element.45), channel_id=1, replica_groups=mesh['row_0'=8,'row_1'=4,'col_0'=8,'col_1'=2] {'row_0','row_1'}, dimensions={0} | all-to-all | bytes 786432 | tf_op jit(solution)/shard_map/all_to_all | solution.py:52
  104.6 14.1 %all_to_all.58.refs_2_ = f32[16,24,128]{2,1,0:T(8,128)S(1)} all-to-all(f32[16,24,128]{2,1,0:T(8,128)S(1)} %row_sum_0.1), channel_id=1, replica_groups=mesh['row_0'=8,'row_1'=4,'col_0'=8,'col_1'=2] {'col_0','col_1'}, dimensions={0} | all-to-all | bytes 393216 | tf_op jit(solution)/shard_map/all_to_all | solution.py:52
  118.7 4.2 %solve_0.1 = (f32[4,64,128]{2,1,0:T(8,128)S(1)}, f32[4,64,128]{2,1,0:T(8,128)S(1)}, f32[4,64,128]{2,1,0:T(8,128)S(1)}, f32[64,128]{1,0:T(8,128)S(1)}, f32[64,128...) custom-call(s32[1]{0:T(128)} %bitcast.6.place_ref.refs_0_, ...), custom_call_target="tpu_custom_call" | custom-call | tf_op jit(solution)/shard_map/solve_0/pallas_call | solution.py:72
  122.9 1.1 product_1.1
  124.0 13.0 %all_to_all.59.got_ref = f32[16,24,128]{2,1,0:T(8,128)S(1)} all-to-all(f32[16,24,128]{2,1,0:T(8,128)S(1)} %product_1.1), channel_id=1, replica_groups=mesh['row_0'=8,'row_1'=4,'col_0'=8,'col_1'=2] {'col_0','col_1'}, dimensions={0} | all-to-all | bytes 393216 | tf_op jit(solution)/shard_map/all_to_all | solution.py:52
  137.0 18.5 %all_to_all.60.got_ref.refs_10_ = f32[32,24,128]{2,1,0:T(8,128)S(1)} all-to-all(f32[32,24,128]{2,1,0:T(8,128)S(1)} %get-tuple-element.52), channel_id=1, replica_groups=mesh['row_0'=8,'row_1'=4,'col_0'=8,'col_1'=2] {'row_0','row_1'}, dimensions={0} | all-to-all | bytes 786432 | tf_op jit(solution)/shard_map/all_to_all | solution.py:52
  155.6 14.5 %all_to_all.61.refs_2_ = f32[16,24,128]{2,1,0:T(8,128)S(1)} all-to-all(f32[16,24,128]{2,1,0:T(8,128)S(1)} %row_sum_1.1), channel_id=1, replica_groups=mesh['row_0'=8,'row_1'=4,'col_0'=8,'col_1'=2] {'col_0','col_1'}, dimensions={0} | all-to-all | bytes 393216 | tf_op jit(solution)/shard_map/all_to_all | solution.py:52
  170.0 5.3 %solve_1.1 = (f32[4,64,128]{2,1,0:T(8,128)S(1)}, f32[4,64,128]{2,1,0:T(8,128)S(1)}, f32[4,64,128]{2,1,0:T(8,128)S(1)}, f32[64,128]{1,0:T(8,128)S(1)}, f32[64,128...) custom-call(s32[1]{0:T(128)} %bitcast.6.place_ref.refs_0_, ...), custom_call_target="tpu_custom_call" | custom-call | tf_op jit(solution)/shard_map/solve_1/pallas_call | solution.py:72
  175.4 1.1 product_2.1
  176.5 12.8 %all_to_all.62.got_ref = f32[16,24,128]{2,1,0:T(8,128)S(1)} all-to-all(f32[16,24,128]{2,1,0:T(8,128)S(1)} %product_2.1), channel_id=1, replica_groups=mesh['row_0'=8,'row_1'=4,'col_0'=8,'col_1'=2] {'col_0','col_1'}, dimensions={0} | all-to-all | bytes 393216 | tf_op jit(solution)/shard_map/all_to_all | solution.py:52
  189.3 13.7 %all_to_all.63.got_ref = f32[32,8,128]{2,1,0:T(8,128)S(1)} all-to-all(f32[32,8,128]{2,1,0:T(8,128)S(1)} %get-tuple-element.62), channel_id=1, replica_groups=mesh['row_0'=8,'row_1'=4,'col_0'=8,'col_1'=2] {'row_0','row_1'}, dimensions={0} | all-to-all | bytes 262144 | tf_op jit(solution)/shard_map/all_to_all | solution.py:52
  203.0 11.8 %all_to_all.64.refs_2_ = f32[16,8,128]{2,1,0:T(8,128)S(1)} all-to-all(f32[16,8,128]{2,1,0:T(8,128)S(1)} %row_sum_2.1), channel_id=1, replica_groups=mesh['row_0'=8,'row_1'=4,'col_0'=8,'col_1'=2] {'col_0','col_1'}, dimensions={0} | all-to-all | bytes 131072 | tf_op jit(solution)/shard_map/all_to_all | solution.py:52
  214.8 3.9 %solve_2.1 = (f32[32,64]{1,0:T(8,128)}, f32[32,64]{1,0:T(8,128)}) custom-call(s32[1]{0:T(128)} %bitcast.6.place_ref.refs_0_, s32[1]{0:T(128)} %bitcast.7.refs_1_, f32[16,8,128]{2,1,0:T(8,128)S(1)} %all_to_all.64.refs_2_, f32[4,64,128]{2,1,0:T(8,128)S(1)} %get-tuple-element.58.refs_3_, f32[4,8,128]{2,1,0:T(8,128)S(1)} %get-tuple-element.42.refs_4_, ...), custom_call_target="tpu_custom_call" | custom-call | tf_op jit(solution)/shard_map/solve_2/pallas_call | solution.py:72
  (7 shorter events, 0.2 us)
Async XLA Ops:
  48.3 22.7 %all-to-all-start.1 = ((f32[32,16,128]{2,1,0:T(8,128)}), f32[32,16,128]{2,1,0:T(8,128)}, u32[]{:S(2)}, u32[]{:S(2)}) async-start(f32[32,16,128]{2,1,0:T(8,128)} %get-tuple-element.38), calls=%async_computation.1 | async-start | bytes 524288 | tf_op jit(solution)/shard_map/all_to_all | solution.py:52

commit v10 on v9

--- a/solution.py
+++ b/solution.py
@@ -23,6 +23,7 @@
 OWN = 2 * STRIP
 GRANT = 16 * 2**20
 NOTES = 56
+BATCHES = 4
 NT = (((1,), (1,)), ((), ()))
 NN = (((1,), (0,)), ((), ()))
 VMEM = pl.BlockSpec(memory_space=pltpu.VMEM)
@@ -80,14 +81,7 @@
     return high, middle, value - high - middle
 
 
-def pack_kernel(right_ref, reg_ref, rows_ref, cols_ref, counts_ref, curv_ref, out_ref):
-    sources = curv_ref.shape[0]
-    base = STRIP * sources
-    for s in range(sources):
-        flipped = curv_ref[s].astype(F32).T
-        for k in range(COLS):
-            strip = flipped[STRIP * k : STRIP * k + STRIP, :].astype(BF16)
-            out_ref[k, STRIP * s : STRIP * s + STRIP, :] = strip
+def pack_share(right_ref, reg_ref, rows_ref, cols_ref, counts_ref, out_ref, base):
     right = right_ref[...].T
     packed = jnp.concatenate([right[16 * j : 16 * j + 16, :] for j in range(4)], axis=1)
     cols = cols_ref[...]
@@ -101,6 +95,27 @@
     for k in range(COLS):
         for i, tile in enumerate(tiles):
             out_ref[k, base + 16 * i : base + 16 * i + tile.shape[0], :] = tile
+
+
+def pack_kernel(
+    right_ref, reg_ref, rows_ref, cols_ref, counts_ref, far_ref, out_ref, curv_ref, done_ref
+):
+    sources = curv_ref.shape[0]
+    base = STRIP * sources
+    batch = sources // BATCHES
+    loads = []
+    for i in range(BATCHES):
+        part = pl.ds(batch * i, batch)
+        loads.append(pltpu.make_async_copy(far_ref.at[part], curv_ref.at[part], done_ref.at[i]))
+        loads[i].start()
+    pack_share(right_ref, reg_ref, rows_ref, cols_ref, counts_ref, out_ref, base)
+    for s in range(sources):
+        if s % batch == 0:
+            loads[s // batch].wait()
+        flipped = curv_ref[s].astype(F32).T
+        for k in range(COLS):
+            strip = flipped[STRIP * k : STRIP * k + STRIP, :].astype(BF16)
+            out_ref[k, STRIP * s : STRIP * s + STRIP, :] = strip
 
 
 def pixel_rows(fields):
@@ -330,8 +345,8 @@
     refs = refs[5:]
     mine = col_ref[0] // 4
     if not first:
-        dir_ref, img_ref, sol_ref, lead_ref = refs[:4]
-        refs = refs[4:]
+        dir_ref, img_ref, sol_ref, inv_ref, curv_ref = refs[:5]
+        refs = refs[5:]
     if last:
         piece_ref, out_sol_ref, out_res_ref = refs
     else:
@@ -340,7 +355,7 @@
         if not first:
             spread_img_ref = refs.pop(0)
         new_res_ref, new_dir_ref, new_img_ref, new_sol_ref = refs[:4]
-        new_lead_ref, new_spread_ref, new_spread_img_ref, own_ref = refs[4:]
+        new_inv_ref, new_curv_ref, new_spread_ref, new_spread_img_ref, own_ref = refs[4:]
     base = got_ref.shape[1] - 8
     pair = jnp.concatenate([got_ref[k, base:, :] for k in range(8)], axis=0)
     gram = pltpu.roll(pair, SMP, 1)[:, 0:SMP]
@@ -348,9 +363,8 @@
     if not first:
         mixed = jnp.concatenate([got_ref[k, base:, :] for k in range(8, 16)], axis=0)
         mixed = mixed[:, 0:SMP]
-        both = exact_dot(gram, lead_ref[...], NN)
-        beta_t = both[:, 0:SMP]
-        curv = curv + exact_dot(mixed + pltpu.roll(both, SMP, 1)[:, 0:SMP], beta_t, NT)
+        beta_t = exact_dot(gram, inv_ref[...], NN)
+        curv = curv + exact_dot(mixed + exact_dot(beta_t, curv_ref[...], NN), beta_t, NT)
     curv = 0.5 * (curv + curv.T)
     if last:
         (alpha,) = solve_systems([(curv, gram)], 8)
@@ -360,7 +374,8 @@
             jnp.int32, square, 1
         )
         alpha, inverse = solve_systems([(curv, gram), (gram, same.astype(F32))], 8)
-        new_lead_ref[...] = jnp.concatenate([inverse, exact_dot(inverse, curv, NN)], axis=1)
+        new_inv_ref[...] = inverse
+        new_curv_ref[...] = curv
         sources = spread_ref.shape[0]
         pixels = OWN * sources
         spread_img = fresh_ref[:, 0:OWN, :].reshape(pixels, LANE)
@@ -429,7 +444,9 @@
     start = ((COLS, STRIP * sources + NOTES, LANE), BF16)
     dense = ((2 * BLKS, pixels, LANE), BF16)
 
-    (packed,) = call(pack_kernel, [VMEM] * 6, [start], [], "pack", near=False)(
+    loaded = [pltpu.VMEM((sources, LANE, LANE), BF16), pltpu.SemaphoreType.DMA((BATCHES,))]
+    far = pl.BlockSpec(memory_space=pltpu.HBM)
+    (packed,) = call(pack_kernel, [VMEM] * 5 + [far], [start], loaded, "pack", near=False)(
         right_side.T, regular.reshape(1, PIECE), *tables, curv
     )
     col_here = lax.axis_index(COL).astype(jnp.int32).reshape(1)
@@ -500,7 +517,7 @@
             )(col_here, row_here, got, res, reg, *state, piece)
             return tuple(part.T for part in shares)
         inputs = [got, res, reg, *state, spread, fresh, *spread_img]
-        outs = [field] * 3 + [((SMP, LANE), F32)] * 2 + [spread_share] * 2 + [own_share]
+        outs = [field] * 3 + [((SMP, LANE), F32)] + [((SMP, SMP), F32)] * 2 + [spread_share] * 2 + [own_share]
         res, *state, spread, img, own = call(
             solve, [SMEM] * 2 + [VMEM] * len(inputs), outs, [], f"solve_{step}"
         )(col_here, row_here, *inputs)

time: 219 us -> 219 us (level)
  no operation moved by 1% of the time
where the time goes in v10:
time: 219 us
  blocking collectives  175 us (80%)
  Pallas kernels  24.5 us (11%)
  starting transfers between devices  9.8 us (4%)
  waiting for transfers between devices  8.72 us (4%)
    all_to_all x10, blocking collectives, swap(): return lax.all_to_all(msg, axes, 0, 0, tiled=True)  175 us
    pallas_call x16, Pallas kernels, placed(): return run(*args)  24.5 us
    all_to_all x1, starting transfers between devices, swap(): return lax.all_to_all(msg, axes, 0, 0, tiled=True)  9.8 us
    all_to_all x1, waiting for transfers between devices, swap(): return lax.all_to_all(msg, axes, 0, 0, tiled=True)  8.72 us
  transfers between devices with their start and end apart: 1, of which 1 were waited for; matrix products, arithmetic and copies ran while one was open for 0% of the time, Pallas kernels for 2%

profile of v10, /device:TPU:1, one launch (start us, length us, event | category | flops | bytes accessed | tf_op | source)
XLA Modules:
  0.0 218.8 jit_solution(10342537169363002143)
XLA Ops:
  0.6 2.3 %pack.1 = bf16[16,312,128]{2,1,0:T(8,128)(2,1)S(1)} custom-call(f32[32,64]{1,0:T(8,128)} %bitcast.13, f32[1,32]{1,0:T(1,128)} %bitcast.14, s32[1,32]{1,0:T(1,128)} %bitcast.15, s32[1,32]{1,0:T(1,128)} %bitcast.16, s32[1,32]{1,0:T(1,128)} %bitcast.17, bf16[32,128,128]{2,1,0:T(8,128)(2,1)} %bitcast.12), custom_call_target="tpu_custom_call" | custom-call | tf_op jit(solution)/shard_map/pack/pallas_call | solution.py:73
  3.0 45.0 %all_to_all.55.got_ref = bf16[16,312,128]{2,1,0:T(8,128)(2,1)S(1)} all-to-all(bf16[16,312,128]{2,1,0:T(8,128)(2,1)S(1)} %pack.1), channel_id=1, replica_groups=mesh['row_0'=8,'row_1'=4,'col_0'=8,'col_1'=2] {'col_0','col_1'}, dimensions={0} | all-to-all | bytes 2555904 | tf_op jit(solution)/shard_map/all_to_all | solution.py:53
  47.9 1.0 own.1
  48.9 9.8 %all-to-all-start.1 = ((f32[32,16,128]{2,1,0:T(8,128)}), f32[32,16,128]{2,1,0:T(8,128)}, u32[]{:S(2)}, u32[]{:S(2)}) async-start(f32[32,16,128]{2,1,0:T(8,128)} %get-tuple-element.40), calls=%async_computation.1 | async-start | bytes 524288 | tf_op jit(solution)/shard_map/all_to_all | solution.py:53
  58.7 0.4 unpack.1
  59.1 3.8 %dense.1 = (bf16[8,512,128]{2,1,0:T(8,128)(2,1)S(1)}, bf16[8,512,128]{2,1,0:T(8,128)(2,1)S(1)}) custom-call(s32[16,32]{1,0:T(8,128)S(1)} %bitcast.11, bf16[16,312,128]{2,1,0:T(8,128)(2,1)S(1)} %all_to_all.55.got_ref), custom_call_target="tpu_custom_call" | custom-call | tf_op jit(solution)/shard_map/dense/pallas_call | solution.py:73
  62.9 8.7 %all-to-all-done.1.refs_0_.refs_5_ = f32[32,16,128]{2,1,0:T(8,128)} async-done(((f32[32,16,128]{2,1,0:T(8,128)}), f32[32,16,128]{2,1,0:T(8,128)}, u32[]{:S(2)}, u32[]{:S(2)}) %all-to-all-start.1) | async-done | bytes 262176 | tf_op jit(solution)/shard_map/all_to_all | solution.py:53
  71.6 1.8 product_0.1
  73.4 13.6 %all_to_all.56.got_ref = f32[16,24,128]{2,1,0:T(8,128)S(1)} all-to-all(f32[16,24,128]{2,1,0:T(8,128)S(1)} %product_0.1), channel_id=1, replica_groups=mesh['row_0'=8,'row_1'=4,'col_0'=8,'col_1'=2] {'col_0','col_1'}, dimensions={0} | all-to-all | bytes 393216 | tf_op jit(solution)/shard_map/all_to_all | solution.py:53
  87.0 18.1 %all_to_all.57.got_ref.refs_6_ = f32[32,24,128]{2,1,0:T(8,128)S(1)} all-to-all(f32[32,24,128]{2,1,0:T(8,128)S(1)} %get-tuple-element.47), channel_id=1, replica_groups=mesh['row_0'=8,'row_1'=4,'col_0'=8,'col_1'=2] {'row_0','row_1'}, dimensions={0} | all-to-all | bytes 786432 | tf_op jit(solution)/shard_map/all_to_all | solution.py:53
  105.2 14.1 %all_to_all.58.refs_2_ = f32[16,24,128]{2,1,0:T(8,128)S(1)} all-to-all(f32[16,24,128]{2,1,0:T(8,128)S(1)} %row_sum_0.1), channel_id=1, replica_groups=mesh['row_0'=8,'row_1'=4,'col_0'=8,'col_1'=2] {'col_0','col_1'}, dimensions={0} | all-to-all | bytes 393216 | tf_op jit(solution)/shard_map/all_to_all | solution.py:53
  119.3 4.2 %solve_0.1 = (f32[4,64,128]{2,1,0:T(8,128)S(1)}, f32[4,64,128]{2,1,0:T(8,128)S(1)}, f32[4,64,128]{2,1,0:T(8,128)S(1)}, f32[64,128]{1,0:T(8,128)S(1)}, f32[64,64]...) custom-call(s32[1]{0:T(128)} %bitcast.6.place_ref.refs_0_, ...), custom_call_target="tpu_custom_call" | custom-call | tf_op jit(solution)/shard_map/solve_0/pallas_call | solution.py:73
  123.4 1.1 product_1.1
  124.5 13.0 %all_to_all.59.got_ref = f32[16,24,128]{2,1,0:T(8,128)S(1)} all-to-all(f32[16,24,128]{2,1,0:T(8,128)S(1)} %product_1.1), channel_id=1, replica_groups=mesh['row_0'=8,'row_1'=4,'col_0'=8,'col_1'=2] {'col_0','col_1'}, dimensions={0} | all-to-all | bytes 393216 | tf_op jit(solution)/shard_map/all_to_all | solution.py:53
  137.5 18.5 %all_to_all.60.got_ref.refs_11_ = f32[32,24,128]{2,1,0:T(8,128)S(1)} all-to-all(f32[32,24,128]{2,1,0:T(8,128)S(1)} %get-tuple-element.54), channel_id=1, replica_groups=mesh['row_0'=8,'row_1'=4,'col_0'=8,'col_1'=2] {'row_0','row_1'}, dimensions={0} | all-to-all | bytes 786432 | tf_op jit(solution)/shard_map/all_to_all | solution.py:53
  156.1 14.5 %all_to_all.61.refs_2_ = f32[16,24,128]{2,1,0:T(8,128)S(1)} all-to-all(f32[16,24,128]{2,1,0:T(8,128)S(1)} %row_sum_1.1), channel_id=1, replica_groups=mesh['row_0'=8,'row_1'=4,'col_0'=8,'col_1'=2] {'col_0','col_1'}, dimensions={0} | all-to-all | bytes 393216 | tf_op jit(solution)/shard_map/all_to_all | solution.py:53
  170.6 4.8 %solve_1.1 = (f32[4,64,128]{2,1,0:T(8,128)S(1)}, f32[4,64,128]{2,1,0:T(8,128)S(1)}, f32[4,64,128]{2,1,0:T(8,128)S(1)}, f32[64,128]{1,0:T(8,128)S(1)}, f32[64,64]...) custom-call(s32[1]{0:T(128)} %bitcast.6.place_ref.refs_0_, ...), custom_call_target="tpu_custom_call" | custom-call | tf_op jit(solution)/shard_map/solve_1/pallas_call | solution.py:73
  175.4 1.1 product_2.1
  176.5 12.8 %all_to_all.62.got_ref = f32[16,24,128]{2,1,0:T(8,128)S(1)} all-to-all(f32[16,24,128]{2,1,0:T(8,128)S(1)} %product_2.1), channel_id=1, replica_groups=mesh['row_0'=8,'row_1'=4,'col_0'=8,'col_1'=2] {'col_0','col_1'}, dimensions={0} | all-to-all | bytes 393216 | tf_op jit(solution)/shard_map/all_to_all | solution.py:53
  189.4 13.7 %all_to_all.63.got_ref = f32[32,8,128]{2,1,0:T(8,128)S(1)} all-to-all(f32[32,8,128]{2,1,0:T(8,128)S(1)} %get-tuple-element.65), channel_id=1, replica_groups=mesh['row_0'=8,'row_1'=4,'col_0'=8,'col_1'=2] {'row_0','row_1'}, dimensions={0} | all-to-all | bytes 262144 | tf_op jit(solution)/shard_map/all_to_all | solution.py:53
  203.1 11.8 %all_to_all.64.refs_2_ = f32[16,8,128]{2,1,0:T(8,128)S(1)} all-to-all(f32[16,8,128]{2,1,0:T(8,128)S(1)} %row_sum_2.1), channel_id=1, replica_groups=mesh['row_0'=8,'row_1'=4,'col_0'=8,'col_1'=2] {'col_0','col_1'}, dimensions={0} | all-to-all | bytes 131072 | tf_op jit(solution)/shard_map/all_to_all | solution.py:53
  214.9 3.9 %solve_2.1 = (f32[32,64]{1,0:T(8,128)}, f32[32,64]{1,0:T(8,128)}) custom-call(s32[1]{0:T(128)} %bitcast.6.place_ref.refs_0_, s32[1]{0:T(128)} %bitcast.7.refs_1_, f32[16,8,128]{2,1,0:T(8,128)S(1)} %all_to_all.64.refs_2_, f32[4,64,128]{2,1,0:T(8,128)S(1)} %get-tuple-element.61.refs_3_, f32[4,8,128]{2,1,0:T(8,128)S(1)} %get-tuple-element.44.refs_4_, ...), custom_call_target="tpu_custom_call" | custom-call | tf_op jit(solution)/shard_map/solve_2/pallas_call | solution.py:73
  (7 shorter events, 0.2 us)
Async XLA Ops:
  48.9 22.7 %all-to-all-start.1 = ((f32[32,16,128]{2,1,0:T(8,128)}), f32[32,16,128]{2,1,0:T(8,128)}, u32[]{:S(2)}, u32[]{:S(2)}) async-start(f32[32,16,128]{2,1,0:T(8,128)} %get-tuple-element.40), calls=%async_computation.1 | async-start | bytes 524288 | tf_op jit(solution)/shard_map/all_to_all | solution.py:53

commit v11 on v9

--- a/solution.py
+++ b/solution.py
@@ -330,8 +330,8 @@
     refs = refs[5:]
     mine = col_ref[0] // 4
     if not first:
-        dir_ref, img_ref, sol_ref, lead_ref = refs[:4]
-        refs = refs[4:]
+        dir_ref, img_ref, sol_ref, inv_ref, curv_ref = refs[:5]
+        refs = refs[5:]
     if last:
         piece_ref, out_sol_ref, out_res_ref = refs
     else:
@@ -340,7 +340,7 @@
         if not first:
             spread_img_ref = refs.pop(0)
         new_res_ref, new_dir_ref, new_img_ref, new_sol_ref = refs[:4]
-        new_lead_ref, new_spread_ref, new_spread_img_ref, own_ref = refs[4:]
+        new_inv_ref, new_curv_ref, new_spread_ref, new_spread_img_ref, own_ref = refs[4:]
     base = got_ref.shape[1] - 8
     pair = jnp.concatenate([got_ref[k, base:, :] for k in range(8)], axis=0)
     gram = pltpu.roll(pair, SMP, 1)[:, 0:SMP]
@@ -348,9 +348,8 @@
     if not first:
         mixed = jnp.concatenate([got_ref[k, base:, :] for k in range(8, 16)], axis=0)
         mixed = mixed[:, 0:SMP]
-        both = exact_dot(gram, lead_ref[...], NN)
-        beta_t = both[:, 0:SMP]
-        curv = curv + exact_dot(mixed + pltpu.roll(both, SMP, 1)[:, 0:SMP], beta_t, NT)
+        beta_t = exact_dot(gram, inv_ref[...], NN)
+        curv = curv + exact_dot(mixed + exact_dot(beta_t, curv_ref[...], NN), beta_t, NT)
     curv = 0.5 * (curv + curv.T)
     if last:
         (alpha,) = solve_systems([(curv, gram)], 8)
@@ -360,7 +359,8 @@
             jnp.int32, square, 1
         )
         alpha, inverse = solve_systems([(curv, gram), (gram, same.astype(F32))], 8)
-        new_lead_ref[...] = jnp.concatenate([inverse, exact_dot(inverse, curv, NN)], axis=1)
+        new_inv_ref[...] = inverse
+        new_curv_ref[...] = curv
         sources = spread_ref.shape[0]
         pixels = OWN * sources
         spread_img = fresh_ref[:, 0:OWN, :].reshape(pixels, LANE)
@@ -500,7 +500,7 @@
             )(col_here, row_here, got, res, reg, *state, piece)
             return tuple(part.T for part in shares)
         inputs = [got, res, reg, *state, spread, fresh, *spread_img]
-        outs = [field] * 3 + [((SMP, LANE), F32)] * 2 + [spread_share] * 2 + [own_share]
+        outs = [field] * 3 + [((SMP, LANE), F32)] + [((SMP, SMP), F32)] * 2 + [spread_share] * 2 + [own_share]
         res, *state, spread, img, own = call(
             solve, [SMEM] * 2 + [VMEM] * len(inputs), outs, [], f"solve_{step}"
         )(col_here, row_here, *inputs)

time: 219 us -> 219 us (level)
  no operation moved by 1% of the time
where the time goes in v11:
time: 219 us; the launch traced here: 218 us
  blocking collectives  175 us (80%)
  Pallas kernels  24 us (11%)
  starting transfers between devices  9.8 us (4%)
  waiting for transfers between devices  8.71 us (4%)
    all_to_all x10, blocking collectives, swap(): return lax.all_to_all(msg, axes, 0, 0, tiled=True)  175 us
    pallas_call x16, Pallas kernels, placed(): return run(*args)  24 us
    all_to_all x1, starting transfers between devices, swap(): return lax.all_to_all(msg, axes, 0, 0, tiled=True)  9.8 us
    all_to_all x1, waiting for transfers between devices, swap(): return lax.all_to_all(msg, axes, 0, 0, tiled=True)  8.71 us
  transfers between devices with their start and end apart: 1, of which 1 were waited for; matrix products, arithmetic and copies ran while one was open for 0% of the time, Pallas kernels for 2%

profile of v11, /device:TPU:1, one launch (start us, length us, event | category | flops | bytes accessed | tf_op | source)
XLA Modules:
  0.0 218.2 jit_solution(18421420644966326326)
XLA Ops:
  0.6 1.7 pack.1
  2.4 45.0 %all_to_all.55.got_ref = bf16[16,312,128]{2,1,0:T(8,128)(2,1)S(1)} all-to-all(bf16[16,312,128]{2,1,0:T(8,128)(2,1)S(1)} %pack.1), channel_id=1, replica_groups=mesh['row_0'=8,'row_1'=4,'col_0'=8,'col_1'=2] {'col_0','col_1'}, dimensions={0} | all-to-all | bytes 2555904 | tf_op jit(solution)/shard_map/all_to_all | solution.py:52
  47.3 1.0 own.1
  48.3 9.8 %all-to-all-start.1 = ((f32[32,16,128]{2,1,0:T(8,128)}), f32[32,16,128]{2,1,0:T(8,128)}, u32[]{:S(2)}, u32[]{:S(2)}) async-start(f32[32,16,128]{2,1,0:T(8,128)} %get-tuple-element.40), calls=%async_computation.1 | async-start | bytes 524288 | tf_op jit(solution)/shard_map/all_to_all | solution.py:52
  58.1 0.4 unpack.1
  58.5 3.8 %dense.1 = (bf16[8,512,128]{2,1,0:T(8,128)(2,1)S(1)}, bf16[8,512,128]{2,1,0:T(8,128)(2,1)S(1)}) custom-call(s32[16,32]{1,0:T(8,128)S(1)} %bitcast.11, bf16[16,312,128]{2,1,0:T(8,128)(2,1)S(1)} %all_to_all.55.got_ref), custom_call_target="tpu_custom_call" | custom-call | tf_op jit(solution)/shard_map/dense/pallas_call | solution.py:72
  62.3 8.7 %all-to-all-done.1.refs_0_.refs_5_ = f32[32,16,128]{2,1,0:T(8,128)} async-done(((f32[32,16,128]{2,1,0:T(8,128)}), f32[32,16,128]{2,1,0:T(8,128)}, u32[]{:S(2)}, u32[]{:S(2)}) %all-to-all-start.1) | async-done | bytes 262176 | tf_op jit(solution)/shard_map/all_to_all | solution.py:52
  71.0 1.8 product_0.1
  72.8 13.6 %all_to_all.56.got_ref = f32[16,24,128]{2,1,0:T(8,128)S(1)} all-to-all(f32[16,24,128]{2,1,0:T(8,128)S(1)} %product_0.1), channel_id=1, replica_groups=mesh['row_0'=8,'row_1'=4,'col_0'=8,'col_1'=2] {'col_0','col_1'}, dimensions={0} | all-to-all | bytes 393216 | tf_op jit(solution)/shard_map/all_to_all | solution.py:52
  86.4 18.1 %all_to_all.57.got_ref.refs_6_ = f32[32,24,128]{2,1,0:T(8,128)S(1)} all-to-all(f32[32,24,128]{2,1,0:T(8,128)S(1)} %get-tuple-element.47), channel_id=1, replica_groups=mesh['row_0'=8,'row_1'=4,'col_0'=8,'col_1'=2] {'row_0','row_1'}, dimensions={0} | all-to-all | bytes 786432 | tf_op jit(solution)/shard_map/all_to_all | solution.py:52
  104.6 14.1 %all_to_all.58.refs_2_ = f32[16,24,128]{2,1,0:T(8,128)S(1)} all-to-all(f32[16,24,128]{2,1,0:T(8,128)S(1)} %row_sum_0.1), channel_id=1, replica_groups=mesh['row_0'=8,'row_1'=4,'col_0'=8,'col_1'=2] {'col_0','col_1'}, dimensions={0} | all-to-all | bytes 393216 | tf_op jit(solution)/shard_map/all_to_all | solution.py:52
  118.7 4.2 %solve_0.1 = (f32[4,64,128]{2,1,0:T(8,128)S(1)}, f32[4,64,128]{2,1,0:T(8,128)S(1)}, f32[4,64,128]{2,1,0:T(8,128)S(1)}, f32[64,128]{1,0:T(8,128)S(1)}, f32[64,64]...) custom-call(s32[1]{0:T(128)} %bitcast.6.place_ref.refs_0_, ...), custom_call_target="tpu_custom_call" | custom-call | tf_op jit(solution)/shard_map/solve_0/pallas_call | solution.py:72
  122.8 1.1 product_1.1
  123.9 13.0 %all_to_all.59.got_ref = f32[16,24,128]{2,1,0:T(8,128)S(1)} all-to-all(f32[16,24,128]{2,1,0:T(8,128)S(1)} %product_1.1), channel_id=1, replica_groups=mesh['row_0'=8,'row_1'=4,'col_0'=8,'col_1'=2] {'col_0','col_1'}, dimensions={0} | all-to-all | bytes 393216 | tf_op jit(solution)/shard_map/all_to_all | solution.py:52
  136.9 18.5 %all_to_all.60.got_ref.refs_11_ = f32[32,24,128]{2,1,0:T(8,128)S(1)} all-to-all(f32[32,24,128]{2,1,0:T(8,128)S(1)} %get-tuple-element.54), channel_id=1, replica_groups=mesh['row_0'=8,'row_1'=4,'col_0'=8,'col_1'=2] {'row_0','row_1'}, dimensions={0} | all-to-all | bytes 786432 | tf_op jit(solution)/shard_map/all_to_all | solution.py:52
  155.5 14.5 %all_to_all.61.refs_2_ = f32[16,24,128]{2,1,0:T(8,128)S(1)} all-to-all(f32[16,24,128]{2,1,0:T(8,128)S(1)} %row_sum_1.1), channel_id=1, replica_groups=mesh['row_0'=8,'row_1'=4,'col_0'=8,'col_1'=2] {'col_0','col_1'}, dimensions={0} | all-to-all | bytes 393216 | tf_op jit(solution)/shard_map/all_to_all | solution.py:52
  170.0 4.8 %solve_1.1 = (f32[4,64,128]{2,1,0:T(8,128)S(1)}, f32[4,64,128]{2,1,0:T(8,128)S(1)}, f32[4,64,128]{2,1,0:T(8,128)S(1)}, f32[64,128]{1,0:T(8,128)S(1)}, f32[64,64]...) custom-call(s32[1]{0:T(128)} %bitcast.6.place_ref.refs_0_, ...), custom_call_target="tpu_custom_call" | custom-call | tf_op jit(solution)/shard_map/solve_1/pallas_call | solution.py:72
  174.8 1.1 product_2.1
  175.9 12.8 %all_to_all.62.got_ref = f32[16,24,128]{2,1,0:T(8,128)S(1)} all-to-all(f32[16,24,128]{2,1,0:T(8,128)S(1)} %product_2.1), channel_id=1, replica_groups=mesh['row_0'=8,'row_1'=4,'col_0'=8,'col_1'=2] {'col_0','col_1'}, dimensions={0} | all-to-all | bytes 393216 | tf_op jit(solution)/shard_map/all_to_all | solution.py:52
  188.8 13.7 %all_to_all.63.got_ref = f32[32,8,128]{2,1,0:T(8,128)S(1)} all-to-all(f32[32,8,128]{2,1,0:T(8,128)S(1)} %get-tuple-element.65), channel_id=1, replica_groups=mesh['row_0'=8,'row_1'=4,'col_0'=8,'col_1'=2] {'row_0','row_1'}, dimensions={0} | all-to-all | bytes 262144 | tf_op jit(solution)/shard_map/all_to_all | solution.py:52
  202.5 11.8 %all_to_all.64.refs_2_ = f32[16,8,128]{2,1,0:T(8,128)S(1)} all-to-all(f32[16,8,128]{2,1,0:T(8,128)S(1)} %row_sum_2.1), channel_id=1, replica_groups=mesh['row_0'=8,'row_1'=4,'col_0'=8,'col_1'=2] {'col_0','col_1'}, dimensions={0} | all-to-all | bytes 131072 | tf_op jit(solution)/shard_map/all_to_all | solution.py:52
  214.3 3.9 %solve_2.1 = (f32[32,64]{1,0:T(8,128)}, f32[32,64]{1,0:T(8,128)}) custom-call(s32[1]{0:T(128)} %bitcast.6.place_ref.refs_0_, s32[1]{0:T(128)} %bitcast.7.refs_1_, f32[16,8,128]{2,1,0:T(8,128)S(1)} %all_to_all.64.refs_2_, f32[4,64,128]{2,1,0:T(8,128)S(1)} %get-tuple-element.61.refs_3_, f32[4,8,128]{2,1,0:T(8,128)S(1)} %get-tuple-element.44.refs_4_, ...), custom_call_target="tpu_custom_call" | custom-call | tf_op jit(solution)/shard_map/solve_2/pallas_call | solution.py:72
  (7 shorter events, 0.3 us)
Async XLA Ops:
  48.3 22.7 %all-to-all-start.1 = ((f32[32,16,128]{2,1,0:T(8,128)}), f32[32,16,128]{2,1,0:T(8,128)}, u32[]{:S(2)}, u32[]{:S(2)}) async-start(f32[32,16,128]{2,1,0:T(8,128)} %get-tuple-element.40), calls=%async_computation.1 | async-start | bytes 524288 | tf_op jit(solution)/shard_map/all_to_all | solution.py:52
